TPU v7x, 512 devices: a whole 4x4x16 slice. The times are simulated.
512 devices in a mesh: depth: 8 (over y, core), gx: 16 (over z), gy: 4 (over x).
Axes of the slice: x: 4, y: 4, z: 16, core: 2. Of those that a mesh axis runs over, the one named last changes fastest.
Arguments:
- slowness: float32 [16, 256, 1024], P('depth', 'gx', 'gy'), may hold values from 0.5 to 1.5
- air_mask: int32 [16, 256, 1024], P('depth', 'gx', 'gy'), may hold values from 0 to 1, as said below
- reflector: int32 [256, 1024], P('gx', 'gy'), may hold values from 4 to 15
- shot_cells: int32 [8, 2], replicated, may hold values from 0 to 255
- receiver_mask: int32 [8, 256, 1024], P(None, 'gx', 'gy'), may hold values 0 or 1
- residual: float32 [8, 256, 1024], P(None, 'gx', 'gy'), may hold values from -6 to 6
Outputs:
- gradient: float32 [16, 256, 1024], P('depth', 'gx', 'gy')
Inputs may be any that keep to these rules, and one draw needn't show every extreme that they name: `air_mask`: each lateral column is air in a top run of 0 to 2 cells and earth below; some column has exactly 2 air cells.
All inputs are finite; a program needn't handle non-finite values. No bound on the sum of `receiver_mask` on one device may be relied on, other than what follows from the above.
Results may differ from a plain program's by a relative error of at most 0.0003.
Values sent between devices are 32-bit elements; how exact they have to be, the bound alone decides.
No kernel may reach another device: no remote copies, remote signals or barrier semaphores. Data moves between devices by JAX's collectives and lax.ppermute only.
A program may use at most 64 MiB of HBM per device.

v0:
```python
import math

import jax
import jax.numpy as jnp
from jax import lax
from jax.sharding import PartitionSpec as P

SOFTMIN_TEMPER = 0.5
SURF = 0.7
AIR_SLOW = 2.5
STEP_PENALTY = 10000.0
STENCIL_SHIFTS = [
    (first_term, second_term) for first_term in (-1, 0, 1) for second_term in (-1, 0, 1)
]


def padded(cells, sides, width):
    for axis, dim in sides:
        count = lax.axis_size(axis)
        ends = count - 1
        head = lax.slice_in_dim(cells, 0, width, axis=dim)
        tail = lax.slice_in_dim(cells, cells.shape[dim] - width, cells.shape[dim], axis=dim)
        cells = jnp.concatenate(
            [
                lax.ppermute(tail, axis, [(i, (i + 1) % count) for i in range(ends)]),
                cells,
                lax.ppermute(head, axis, [((i + 1) % count, i) for i in range(ends)]),
            ],
            axis=dim,
        )
    return cells


def passed_along(value, axis, steps):
    count = lax.axis_size(axis)
    initial, last = (max(0, -steps), min(count, count - steps))
    return lax.ppermute(value, axis, [(source, source + steps) for source in range(initial, last)])


def soft_front(candidate_times):
    lowest = candidate_times[0]
    for cand in candidate_times[1:]:
        lowest = jnp.minimum(lowest, cand)
    total = jnp.exp(-(candidate_times[0] - lowest) / SOFTMIN_TEMPER)
    for cand in candidate_times[1:]:
        total = total + jnp.exp(-(cand - lowest) / SOFTMIN_TEMPER)
    return lowest - SOFTMIN_TEMPER * jnp.log(total)


def local(slowness, air_mask, reflector, shot_cells, receiver_mask, residual):
    depth_count = lax.axis_size("depth")
    depth_pos = lax.axis_index("depth")
    cz, shift_along_x, shift_along_y = slowness.shape
    shots = shot_cells.shape[0]
    nx_total = shift_along_x * lax.axis_size("gx")
    ny_total = shift_along_y * lax.axis_size("gy")
    xpos = lax.axis_index("gx") * shift_along_x + jnp.arange(shift_along_x, dtype=jnp.int32)
    ypos = lax.axis_index("gy") * shift_along_y + jnp.arange(shift_along_y, dtype=jnp.int32)
    zpos = depth_pos * cz + jnp.arange(cz, dtype=jnp.int32)
    earth = air_mask == 0
    speed = jnp.where(air_mask == 1, jnp.float32(AIR_SLOW), slowness)
    shot_x = shot_cells[:, 0].astype(jnp.float32)
    shot_y = shot_cells[:, 1].astype(jnp.float32)
    surface = SURF * jnp.sqrt(
        (xpos.astype(jnp.float32)[None, :, None] - shot_x[:, None, None]) ** 2
        + (ypos.astype(jnp.float32)[None, None, :] - shot_y[:, None, None]) ** 2
    )
    penalty_terms = []
    span_lengths = []
    for first_term, second_term in STENCIL_SHIFTS:
        valid_mask = ((xpos + first_term >= 0) & (xpos + first_term < nx_total))[:, None] & (
            (ypos + second_term >= 0) & (ypos + second_term < ny_total)
        )[None, :]
        penalty_terms.append(jnp.where(valid_mask, jnp.float32(0.0), jnp.float32(STEP_PENALTY)))
        span_lengths.append(math.sqrt(1.0 + first_term * first_term + second_term * second_term))

    def sweep_plane(prior_layer, depth_layer):
        padded_layer = padded(prior_layer, (("gx", 1), ("gy", 2)), 1)
        candidate_times = [
            padded_layer[
                :,
                1 + first_term : 1 + first_term + shift_along_x,
                1 + second_term : 1 + second_term + shift_along_y,
            ]
            + depth_layer * span_lengths[stencil_index]
            + penalty_terms[stencil_index]
            for stencil_index, (first_term, second_term) in enumerate(STENCIL_SHIFTS)
        ]
        nxt = soft_front(candidate_times)
        return (nxt, nxt)

    def make_adjoint(source_block, count):

        def adjoint_plane(back, inputs):
            depth_layer, hit, previous_times, current_layer = inputs
            lam = source_block * hit[None] + back
            stacked = jnp.concatenate([lam, current_layer, previous_times, depth_layer[None]], 0)
            padded_layer = padded(stacked, (("gx", 1), ("gy", 2)), 1)
            lam_pad = padded_layer[:count]
            cur_pad = padded_layer[count : 2 * count]
            prev_pad = padded_layer[2 * count : 3 * count]
            layer_pad = padded_layer[3 * count]
            weight_sum = jnp.zeros_like(lam)
            back_new = jnp.zeros_like(lam)
            for stencil_index, (first_term, second_term) in enumerate(STENCIL_SHIFTS):
                lateral_value = prev_pad[
                    :,
                    1 + first_term : 1 + first_term + shift_along_x,
                    1 + second_term : 1 + second_term + shift_along_y,
                ]
                softmin_weight = jnp.exp(
                    -(
                        lateral_value
                        + depth_layer * span_lengths[stencil_index]
                        + penalty_terms[stencil_index]
                        - current_layer
                    )
                    / SOFTMIN_TEMPER
                )
                weight_sum = weight_sum + softmin_weight * span_lengths[stencil_index]
                lam_from = lam_pad[
                    :,
                    1 - first_term : 1 - first_term + shift_along_x,
                    1 - second_term : 1 - second_term + shift_along_y,
                ]
                cur_from = cur_pad[
                    :,
                    1 - first_term : 1 - first_term + shift_along_x,
                    1 - second_term : 1 - second_term + shift_along_y,
                ]
                layer_from = layer_pad[
                    1 - first_term : 1 - first_term + shift_along_x,
                    1 - second_term : 1 - second_term + shift_along_y,
                ]
                prob_from = jnp.exp(
                    -(previous_times + layer_from * span_lengths[stencil_index] - cur_from)
                    / SOFTMIN_TEMPER
                )
                back_new = back_new + lam_from * prob_from
            return (back_new, jnp.sum(lam * weight_sum, axis=0))

        return adjoint_plane

    source_all = jnp.where(receiver_mask == 1, residual, jnp.float32(0.0))
    blocks = 1
    width = shots // blocks
    rounds = depth_count + blocks - 1

    def forward_round(step, carry):
        incoming, store = carry
        group = step - depth_pos
        valid_mask = (group >= 0) & (group < blocks)
        top = jnp.where(depth_pos == 0, surface, incoming)
        last, planes = lax.scan(sweep_plane, top, speed)
        block = jnp.concatenate([top[None], planes], 0)
        old = store
        store = jnp.where(valid_mask, block, old)
        incoming = passed_along(last, "depth", 1)
        return (incoming, store)

    store = jnp.zeros((cz + 1, shots, shift_along_x, shift_along_y), jnp.float32)
    incoming = jnp.zeros((width, shift_along_x, shift_along_y), jnp.float32)
    incoming, store = lax.fori_loop(0, rounds, forward_round, (incoming, store))
    hits = (zpos[:, None, None] == reflector[None]).astype(jnp.float32)

    def adjoint_round(step, carry):
        incoming_back, grad_sum = carry
        group = step - (depth_count - 1 - depth_pos)
        valid_mask = (group >= 0) & (group < blocks)
        back_top, grads = lax.scan(
            make_adjoint(source_all, width),
            incoming_back,
            (speed, hits, store[:-1], store[1:]),
            reverse=True,
        )
        grad_sum = grad_sum + jnp.where(valid_mask, grads, jnp.float32(0.0))
        incoming_back = passed_along(back_top, "depth", -1)
        return (incoming_back, grad_sum)

    start_back = jnp.zeros((width, shift_along_x, shift_along_y), jnp.float32)
    grad_total = jnp.zeros((cz, shift_along_x, shift_along_y), jnp.float32)
    start_back, grad_total = lax.fori_loop(0, rounds, adjoint_round, (start_back, grad_total))
    colsum = jnp.sum(source_all, axis=0)
    below = zpos[:, None, None] <= reflector[None]
    raw = jnp.where(earth, grad_total, jnp.float32(0.0)) + jnp.where(
        earth & below, colsum[None], jnp.float32(0.0)
    )
    padded_layer = padded(raw, (("gx", 1), ("gy", 2)), 1)
    beside_all = jnp.zeros_like(raw)
    for first_term, second_term in STENCIL_SHIFTS:
        if first_term != 0 or second_term != 0:
            beside_all = (
                beside_all
                + padded_layer[
                    :,
                    1 + first_term : 1 + first_term + shift_along_x,
                    1 + second_term : 1 + second_term + shift_along_y,
                ]
            )
    return 0.5 * raw + 0.0625 * beside_all


def solution(mesh):
    in_specs = (
        P("depth", "gx", "gy"),
        P("depth", "gx", "gy"),
        P("gx", "gy"),
        P(),
        P(None, "gx", "gy"),
        P(None, "gx", "gy"),
    )
    out_specs = P("depth", "gx", "gy")
    return jax.shard_map(local, mesh=mesh, in_specs=in_specs, out_specs=out_specs, check_vma=False)
```

profile of v0, /device:TPU:356, one launch (start us, length us, event | category | flops | bytes accessed | tf_op | source)
XLA Modules:
  0.0 766.5 jit_solution(17921035878970821006)
XLA Ops:
  2.7 332.3 %while.130 = (s32[]{:T(128)}, f32[8,16,256]{2,1,0:T(8,128)S(1)}, f32[3,8,16,256]{3,2,1,0:T(8,128)S(1)}, pred[]{:T(512)}, f32[2,16,256]{2,1,0:T(8,128)S(1)}, /*in...) while((s32[]{:T(128)}, f32[8,16,256]{2,1,0:T(8,128)S(1)}, ...), condition=%wide.region_3.4_spmd.clone.clone.clone, body=%wide.region_0.3_spmd.clone.clone.clone.sunk | while | flops 2999145 | bytes 5221840 | solution.py:163
  3.0 36.8 %while.133 = (s32[]{:T(128)}, f32[8,16,256]{2,1,0:T(8,128)S(1)}, f32[2,8,16,256]{3,2,1,0:T(8,128)S(1)}, f32[2,16,256]{2,1,0:T(8,128)S(1)}, f32[16,256]{1,0:T(8,1...) while((s32[]{:T(128)}, f32[8,16,256]{2,1,0:T(8,128)S(1)}, ...), condition=%wide.region_2.2_spmd, body=%wide.region_1.1_spmd.sunk | while | flops 2433890 | bytes 2565429 | solution.py:154
  24.9 4.4 collective-permute-start.6
  42.3 36.1 %while.133 = (s32[]{:T(128)}, f32[8,16,256]{2,1,0:T(8,128)S(1)}, f32[2,8,16,256]{3,2,1,0:T(8,128)S(1)}, f32[2,16,256]{2,1,0:T(8,128)S(1)}, f32[16,256]{1,0:T(8,1...) while((s32[]{:T(128)}, f32[8,16,256]{2,1,0:T(8,128)S(1)}, ...), condition=%wide.region_2.2_spmd, body=%wide.region_1.1_spmd.sunk | while | flops 2433890 | bytes 2565429 | solution.py:154
  45.2 4.6 collective-permute-start.6
  63.4 4.3 collective-permute-start.6
  81.0 36.0 %while.133 = (s32[]{:T(128)}, f32[8,16,256]{2,1,0:T(8,128)S(1)}, f32[2,8,16,256]{3,2,1,0:T(8,128)S(1)}, f32[2,16,256]{2,1,0:T(8,128)S(1)}, f32[16,256]{1,0:T(8,1...) while((s32[]{:T(128)}, f32[8,16,256]{2,1,0:T(8,128)S(1)}, ...), condition=%wide.region_2.2_spmd, body=%wide.region_1.1_spmd.sunk | while | flops 2433890 | bytes 2565429 | solution.py:154
  83.9 4.5 collective-permute-start.6
  101.7 4.8 collective-permute-start.6
  117.0 4.6 collective-permute-start.9
  122.9 35.7 %while.133 = (s32[]{:T(128)}, f32[8,16,256]{2,1,0:T(8,128)S(1)}, f32[2,8,16,256]{3,2,1,0:T(8,128)S(1)}, f32[2,16,256]{2,1,0:T(8,128)S(1)}, f32[16,256]{1,0:T(8,1...) while((s32[]{:T(128)}, f32[8,16,256]{2,1,0:T(8,128)S(1)}, ...), condition=%wide.region_2.2_spmd, body=%wide.region_1.1_spmd.sunk | while | flops 2433890 | bytes 2565429 | solution.py:154
  125.2 4.8 collective-permute-start.6
  143.2 4.8 collective-permute-start.6
  158.5 5.6 collective-permute-start.9
  165.3 35.7 %while.133 = (s32[]{:T(128)}, f32[8,16,256]{2,1,0:T(8,128)S(1)}, f32[2,8,16,256]{3,2,1,0:T(8,128)S(1)}, f32[2,16,256]{2,1,0:T(8,128)S(1)}, f32[16,256]{1,0:T(8,1...) while((s32[]{:T(128)}, f32[8,16,256]{2,1,0:T(8,128)S(1)}, ...), condition=%wide.region_2.2_spmd, body=%wide.region_1.1_spmd.sunk | while | flops 2433890 | bytes 2565429 | solution.py:154
  167.6 4.9 collective-permute-start.6
  185.6 4.8 collective-permute-start.6
  201.0 5.6 collective-permute-start.9
  207.8 35.7 %while.133 = (s32[]{:T(128)}, f32[8,16,256]{2,1,0:T(8,128)S(1)}, f32[2,8,16,256]{3,2,1,0:T(8,128)S(1)}, f32[2,16,256]{2,1,0:T(8,128)S(1)}, f32[16,256]{1,0:T(8,1...) while((s32[]{:T(128)}, f32[8,16,256]{2,1,0:T(8,128)S(1)}, ...), condition=%wide.region_2.2_spmd, body=%wide.region_1.1_spmd.sunk | while | flops 2433890 | bytes 2565429 | solution.py:154
  210.0 4.9 collective-permute-start.6
  228.1 4.8 collective-permute-start.6
  243.5 5.6 collective-permute-start.9
  250.3 35.7 %while.133 = (s32[]{:T(128)}, f32[8,16,256]{2,1,0:T(8,128)S(1)}, f32[2,8,16,256]{3,2,1,0:T(8,128)S(1)}, f32[2,16,256]{2,1,0:T(8,128)S(1)}, f32[16,256]{1,0:T(8,1...) while((s32[]{:T(128)}, f32[8,16,256]{2,1,0:T(8,128)S(1)}, ...), condition=%wide.region_2.2_spmd, body=%wide.region_1.1_spmd.sunk | while | flops 2433890 | bytes 2565429 | solution.py:154
  252.5 4.9 collective-permute-start.6
  270.6 4.8 collective-permute-start.6
  286.0 5.6 collective-permute-start.9
  292.8 35.7 %while.133 = (s32[]{:T(128)}, f32[8,16,256]{2,1,0:T(8,128)S(1)}, f32[2,8,16,256]{3,2,1,0:T(8,128)S(1)}, f32[2,16,256]{2,1,0:T(8,128)S(1)}, f32[16,256]{1,0:T(8,1...) while((s32[]{:T(128)}, f32[8,16,256]{2,1,0:T(8,128)S(1)}, ...), condition=%wide.region_2.2_spmd, body=%wide.region_1.1_spmd.sunk | while | flops 2433890 | bytes 2565429 | solution.py:154
  295.0 4.9 collective-permute-start.6
  313.1 4.8 collective-permute-start.6
  328.4 5.6 collective-permute-start.9
  335.7 408.5 %while.132 = (s32[]{:T(128)}, f32[8,16,256]{2,1,0:T(8,128)S(1)}, f32[2,16,256]{2,1,0:T(8,128)S(1)}, f32[3,8,16,256]{3,2,1,0:T(8,128)S(1)}, f32[8,16,256]{2,1,0:T...) while((s32[]{:T(128)}, f32[8,16,256]{2,1,0:T(8,128)S(1)}, ...), condition=%wide.region_8.9_spmd.clone.clone.clone, body=%wide.region_4.8_spmd.clone.clone.clone.sunk | while | flops 6839326 | bytes 10794326 | solution.py:182
  336.0 46.7 %while.134 = (s32[]{:T(128)}, f32[8,16,256]{2,1,0:T(8,128)S(1)}, f32[2,16,256]{2,1,0:T(8,128)S(1)}, f32[2,16,256]{2,1,0:T(8,128)S(1)}, f32[8,16,256]{2,1,0:T(8,1...) while((s32[]{:T(128)}, f32[8,16,256]{2,1,0:T(8,128)S(1)}, ...), condition=%wide.region_7.7_spmd, body=%wide.region_5.6_spmd.sunk | while | flops 6724631 | bytes 8630401 | solution.py:170
  338.3 4.9 collective-permute-start.1
  362.1 4.8 collective-permute-start.1
  384.1 4.8 collective-permute-done.4
  389.1 43.3 %while.134 = (s32[]{:T(128)}, f32[8,16,256]{2,1,0:T(8,128)S(1)}, f32[2,16,256]{2,1,0:T(8,128)S(1)}, f32[2,16,256]{2,1,0:T(8,128)S(1)}, f32[8,16,256]{2,1,0:T(8,1...) while((s32[]{:T(128)}, f32[8,16,256]{2,1,0:T(8,128)S(1)}, ...), condition=%wide.region_7.7_spmd, body=%wide.region_5.6_spmd.sunk | while | flops 6724631 | bytes 8630401 | solution.py:170
  391.9 4.5 collective-permute-start.1
  413.5 4.7 collective-permute-start.1
  433.8 6.4 collective-permute-done.4
  440.4 43.2 %while.134 = (s32[]{:T(128)}, f32[8,16,256]{2,1,0:T(8,128)S(1)}, f32[2,16,256]{2,1,0:T(8,128)S(1)}, f32[2,16,256]{2,1,0:T(8,128)S(1)}, f32[8,16,256]{2,1,0:T(8,1...) while((s32[]{:T(128)}, f32[8,16,256]{2,1,0:T(8,128)S(1)}, ...), condition=%wide.region_7.7_spmd, body=%wide.region_5.6_spmd.sunk | while | flops 6724631 | bytes 8630401 | solution.py:170
  443.2 4.4 collective-permute-start.1
  465.0 4.5 collective-permute-start.1
  484.9 7.1 collective-permute-done.4
  492.3 43.0 %while.134 = (s32[]{:T(128)}, f32[8,16,256]{2,1,0:T(8,128)S(1)}, f32[2,16,256]{2,1,0:T(8,128)S(1)}, f32[2,16,256]{2,1,0:T(8,128)S(1)}, f32[8,16,256]{2,1,0:T(8,1...) while((s32[]{:T(128)}, f32[8,16,256]{2,1,0:T(8,128)S(1)}, ...), condition=%wide.region_7.7_spmd, body=%wide.region_5.6_spmd.sunk | while | flops 6724631 | bytes 8630401 | solution.py:170
  495.1 4.5 collective-permute-start.1
  516.7 4.5 collective-permute-start.1
  536.6 6.5 collective-permute-done.4
  543.4 43.9 %while.134 = (s32[]{:T(128)}, f32[8,16,256]{2,1,0:T(8,128)S(1)}, f32[2,16,256]{2,1,0:T(8,128)S(1)}, f32[2,16,256]{2,1,0:T(8,128)S(1)}, f32[8,16,256]{2,1,0:T(8,1...) while((s32[]{:T(128)}, f32[8,16,256]{2,1,0:T(8,128)S(1)}, ...), condition=%wide.region_7.7_spmd, body=%wide.region_5.6_spmd.sunk | while | flops 6724631 | bytes 8630401 | solution.py:170
  546.2 4.4 collective-permute-start.1
  567.9 4.5 collective-permute-start.1
  592.6 45.3 %while.134 = (s32[]{:T(128)}, f32[8,16,256]{2,1,0:T(8,128)S(1)}, f32[2,16,256]{2,1,0:T(8,128)S(1)}, f32[2,16,256]{2,1,0:T(8,128)S(1)}, f32[8,16,256]{2,1,0:T(8,1...) while((s32[]{:T(128)}, f32[8,16,256]{2,1,0:T(8,128)S(1)}, ...), condition=%wide.region_7.7_spmd, body=%wide.region_5.6_spmd.sunk | while | flops 6724631 | bytes 8630401 | solution.py:170
  595.6 4.5 collective-permute-start.1
  617.5 4.2 collective-permute-start.1
  629.4 4.8 collective-permute-done.2
  642.0 47.9 %while.134 = (s32[]{:T(128)}, f32[8,16,256]{2,1,0:T(8,128)S(1)}, f32[2,16,256]{2,1,0:T(8,128)S(1)}, f32[2,16,256]{2,1,0:T(8,128)S(1)}, f32[8,16,256]{2,1,0:T(8,1...) while((s32[]{:T(128)}, f32[8,16,256]{2,1,0:T(8,128)S(1)}, ...), condition=%wide.region_7.7_spmd, body=%wide.region_5.6_spmd.sunk | while | flops 6724631 | bytes 8630401 | solution.py:170
  668.3 4.2 collective-permute-start.1
  680.2 6.1 collective-permute-done.2
  693.4 47.6 %while.134 = (s32[]{:T(128)}, f32[8,16,256]{2,1,0:T(8,128)S(1)}, f32[2,16,256]{2,1,0:T(8,128)S(1)}, f32[2,16,256]{2,1,0:T(8,128)S(1)}, f32[8,16,256]{2,1,0:T(8,1...) while((s32[]{:T(128)}, f32[8,16,256]{2,1,0:T(8,128)S(1)}, ...), condition=%wide.region_7.7_spmd, body=%wide.region_5.6_spmd.sunk | while | flops 6724631 | bytes 8630401 | solution.py:170
  695.9 4.8 collective-permute-start.1
  708.3 5.1 collective-permute-done.2
  720.6 4.3 collective-permute-start.1
  732.5 4.8 collective-permute-done.2
  744.4 5.1 collective-permute-start.10
  751.5 4.8 collective-permute-done.11
  (710 shorter events, 534.8 us)
Async XLA Ops:
  3.0 7.1 collective-permute-start.5
  22.0 7.3 collective-permute-start.5
  42.4 7.3 collective-permute-start.5
  60.4 7.3 collective-permute-start.5
  81.0 7.4 collective-permute-start.5
  99.1 7.3 collective-permute-start.5
  122.9 7.1 collective-permute-start.5
  140.6 7.3 collective-permute-start.5
  165.4 7.1 collective-permute-start.5
  183.1 7.3 collective-permute-start.5
  207.9 7.1 collective-permute-start.5
  225.6 7.3 collective-permute-start.5
  250.3 7.1 collective-permute-start.5
  268.0 7.3 collective-permute-start.5
  292.8 7.1 collective-permute-start.5
  310.5 7.3 collective-permute-start.5
  336.1 7.1 collective-permute-start
  345.0 8.7 %collective-permute-start.2 = (f32[25,18,1]{2,1,0:T(8,128)S(1)}, f32[25,18,1]{2,1,0:T(8,128)S(1)}, u32[]{:S(2)}, u32[]{:S(2)}) collective-permute-start(f32[25,18,1]{2,1,0:T(8,128)S(1)} %get-tuple-element.2387), channel_id=1, source_target_pairs={{1,0},{2,1},{3,2},{5,4},{6,5},{7,6},{9,8},{10,9},{11,10},{13,12},{... | collective-permute-start | bytes 5408 | tf_op jit(solution)/shard_map/while/body/eval_jaxpr/while/body/eval_jaxpr/ppermute | solution.py:27
  348.9 8.7 %collective-permute-start.3 = (f32[25,18,1]{2,1,0:T(8,128)S(1)}, f32[25,18,1]{2,1,0:T(8,128)S(1)}, u32[]{:S(2)}, u32[]{:S(2)}) collective-permute-start(f32[25,18,1]{2,1,0:T(8,128)S(1)} %get-tuple-element.2388), channel_id=1, source_target_pairs={{0,1},{1,2},{2,3},{4,5},{5,6},{6,7},{8,9},{9,10},{10,11},{12,13},{... | collective-permute-start | bytes 5408 | tf_op jit(solution)/shard_map/while/body/eval_jaxpr/while/body/eval_jaxpr/ppermute | solution.py:25
  359.5 7.4 collective-permute-start
  368.6 8.7 %collective-permute-start.2 = (f32[25,18,1]{2,1,0:T(8,128)S(1)}, f32[25,18,1]{2,1,0:T(8,128)S(1)}, u32[]{:S(2)}, u32[]{:S(2)}) collective-permute-start(f32[25,18,1]{2,1,0:T(8,128)S(1)} %get-tuple-element.2387), channel_id=1, source_target_pairs={{1,0},{2,1},{3,2},{5,4},{6,5},{7,6},{9,8},{10,9},{11,10},{13,12},{... | collective-permute-start | bytes 5408 | tf_op jit(solution)/shard_map/while/body/eval_jaxpr/while/body/eval_jaxpr/ppermute | solution.py:27
  372.3 8.7 %collective-permute-start.3 = (f32[25,18,1]{2,1,0:T(8,128)S(1)}, f32[25,18,1]{2,1,0:T(8,128)S(1)}, u32[]{:S(2)}, u32[]{:S(2)}) collective-permute-start(f32[25,18,1]{2,1,0:T(8,128)S(1)} %get-tuple-element.2388), channel_id=1, source_target_pairs={{0,1},{1,2},{2,3},{4,5},{5,6},{6,7},{8,9},{9,10},{10,11},{12,13},{... | collective-permute-start | bytes 5408 | tf_op jit(solution)/shard_map/while/body/eval_jaxpr/while/body/eval_jaxpr/ppermute | solution.py:25
  389.3 7.1 collective-permute-start
  398.1 8.7 %collective-permute-start.2 = (f32[25,18,1]{2,1,0:T(8,128)S(1)}, f32[25,18,1]{2,1,0:T(8,128)S(1)}, u32[]{:S(2)}, u32[]{:S(2)}) collective-permute-start(f32[25,18,1]{2,1,0:T(8,128)S(1)} %get-tuple-element.2387), channel_id=1, source_target_pairs={{1,0},{2,1},{3,2},{5,4},{6,5},{7,6},{9,8},{10,9},{11,10},{13,12},{... | collective-permute-start | bytes 5408 | tf_op jit(solution)/shard_map/while/body/eval_jaxpr/while/body/eval_jaxpr/ppermute | solution.py:27
  400.3 8.7 %collective-permute-start.3 = (f32[25,18,1]{2,1,0:T(8,128)S(1)}, f32[25,18,1]{2,1,0:T(8,128)S(1)}, u32[]{:S(2)}, u32[]{:S(2)}) collective-permute-start(f32[25,18,1]{2,1,0:T(8,128)S(1)} %get-tuple-element.2388), channel_id=1, source_target_pairs={{0,1},{1,2},{2,3},{4,5},{5,6},{6,7},{8,9},{9,10},{10,11},{12,13},{... | collective-permute-start | bytes 5408 | tf_op jit(solution)/shard_map/while/body/eval_jaxpr/while/body/eval_jaxpr/ppermute | solution.py:25
  410.9 7.4 collective-permute-start
  420.1 8.7 %collective-permute-start.2 = (f32[25,18,1]{2,1,0:T(8,128)S(1)}, f32[25,18,1]{2,1,0:T(8,128)S(1)}, u32[]{:S(2)}, u32[]{:S(2)}) collective-permute-start(f32[25,18,1]{2,1,0:T(8,128)S(1)} %get-tuple-element.2387), channel_id=1, source_target_pairs={{1,0},{2,1},{3,2},{5,4},{6,5},{7,6},{9,8},{10,9},{11,10},{13,12},{... | collective-permute-start | bytes 5408 | tf_op jit(solution)/shard_map/while/body/eval_jaxpr/while/body/eval_jaxpr/ppermute | solution.py:27
  422.0 8.7 %collective-permute-start.3 = (f32[25,18,1]{2,1,0:T(8,128)S(1)}, f32[25,18,1]{2,1,0:T(8,128)S(1)}, u32[]{:S(2)}, u32[]{:S(2)}) collective-permute-start(f32[25,18,1]{2,1,0:T(8,128)S(1)} %get-tuple-element.2388), channel_id=1, source_target_pairs={{0,1},{1,2},{2,3},{4,5},{5,6},{6,7},{8,9},{9,10},{10,11},{12,13},{... | collective-permute-start | bytes 5408 | tf_op jit(solution)/shard_map/while/body/eval_jaxpr/while/body/eval_jaxpr/ppermute | solution.py:25
  432.4 7.7 %collective-permute-start.4 = (f32[8,16,256]{2,1,0:T(8,128)S(1)}, f32[8,16,256]{2,1,0:T(8,128)S(1)}, u32[]{:S(2)}, u32[]{:S(2)}) collective-permute-start(f32[8,16,256]{2,1,0:T(8,128)S(1)} %get-tuple-element.2362), channel_id=1, source_target_pairs={{64,0},{128,64},{192,128},{256,192},{320,256},{384,320},{448,384},... | collective-permute-start | bytes 393224 | tf_op jit(solution)/shard_map/while/body/eval_jaxpr/ppermute | solution.py:37
  440.6 7.1 collective-permute-start
  449.4 8.7 %collective-permute-start.2 = (f32[25,18,1]{2,1,0:T(8,128)S(1)}, f32[25,18,1]{2,1,0:T(8,128)S(1)}, u32[]{:S(2)}, u32[]{:S(2)}) collective-permute-start(f32[25,18,1]{2,1,0:T(8,128)S(1)} %get-tuple-element.2387), channel_id=1, source_target_pairs={{1,0},{2,1},{3,2},{5,4},{6,5},{7,6},{9,8},{10,9},{11,10},{13,12},{... | collective-permute-start | bytes 5408 | tf_op jit(solution)/shard_map/while/body/eval_jaxpr/while/body/eval_jaxpr/ppermute | solution.py:27
  451.5 8.7 %collective-permute-start.3 = (f32[25,18,1]{2,1,0:T(8,128)S(1)}, f32[25,18,1]{2,1,0:T(8,128)S(1)}, u32[]{:S(2)}, u32[]{:S(2)}) collective-permute-start(f32[25,18,1]{2,1,0:T(8,128)S(1)} %get-tuple-element.2388), channel_id=1, source_target_pairs={{0,1},{1,2},{2,3},{4,5},{5,6},{6,7},{8,9},{9,10},{10,11},{12,13},{... | collective-permute-start | bytes 5408 | tf_op jit(solution)/shard_map/while/body/eval_jaxpr/while/body/eval_jaxpr/ppermute | solution.py:25
  462.1 7.4 collective-permute-start
  471.2 8.7 %collective-permute-start.2 = (f32[25,18,1]{2,1,0:T(8,128)S(1)}, f32[25,18,1]{2,1,0:T(8,128)S(1)}, u32[]{:S(2)}, u32[]{:S(2)}) collective-permute-start(f32[25,18,1]{2,1,0:T(8,128)S(1)} %get-tuple-element.2387), channel_id=1, source_target_pairs={{1,0},{2,1},{3,2},{5,4},{6,5},{7,6},{9,8},{10,9},{11,10},{13,12},{... | collective-permute-start | bytes 5408 | tf_op jit(solution)/shard_map/while/body/eval_jaxpr/while/body/eval_jaxpr/ppermute | solution.py:27
  473.1 8.7 %collective-permute-start.3 = (f32[25,18,1]{2,1,0:T(8,128)S(1)}, f32[25,18,1]{2,1,0:T(8,128)S(1)}, u32[]{:S(2)}, u32[]{:S(2)}) collective-permute-start(f32[25,18,1]{2,1,0:T(8,128)S(1)} %get-tuple-element.2388), channel_id=1, source_target_pairs={{0,1},{1,2},{2,3},{4,5},{5,6},{6,7},{8,9},{9,10},{10,11},{12,13},{... | collective-permute-start | bytes 5408 | tf_op jit(solution)/shard_map/while/body/eval_jaxpr/while/body/eval_jaxpr/ppermute | solution.py:25
  483.6 8.4 %collective-permute-start.4 = (f32[8,16,256]{2,1,0:T(8,128)S(1)}, f32[8,16,256]{2,1,0:T(8,128)S(1)}, u32[]{:S(2)}, u32[]{:S(2)}) collective-permute-start(f32[8,16,256]{2,1,0:T(8,128)S(1)} %get-tuple-element.2362), channel_id=1, source_target_pairs={{64,0},{128,64},{192,128},{256,192},{320,256},{384,320},{448,384},... | collective-permute-start | bytes 393224 | tf_op jit(solution)/shard_map/while/body/eval_jaxpr/ppermute | solution.py:37
  492.5 7.1 collective-permute-start
  501.3 8.7 %collective-permute-start.2 = (f32[25,18,1]{2,1,0:T(8,128)S(1)}, f32[25,18,1]{2,1,0:T(8,128)S(1)}, u32[]{:S(2)}, u32[]{:S(2)}) collective-permute-start(f32[25,18,1]{2,1,0:T(8,128)S(1)} %get-tuple-element.2387), channel_id=1, source_target_pairs={{1,0},{2,1},{3,2},{5,4},{6,5},{7,6},{9,8},{10,9},{11,10},{13,12},{... | collective-permute-start | bytes 5408 | tf_op jit(solution)/shard_map/while/body/eval_jaxpr/while/body/eval_jaxpr/ppermute | solution.py:27
  503.2 8.7 %collective-permute-start.3 = (f32[25,18,1]{2,1,0:T(8,128)S(1)}, f32[25,18,1]{2,1,0:T(8,128)S(1)}, u32[]{:S(2)}, u32[]{:S(2)}) collective-permute-start(f32[25,18,1]{2,1,0:T(8,128)S(1)} %get-tuple-element.2388), channel_id=1, source_target_pairs={{0,1},{1,2},{2,3},{4,5},{5,6},{6,7},{8,9},{9,10},{10,11},{12,13},{... | collective-permute-start | bytes 5408 | tf_op jit(solution)/shard_map/while/body/eval_jaxpr/while/body/eval_jaxpr/ppermute | solution.py:25
  513.8 7.4 collective-permute-start
  522.9 8.7 %collective-permute-start.2 = (f32[25,18,1]{2,1,0:T(8,128)S(1)}, f32[25,18,1]{2,1,0:T(8,128)S(1)}, u32[]{:S(2)}, u32[]{:S(2)}) collective-permute-start(f32[25,18,1]{2,1,0:T(8,128)S(1)} %get-tuple-element.2387), channel_id=1, source_target_pairs={{1,0},{2,1},{3,2},{5,4},{6,5},{7,6},{9,8},{10,9},{11,10},{13,12},{... | collective-permute-start | bytes 5408 | tf_op jit(solution)/shard_map/while/body/eval_jaxpr/while/body/eval_jaxpr/ppermute | solution.py:27
  524.9 8.7 %collective-permute-start.3 = (f32[25,18,1]{2,1,0:T(8,128)S(1)}, f32[25,18,1]{2,1,0:T(8,128)S(1)}, u32[]{:S(2)}, u32[]{:S(2)}) collective-permute-start(f32[25,18,1]{2,1,0:T(8,128)S(1)} %get-tuple-element.2388), channel_id=1, source_target_pairs={{0,1},{1,2},{2,3},{4,5},{5,6},{6,7},{8,9},{9,10},{10,11},{12,13},{... | collective-permute-start | bytes 5408 | tf_op jit(solution)/shard_map/while/body/eval_jaxpr/while/body/eval_jaxpr/ppermute | solution.py:25
  535.3 7.9 %collective-permute-start.4 = (f32[8,16,256]{2,1,0:T(8,128)S(1)}, f32[8,16,256]{2,1,0:T(8,128)S(1)}, u32[]{:S(2)}, u32[]{:S(2)}) collective-permute-start(f32[8,16,256]{2,1,0:T(8,128)S(1)} %get-tuple-element.2362), channel_id=1, source_target_pairs={{64,0},{128,64},{192,128},{256,192},{320,256},{384,320},{448,384},... | collective-permute-start | bytes 393224 | tf_op jit(solution)/shard_map/while/body/eval_jaxpr/ppermute | solution.py:37
  552.4 8.7 %collective-permute-start.2 = (f32[25,18,1]{2,1,0:T(8,128)S(1)}, f32[25,18,1]{2,1,0:T(8,128)S(1)}, u32[]{:S(2)}, u32[]{:S(2)}) collective-permute-start(f32[25,18,1]{2,1,0:T(8,128)S(1)} %get-tuple-element.2387), channel_id=1, source_target_pairs={{1,0},{2,1},{3,2},{5,4},{6,5},{7,6},{9,8},{10,9},{11,10},{13,12},{... | collective-permute-start | bytes 5408 | tf_op jit(solution)/shard_map/while/body/eval_jaxpr/while/body/eval_jaxpr/ppermute | solution.py:27
  554.3 8.7 %collective-permute-start.3 = (f32[25,18,1]{2,1,0:T(8,128)S(1)}, f32[25,18,1]{2,1,0:T(8,128)S(1)}, u32[]{:S(2)}, u32[]{:S(2)}) collective-permute-start(f32[25,18,1]{2,1,0:T(8,128)S(1)} %get-tuple-element.2388), channel_id=1, source_target_pairs={{0,1},{1,2},{2,3},{4,5},{5,6},{6,7},{8,9},{9,10},{10,11},{12,13},{... | collective-permute-start | bytes 5408 | tf_op jit(solution)/shard_map/while/body/eval_jaxpr/while/body/eval_jaxpr/ppermute | solution.py:25
  565.0 7.4 collective-permute-start
  574.1 9.6 %collective-permute-start.2 = (f32[25,18,1]{2,1,0:T(8,128)S(1)}, f32[25,18,1]{2,1,0:T(8,128)S(1)}, u32[]{:S(2)}, u32[]{:S(2)}) collective-permute-start(f32[25,18,1]{2,1,0:T(8,128)S(1)} %get-tuple-element.2387), channel_id=1, source_target_pairs={{1,0},{2,1},{3,2},{5,4},{6,5},{7,6},{9,8},{10,9},{11,10},{13,12},{... | collective-permute-start | bytes 5408 | tf_op jit(solution)/shard_map/while/body/eval_jaxpr/while/body/eval_jaxpr/ppermute | solution.py:27
  576.0 9.6 %collective-permute-start.3 = (f32[25,18,1]{2,1,0:T(8,128)S(1)}, f32[25,18,1]{2,1,0:T(8,128)S(1)}, u32[]{:S(2)}, u32[]{:S(2)}) collective-permute-start(f32[25,18,1]{2,1,0:T(8,128)S(1)} %get-tuple-element.2388), channel_id=1, source_target_pairs={{0,1},{1,2},{2,3},{4,5},{5,6},{6,7},{8,9},{9,10},{10,11},{12,13},{... | collective-permute-start | bytes 5408 | tf_op jit(solution)/shard_map/while/body/eval_jaxpr/while/body/eval_jaxpr/ppermute | solution.py:25
  592.7 7.4 collective-permute-start
  601.9 8.7 %collective-permute-start.2 = (f32[25,18,1]{2,1,0:T(8,128)S(1)}, f32[25,18,1]{2,1,0:T(8,128)S(1)}, u32[]{:S(2)}, u32[]{:S(2)}) collective-permute-start(f32[25,18,1]{2,1,0:T(8,128)S(1)} %get-tuple-element.2387), channel_id=1, source_target_pairs={{1,0},{2,1},{3,2},{5,4},{6,5},{7,6},{9,8},{10,9},{11,10},{13,12},{... | collective-permute-start | bytes 5408 | tf_op jit(solution)/shard_map/while/body/eval_jaxpr/while/body/eval_jaxpr/ppermute | solution.py:27
  603.8 8.7 %collective-permute-start.3 = (f32[25,18,1]{2,1,0:T(8,128)S(1)}, f32[25,18,1]{2,1,0:T(8,128)S(1)}, u32[]{:S(2)}, u32[]{:S(2)}) collective-permute-start(f32[25,18,1]{2,1,0:T(8,128)S(1)} %get-tuple-element.2388), channel_id=1, source_target_pairs={{0,1},{1,2},{2,3},{4,5},{5,6},{6,7},{8,9},{9,10},{10,11},{12,13},{... | collective-permute-start | bytes 5408 | tf_op jit(solution)/shard_map/while/body/eval_jaxpr/while/body/eval_jaxpr/ppermute | solution.py:25
  614.4 7.4 collective-permute-start
  623.5 10.7 %collective-permute-start.2 = (f32[25,18,1]{2,1,0:T(8,128)S(1)}, f32[25,18,1]{2,1,0:T(8,128)S(1)}, u32[]{:S(2)}, u32[]{:S(2)}) collective-permute-start(f32[25,18,1]{2,1,0:T(8,128)S(1)} %get-tuple-element.2387), channel_id=1, source_target_pairs={{1,0},{2,1},{3,2},{5,4},{6,5},{7,6},{9,8},{10,9},{11,10},{13,12},{... | collective-permute-start | bytes 5408 | tf_op jit(solution)/shard_map/while/body/eval_jaxpr/while/body/eval_jaxpr/ppermute | solution.py:27
  625.5 10.7 %collective-permute-start.3 = (f32[25,18,1]{2,1,0:T(8,128)S(1)}, f32[25,18,1]{2,1,0:T(8,128)S(1)}, u32[]{:S(2)}, u32[]{:S(2)}) collective-permute-start(f32[25,18,1]{2,1,0:T(8,128)S(1)} %get-tuple-element.2388), channel_id=1, source_target_pairs={{0,1},{1,2},{2,3},{4,5},{5,6},{6,7},{8,9},{9,10},{10,11},{12,13},{... | collective-permute-start | bytes 5408 | tf_op jit(solution)/shard_map/while/body/eval_jaxpr/while/body/eval_jaxpr/ppermute | solution.py:25
  642.2 7.4 collective-permute-start
  651.6 10.0 %collective-permute-start.2 = (f32[25,18,1]{2,1,0:T(8,128)S(1)}, f32[25,18,1]{2,1,0:T(8,128)S(1)}, u32[]{:S(2)}, u32[]{:S(2)}) collective-permute-start(f32[25,18,1]{2,1,0:T(8,128)S(1)} %get-tuple-element.2387), channel_id=1, source_target_pairs={{1,0},{2,1},{3,2},{5,4},{6,5},{7,6},{9,8},{10,9},{11,10},{13,12},{... | collective-permute-start | bytes 5408 | tf_op jit(solution)/shard_map/while/body/eval_jaxpr/while/body/eval_jaxpr/ppermute | solution.py:27
  653.5 10.0 %collective-permute-start.3 = (f32[25,18,1]{2,1,0:T(8,128)S(1)}, f32[25,18,1]{2,1,0:T(8,128)S(1)}, u32[]{:S(2)}, u32[]{:S(2)}) collective-permute-start(f32[25,18,1]{2,1,0:T(8,128)S(1)} %get-tuple-element.2388), channel_id=1, source_target_pairs={{0,1},{1,2},{2,3},{4,5},{5,6},{6,7},{8,9},{9,10},{10,11},{12,13},{... | collective-permute-start | bytes 5408 | tf_op jit(solution)/shard_map/while/body/eval_jaxpr/while/body/eval_jaxpr/ppermute | solution.py:25
  674.3 12.0 %collective-permute-start.2 = (f32[25,18,1]{2,1,0:T(8,128)S(1)}, f32[25,18,1]{2,1,0:T(8,128)S(1)}, u32[]{:S(2)}, u32[]{:S(2)}) collective-permute-start(f32[25,18,1]{2,1,0:T(8,128)S(1)} %get-tuple-element.2387), channel_id=1, source_target_pairs={{1,0},{2,1},{3,2},{5,4},{6,5},{7,6},{9,8},{10,9},{11,10},{13,12},{... | collective-permute-start | bytes 5408 | tf_op jit(solution)/shard_map/while/body/eval_jaxpr/while/body/eval_jaxpr/ppermute | solution.py:27
  676.2 12.0 %collective-permute-start.3 = (f32[25,18,1]{2,1,0:T(8,128)S(1)}, f32[25,18,1]{2,1,0:T(8,128)S(1)}, u32[]{:S(2)}, u32[]{:S(2)}) collective-permute-start(f32[25,18,1]{2,1,0:T(8,128)S(1)} %get-tuple-element.2388), channel_id=1, source_target_pairs={{0,1},{1,2},{2,3},{4,5},{5,6},{6,7},{8,9},{9,10},{10,11},{12,13},{... | collective-permute-start | bytes 5408 | tf_op jit(solution)/shard_map/while/body/eval_jaxpr/while/body/eval_jaxpr/ppermute | solution.py:25
  702.4 11.0 %collective-permute-start.2 = (f32[25,18,1]{2,1,0:T(8,128)S(1)}, f32[25,18,1]{2,1,0:T(8,128)S(1)}, u32[]{:S(2)}, u32[]{:S(2)}) collective-permute-start(f32[25,18,1]{2,1,0:T(8,128)S(1)} %get-tuple-element.2387), channel_id=1, source_target_pairs={{1,0},{2,1},{3,2},{5,4},{6,5},{7,6},{9,8},{10,9},{11,10},{13,12},{... | collective-permute-start | bytes 5408 | tf_op jit(solution)/shard_map/while/body/eval_jaxpr/while/body/eval_jaxpr/ppermute | solution.py:27
  704.3 11.0 %collective-permute-start.3 = (f32[25,18,1]{2,1,0:T(8,128)S(1)}, f32[25,18,1]{2,1,0:T(8,128)S(1)}, u32[]{:S(2)}, u32[]{:S(2)}) collective-permute-start(f32[25,18,1]{2,1,0:T(8,128)S(1)} %get-tuple-element.2388), channel_id=1, source_target_pairs={{0,1},{1,2},{2,3},{4,5},{5,6},{6,7},{8,9},{9,10},{10,11},{12,13},{... | collective-permute-start | bytes 5408 | tf_op jit(solution)/shard_map/while/body/eval_jaxpr/while/body/eval_jaxpr/ppermute | solution.py:25
  717.2 7.7 %collective-permute-start = (f32[25,1,256]{2,1,0:T(1,128)S(1)}, f32[25,1,256]{2,1,0:T(1,128)S(1)}, u32[]{:S(2)}, u32[]{:S(2)}) collective-permute-start(f32[25,1,256]{2,1,0:T(1,128)S(1)} %get-tuple-element.2385), channel_id=1, source_target_pairs={{4,0},{8,4},{12,8},{16,12},{20,16},{24,20},{28,24},{32,28},{36,32}... | collective-permute-start | bytes 76808 | tf_op jit(solution)/shard_map/while/body/eval_jaxpr/while/body/eval_jaxpr/ppermute | solution.py:27
  726.7 10.7 %collective-permute-start.2 = (f32[25,18,1]{2,1,0:T(8,128)S(1)}, f32[25,18,1]{2,1,0:T(8,128)S(1)}, u32[]{:S(2)}, u32[]{:S(2)}) collective-permute-start(f32[25,18,1]{2,1,0:T(8,128)S(1)} %get-tuple-element.2387), channel_id=1, source_target_pairs={{1,0},{2,1},{3,2},{5,4},{6,5},{7,6},{9,8},{10,9},{11,10},{13,12},{... | collective-permute-start | bytes 5408 | tf_op jit(solution)/shard_map/while/body/eval_jaxpr/while/body/eval_jaxpr/ppermute | solution.py:27
  728.6 10.7 %collective-permute-start.3 = (f32[25,18,1]{2,1,0:T(8,128)S(1)}, f32[25,18,1]{2,1,0:T(8,128)S(1)}, u32[]{:S(2)}, u32[]{:S(2)}) collective-permute-start(f32[25,18,1]{2,1,0:T(8,128)S(1)} %get-tuple-element.2388), channel_id=1, source_target_pairs={{0,1},{1,2},{2,3},{4,5},{5,6},{6,7},{8,9},{9,10},{10,11},{12,13},{... | collective-permute-start | bytes 5408 | tf_op jit(solution)/shard_map/while/body/eval_jaxpr/while/body/eval_jaxpr/ppermute | solution.py:25
  (87 other events, 516.0 us)
where the time goes:
time: 771 us; the launch traced here: 766 us
  starting transfers between devices  477 us (62%)
  waiting for transfers between devices  229 us (30%)
  other arithmetic  49 us (6%)
    ppermute x66, starting transfers between devices, padded(): lax.ppermute(tail, axis, [(i, (i + 1) % count) for i in range(ends)])  246 us
    ppermute x66, starting transfers between devices, padded(): lax.ppermute(head, axis, [((i + 1) % count, i) for i in range(ends)])  186 us
    ppermute x66, waiting for transfers between devices, padded(): lax.ppermute(head, axis, [((i + 1) % count, i) for i in range(ends)])  97.5 us
    ppermute x66, waiting for transfers between devices, padded(): lax.ppermute(tail, axis, [(i, (i + 1) % count) for i in range(ends)])  91.3 us
    ppermute x16, starting transfers between devices, passed_along(): lax.ppermute(value, axis, [(source, source + steps) for source in range(i...  45.5 us
    ppermute x16, waiting for transfers between devices, passed_along(): lax.ppermute(value, axis, [(source, source + steps) for source in range(i...  40.3 us
  transfers between devices with their start and end apart: 148, of which 114 were waited for; matrix products, arithmetic and copies ran while one was open for 0% of the time, Pallas kernels for 0%

commit v1 on v0

v1 whole, which is shorter than its diff:
```python
import math

import jax
import jax.numpy as jnp
from jax import lax
from jax.experimental import pallas as pl
from jax.experimental.pallas import tpu as pltpu
from jax.sharding import PartitionSpec as P

SOFTMIN_TEMPER = 0.5
SURF = 0.7
AIR_SLOW = 2.5
AIR_TEST = 2.0
STEP_PENALTY = 10000.0
RATE = 1.0 / SOFTMIN_TEMPER
ROOT2 = math.sqrt(2.0)
ROOT3 = math.sqrt(3.0)

LANES = 128
STRIP = 32
ROWS = 16
PLANES = 16
SHOTS = 8
FRAME = 80
PAD = 8
FULL = FRAME + 2 * PAD
A_ROWS = 64
S_ROWS = 40
A_AT = (0, A_ROWS, 2 * A_ROWS + S_ROWS, 3 * A_ROWS + 2 * S_ROWS, 4 * A_ROWS + 3 * S_ROWS)
S_AT = (2 * A_ROWS, 3 * A_ROWS + S_ROWS, 4 * A_ROWS + 2 * S_ROWS)
HALF = 8
VMEM_BYTES = 40 * 1024 * 1024


def rolled(value, shift):
    shift = shift % LANES
    return value if shift == 0 else pltpu.roll(value, shift, value.ndim - 1)


def lane_index(rows=8):
    return lax.broadcasted_iota(jnp.int32, (rows, LANES), 1)


def quarters(parts, lane):
    out = parts[0]
    for j in range(1, len(parts)):
        out = jnp.where(lane >= STRIP * j, parts[j], out)
    return out


def pack_kernel(pos, slow_ref, air_ref, refl_ref, mask_ref, resid_ref, a_ref, s_ref):
    lane = lane_index()
    speed = {}
    for p in range(2):
        for h in range(2):
            for c in range(2):
                at = (p, pl.ds(HALF * h, HALF), pl.ds(LANES * c, LANES))
                speed[p, h, c] = jnp.where(air_ref[at] == 1, jnp.float32(AIR_SLOW), slow_ref[at])
    for target in range(8):
        c, q = divmod(target, 4)
        parts = [rolled(speed[j // 2, j % 2, c], STRIP * (j - q)) for j in range(4)]
        a_ref[pl.ds(HALF * target, HALF), :] = quarters(parts, lane)
    depth_pos = pos[0]
    high = depth_pos >= 4
    back = (LANES - STRIP * (depth_pos % 4)) % LANES

    def strip(low_part, high_part):
        return pltpu.roll(jnp.where(high, high_part, low_part), back, 1)

    for v in range(4):
        parts = []
        for i in range(4):
            x = 4 * v + i
            pieces = [
                jnp.where(
                    mask_ref[:, x, pl.ds(LANES * c, LANES)] == 1,
                    resid_ref[:, x, pl.ds(LANES * c, LANES)],
                    jnp.float32(0.0),
                )
                for c in range(2)
            ]
            parts.append(rolled(strip(*pieces), STRIP * i))
        s_ref[pl.ds(HALF * v, HALF), :] = quarters(parts, lane)
    parts = []
    for h in range(2):
        pieces = [
            refl_ref[pl.ds(HALF * h, HALF), pl.ds(LANES * c, LANES)].astype(jnp.float32)
            for c in range(2)
        ]
        parts.append(rolled(strip(*pieces), STRIP * h))
    s_ref[pl.ds(32, HALF), :] = quarters(parts, lane)


def sweep_kernel(
    pos,
    shot_ref,
    left_ref,
    here_ref,
    right_ref,
    out_ref,
    w_ref,
    e1_ref,
    e2_ref,
    e3_ref,
    gm_ref,
    gp_ref,
    hm_ref,
    hp_ref,
    head_ref,
    mu_ref,
    src_ref,
    refl_ref,
    wsel_ref,
    earth_ref,
    grad_ref,
    col_ref,
    raw_ref,
    nx_total,
    ny_total,
):
    lane = lane_index()
    sub = lax.broadcasted_iota(jnp.int32, (8, LANES), 0)
    x_base = pos[1] * ROWS - 2 * ROWS
    y_base = pos[2] * (8 * STRIP) + pos[0] * STRIP - STRIP
    y_cell = y_base + lane
    y_inside = (y_cell >= 0) & (y_cell < ny_total)
    zero = jnp.zeros((8, LANES), jnp.float32)

    def row_of(ref, lead, r):
        if lead is None:
            return ref[pl.ds(r, 8, stride=0), :]
        return ref[lead, pl.ds(r, 8, stride=0), :]

    def rim_factor(x_cell):
        inside = (x_cell >= 0) & (x_cell < nx_total) & y_inside
        penalty = jnp.where(inside, jnp.float32(0.0), jnp.float32(STEP_PENALTY))
        return jnp.exp(-penalty * RATE)

    shot_x = jnp.broadcast_to(shot_ref[:, 0:1].astype(jnp.float32), (8, LANES))
    shot_y = jnp.broadcast_to(shot_ref[:, 1:2].astype(jnp.float32), (8, LANES))
    y_square = (y_cell.astype(jnp.float32) - shot_y) ** 2

    def surface(r):
        x_cell = (x_base + r).astype(jnp.float32)
        return SURF * jnp.sqrt((x_cell - shot_x) ** 2 + y_square)

    def weight(diff):
        return jnp.exp(-diff * RATE)

    def near(diff):
        return jnp.clip(diff, -1.0, 1.0)

    def geometry(block, carry):
        before, now = carry
        for i in range(8):
            r = block * 8 + i
            after = surface(r + 1)
            gm_ref[r + PAD] = weight(near(pltpu.roll(now, 1, 1) - now))
            gp_ref[r + PAD] = weight(near(pltpu.roll(now, LANES - 1, 1) - now))
            hm_ref[r + PAD] = weight(before - now)
            hp_ref[r + PAD] = weight(after - now)
            w_ref[0, r + PAD] = rim_factor(x_base + r)
            before, now = now, after
        return before, now

    lax.fori_loop(0, FRAME // 8, geometry, (surface(-1), surface(0)))
    for ref in (gm_ref, gp_ref, hm_ref, hp_ref):
        ref[PAD - 1] = zero
        ref[PAD + FRAME] = zero
    for k in range(PLANES + 1):
        low, high = (-1, FRAME) if k < 8 else (7, FRAME - 8)
        w_ref[k, low + PAD] = zero
        w_ref[k, high + PAD] = zero

    def merged(tiles, j):
        part = tiles[0]
        one, two = (j + 1) % 4, (j + 2) % 4
        part = jnp.where((lane >= STRIP * one) & (lane < STRIP * (one + 1)), tiles[1], part)
        part = jnp.where((lane >= STRIP * two) & (lane < STRIP * (two + 1)), tiles[2], part)
        return rolled(part, -STRIP * j)

    def strips(row):
        at = (pl.ds(row, HALF), slice(None))
        return left_ref[at], rolled(here_ref[at], STRIP), rolled(right_ref[at], 2 * STRIP)

    rims = [rim_factor(x_base + HALF * g + sub) for g in range(FRAME // HALF)]

    def exponents(pair, carry):
        for offset in range(5):
            tiles = strips(pl.multiple_of(A_AT[offset] + HALF * pair, HALF))
            for j in range(4):
                p, h = divmod(j, 2)
                group = 2 * offset + h
                speed = merged(tiles, j)
                at = (2 * pair + p, pl.ds(HALF * group, HALF), slice(None))
                e1_ref[at] = jnp.exp(-speed * RATE) * rims[group]
                e2_ref[at] = jnp.exp(-(speed * ROOT2) * RATE) * rims[group]
                e3_ref[at] = jnp.exp(-(speed * ROOT3) * RATE) * rims[group]
                if 3 <= group < 7:
                    here = (2 * pair + p, pl.ds(HALF * (group - 3), HALF), slice(None))
                    earth_ref[here] = speed
        return carry

    lax.fori_loop(0, PLANES // 2, exponents, 0)

    for offset in range(3):
        for v in range(4):
            tiles = strips(S_AT[offset] + HALF * v)
            for i in range(4):
                src_ref[ROWS * offset + 4 * v + i] = merged(tiles, i)
        tiles = strips(S_AT[offset] + 32)
        for h in range(2):
            inside = rims[2 + 2 * offset + h] > 0.5
            refl_ref[pl.ds(ROWS * offset + HALF * h, HALF), :] = jnp.where(
                inside, merged(tiles, h), jnp.float32(-1.0)
            )

    def clear(r, carry):
        wsel_ref[r] = zero + 1.0
        return carry

    lax.fori_loop(0, 48, clear, 0)

    def along_y(value, r):
        return (
            gm_ref[r + PAD] * pltpu.roll(value, 1, 1)
            + gp_ref[r + PAD] * pltpu.roll(value, LANES - 1, 1)
        )

    def down_rows(k, first, last, carry, select, keep):
        level = k.astype(jnp.float32)

        def block(b, carry):
            w_before, q_before, w_now, q_now = carry
            for i in range(8):
                r = b * 8 + i
                w_after = w_ref[k, r + 1 + PAD]
                q_after = along_y(w_after, r + 1)
                hm = hm_ref[r + PAD]
                hp = hp_ref[r + PAD]
                edge = q_now + (hm * w_before + hp * w_after)
                corner = hm * q_before + hp * q_after
                part1 = row_of(e1_ref, k, r) * w_now
                part2 = row_of(e2_ref, k, r) * edge
                part3 = row_of(e3_ref, k, r) * corner
                w_next = part1 + part2 + part3
                w_ref[k + 1, r + PAD] = w_next
                if keep:
                    head_ref[k, r - 24] = part1 + ROOT2 * part2 + ROOT3 * part3
                if select:
                    hit = row_of(refl_ref, None, r - 16) == level
                    wsel_ref[r - 16] = jnp.where(hit, w_next, wsel_ref[r - 16])
                w_before, q_before, w_now, q_now = w_now, q_now, w_after, q_after
            return w_before, q_before, w_now, q_now

        return lax.fori_loop(first, last, block, carry)

    def down(first_block, segments):
        def plane(k, carry):
            r = first_block * 8
            w_before, w_now = w_ref[k, r - 1 + PAD], w_ref[k, r + PAD]
            state = (w_before, along_y(w_before, r - 1), w_now, along_y(w_now, r))
            for first, last, select, keep in segments:
                state = down_rows(k, first, last, state, select, keep)
            return carry

        return plane

    lax.fori_loop(
        0, 4, down(0, ((0, 3, False, False), (3, 7, False, True), (7, 10, False, False))), 0
    )
    hits = ((2, 3, True, False), (3, 7, True, True), (7, 8, True, False))
    lax.fori_loop(
        4, 7, down(0, ((0, 2, False, False), *hits, (8, 10, False, False))), 0
    )
    lax.fori_loop(
        7, PLANES, down(1, ((1, 2, False, False), *hits, (8, 9, False, False))), 0
    )

    mu_ref[15 + PAD] = zero
    mu_ref[64 + PAD] = zero

    def start(r, carry):
        share = src_ref[r] / wsel_ref[r]
        wsel_ref[r] = share
        hit = row_of(refl_ref, None, r) == float(PLANES - 1)
        mu_ref[r + 16 + PAD] = jnp.where(hit, share, jnp.float32(0.0))
        return carry

    lax.fori_loop(0, 48, start, 0)
    for i in range(18):
        col_ref[i : i + 1, :] = jnp.sum(src_ref[15 + i], axis=0, keepdims=True)

    def gradient_rows(k):
        for i in range(18):
            product = mu_ref[31 + i + PAD] * head_ref[k, 7 + i]
            grad_ref[k, i : i + 1, :] = jnp.sum(product, axis=0, keepdims=True)

    def spread(k, r):
        mu = mu_ref[r + PAD]
        u2 = row_of(e2_ref, k, r) * mu
        u3 = row_of(e3_ref, k, r) * mu
        hm = hm_ref[r + PAD]
        hp = hp_ref[r + PAD]
        return row_of(e1_ref, k, r) * mu, u2, hp * u2, hp * u3, hm * u2, hm * u3

    def up(first_block, last_block, base):
        def plane(step, carry):
            k = base - step
            gradient_rows(k)
            level = (k - 1).astype(jnp.float32)

            def block(b, carry):
                a_before, c_before, u1, u2, a_now, c_now = carry
                for i in range(8):
                    r = b * 8 + i
                    n1, n2, a_next, c_next, a_back, c_back = spread(k, r + 1)
                    both = u2 + (c_before + c_back)
                    side = pltpu.roll(gp_ref[r + PAD] * both, 1, 1) + pltpu.roll(
                        gm_ref[r + PAD] * both, LANES - 1, 1
                    )
                    hit = row_of(refl_ref, None, r - 16) == level
                    own = jnp.where(hit, wsel_ref[r - 16], jnp.float32(0.0))
                    mu_ref[r + PAD] = (u1 + own) + (a_before + a_back) + side
                    a_before, c_before, u1, u2, a_now, c_now = a_now, c_now, n1, n2, a_next, c_next
                return a_before, c_before, u1, u2, a_now, c_now

            _, _, a_before, c_before, _, _ = spread(k, first_block * 8 - 1)
            u1, u2, a_now, c_now, _, _ = spread(k, first_block * 8)
            lax.fori_loop(
                first_block, last_block, block, (a_before, c_before, u1, u2, a_now, c_now)
            )
            return carry

        return plane

    lax.fori_loop(0, 7, up(2, 8, 15), 0)
    lax.fori_loop(0, 8, up(3, 7, 8), 0)
    gradient_rows(0)

    def finish(pair, carry):
        parts = []
        for p in range(2):
            k = 2 * pair + p
            shown = jnp.where(
                k.astype(jnp.float32) <= refl_ref[15:33, :], col_ref[0:18, :], jnp.float32(0.0)
            )
            raw_ref[p, 0:18, :] = jnp.where(
                earth_ref[k, 7:25, :] < AIR_TEST, grad_ref[k, 0:18, :] + shown, jnp.float32(0.0)
            )
            for h in range(2):
                mid = raw_ref[p, HALF * h + 1 : HALF * h + 9, :]
                column = (raw_ref[p, HALF * h : HALF * h + 8, :] + mid) + raw_ref[
                    p, HALF * h + 2 : HALF * h + 10, :
                ]
                total = column + (pltpu.roll(column, 1, 1) + pltpu.roll(column, LANES - 1, 1))
                smooth = 0.4375 * mid + 0.0625 * total
                parts.append(rolled(smooth, STRIP * (2 * p + h - 1)))
        out_ref[pl.ds(pl.multiple_of(HALF * pair, HALF), HALF), :] = quarters(parts, lane)
        return carry

    lax.fori_loop(0, PLANES // 2, finish, 0)


def unpack_kernel(in_ref, out_ref):
    lane = lane_index()
    for c in range(2):
        tiles = [in_ref[pl.ds(HALF * (4 * c + q), HALF), :] for q in range(4)]
        for j in range(4):
            parts = [rolled(tiles[q], STRIP * (q - j)) for q in range(4)]
            out_ref[j // 2, pl.ds(HALF * (j % 2), HALF), pl.ds(LANES * c, LANES)] = quarters(
                parts, lane
            )


def in_vmem(count):
    return [pl.BlockSpec(memory_space=pltpu.VMEM)] * count


def line(count, shift):
    return [(i, i + shift) for i in range(count) if 0 <= i + shift < count]


def local(slowness, air_mask, reflector, shot_cells, receiver_mask, residual):
    depth_count = lax.axis_size("depth")
    x_count = lax.axis_size("gx")
    y_count = lax.axis_size("gy")
    nx_total = ROWS * x_count
    ny_total = STRIP * depth_count * y_count
    pos = jnp.stack(
        [lax.axis_index("depth"), lax.axis_index("gx"), lax.axis_index("gy")]
    ).astype(jnp.int32)
    smem = pl.BlockSpec(memory_space=pltpu.SMEM)
    f32 = jnp.float32

    packed, sources = pl.pallas_call(
        pack_kernel,
        out_shape=(
            jax.ShapeDtypeStruct((A_ROWS, LANES), f32),
            jax.ShapeDtypeStruct((S_ROWS, LANES), f32),
        ),
        in_specs=[smem, *in_vmem(5)],
        out_specs=tuple(in_vmem(2)),
        name="pack",
    )(pos, slowness, air_mask, reflector, receiver_mask, residual)

    strip = lax.all_to_all(
        packed.reshape(8, HALF, LANES), "depth", 0, 0, tiled=True
    ).reshape(A_ROWS, LANES)
    whole = jnp.concatenate([strip, sources], 0)
    above1 = lax.ppermute(whole, "gx", line(x_count, 1))
    below1 = lax.ppermute(whole, "gx", line(x_count, -1))
    above2 = lax.ppermute(strip, "gx", line(x_count, 2))
    below2 = lax.ppermute(strip, "gx", line(x_count, -2))
    column = jnp.concatenate([above2, above1, whole, below1, below2], 0)

    def place(q):
        return (q % depth_count) * y_count + q // depth_count

    def along(shift):
        return [(place(i), place(j)) for i, j in line(depth_count * y_count, shift)]

    left = lax.ppermute(column, ("depth", "gy"), along(1))
    right = lax.ppermute(column, ("depth", "gy"), along(-1))

    def kernel(*refs):
        sweep_kernel(*refs, nx_total=nx_total, ny_total=ny_total)

    field = (FULL, SHOTS, LANES)
    strips_out = pl.pallas_call(
        kernel,
        out_shape=jax.ShapeDtypeStruct((A_ROWS, LANES), f32),
        in_specs=[smem, *in_vmem(4)],
        out_specs=in_vmem(1)[0],
        scratch_shapes=[
            pltpu.VMEM((PLANES + 1, *field), f32),
            *[pltpu.VMEM((PLANES, FULL, LANES), f32)] * 3,
            *[pltpu.VMEM(field, f32)] * 4,
            pltpu.VMEM((PLANES, 32, SHOTS, LANES), f32),
            pltpu.VMEM(field, f32),
            pltpu.VMEM((48, SHOTS, LANES), f32),
            pltpu.VMEM((56, LANES), f32),
            pltpu.VMEM((48, SHOTS, LANES), f32),
            pltpu.VMEM((PLANES, 32, LANES), f32),
            pltpu.VMEM((PLANES, 24, LANES), f32),
            pltpu.VMEM((24, LANES), f32),
            pltpu.VMEM((2, 24, LANES), f32),
        ],
        compiler_params=pltpu.CompilerParams(vmem_limit_bytes=VMEM_BYTES),
        name="sweep",
    )(pos, shot_cells, left, column, right)

    parts = lax.all_to_all(
        strips_out.reshape(8, HALF, LANES), "depth", 0, 0, tiled=True
    ).reshape(A_ROWS, LANES)
    return pl.pallas_call(
        unpack_kernel,
        out_shape=jax.ShapeDtypeStruct(slowness.shape, f32),
        in_specs=in_vmem(1),
        out_specs=in_vmem(1)[0],
        name="unpack",
    )(parts)


def solution(mesh):
    in_specs = (
        P("depth", "gx", "gy"),
        P("depth", "gx", "gy"),
        P("gx", "gy"),
        P(),
        P(None, "gx", "gy"),
        P(None, "gx", "gy"),
    )
    out_specs = P("depth", "gx", "gy")
    return jax.shard_map(local, mesh=mesh, in_specs=in_specs, out_specs=out_specs, check_vma=False)
```

time: 771 us -> 79 us (0.10)
  the two profiles are of different devices: /device:TPU:356 before, /device:TPU:388 now
where the time goes in v1:
time: 79 us; the launch traced here: 78.6 us
  Pallas kernels  28.6 us (36%)
  blocking collectives  18.5 us (23%)
  starting transfers between devices  18.3 us (23%)
  waiting for transfers between devices  12.2 us (15%)
    pallas_call x1, Pallas kernels, local(): pl.pallas_call(kernel, out_shape=jax.ShapeDtypeStruct((A_ROWS, LANES), f3...  25.2 us
    all_to_all x1, blocking collectives, local(): lax.all_to_all(packed.reshape(8, HALF, LANES), 'depth', 0, 0, tiled=True)  10 us
    all_to_all x1, blocking collectives, local(): lax.all_to_all(strips_out.reshape(8, HALF, LANES), 'depth', 0, 0, tiled=T...  8.49 us
    ppermute x1, waiting for transfers between devices, local(): left = lax.ppermute(column, ('depth', 'gy'), along(1))  5.93 us
    ppermute x1, starting transfers between devices, local(): below1 = lax.ppermute(whole, 'gx', line(x_count, -1))  5.34 us
    ppermute x1, waiting for transfers between devices, local(): above1 = lax.ppermute(whole, 'gx', line(x_count, 1))  5.29 us
    ppermute x1, starting transfers between devices, local(): below2 = lax.ppermute(strip, 'gx', line(x_count, -2))  4.56 us
    ppermute x1, starting transfers between devices, local(): left = lax.ppermute(column, ('depth', 'gy'), along(1))  2.41 us
  transfers between devices with their start and end apart: 6, of which 3 were waited for; matrix products, arithmetic and copies ran while one was open for 0% of the time, Pallas kernels for 0%

profile of v1, /device:TPU:388, one launch (start us, length us, event | category | flops | bytes accessed | tf_op | source)
XLA Modules:
  0.0 78.6 jit_solution(9901216803023592868)
XLA Ops:
  0.0 0.7 pad_add_fusion.pos.refs_0_
  0.7 1.9 %pack.1 = (f32[64,128]{1,0:T(8,128)}, f32[40,128]{1,0:T(8,128)}) custom-call(s32[3]{0:T(128)} %pad_add_fusion.pos.refs_0_, f32[2,16,256]{2,1,0:T(8,128)} %slow_ref.1, s32[2,16,256]{2,1,0:T(8,128)} %air_ref.1, s32[16,256]{1,0:T(8,128)} %refl_ref.1, s32[8,16,256]{2,1,0:T(8,128)} %mask_ref.1, f32[8,16,256]{2,1,0:T(8,128)} %resid_ref.1), custom_call_target="tpu_custom_call" | custom-call | tf_op jit(solution)/shard_map/pack/pallas_call | solution.py:396
  2.5 0.0 copy-start.1
  2.5 10.0 %all_to_all.10 = f32[8,8,128]{2,1,0:T(8,128)S(1)} all-to-all(f32[8,8,128]{2,1,0:T(8,128)} %bitcast.13), channel_id=1, replica_groups=mesh['depth'=8,'gx'=16,'gy'=4] {'depth'}, dimensions={0} | all-to-all | bytes 65536 | tf_op jit(solution)/shard_map/all_to_all | solution.py:407
  12.6 4.6 %collective-permute-start.3 = (f32[64,128]{1,0:T(8,128)S(1)}, f32[64,128]{1,0:T(8,128)S(1)}, u32[]{:S(2)}, u32[]{:S(2)}) collective-permute-start(f32[64,128]{1,0:T(8,128)S(1)} %bitcast.9), channel_id=1, source_target_pairs={{8,0},{12,4},{16,8},{20,12},{24,16},{28,20},{32,24},{36,28},{40,32... | collective-permute-start | bytes 98312 | tf_op jit(solution)/shard_map/ppermute | solution.py:414
  17.1 2.2 %collective-permute-start = (f32[64,128]{1,0:T(8,128)S(1)}, f32[64,128]{1,0:T(8,128)S(1)}, u32[]{:S(2)}, u32[]{:S(2)}) collective-permute-start(f32[64,128]{1,0:T(8,128)S(1)} %bitcast.10), channel_id=1, source_target_pairs={{0,8},{4,12},{8,16},{12,20},{16,24},{20,28},{24,32},{28,36},{32,40... | collective-permute-start | bytes 98312 | tf_op jit(solution)/shard_map/ppermute | solution.py:413
  19.3 0.0 copy-done.1
  19.4 5.3 %collective-permute-start.2 = (f32[104,128]{1,0:T(8,128)S(1)}, f32[104,128]{1,0:T(8,128)S(1)}, u32[]{:S(2)}, u32[]{:S(2)}) collective-permute-start(f32[104,128]{1,0:T(8,128)S(1)} %pad_maximum_fusion), channel_id=1, source_target_pairs={{4,0},{8,4},{12,8},{16,12},{20,16},{24,20},{28,24},{32,28},{36,32}... | collective-permute-start | bytes 159752 | tf_op jit(solution)/shard_map/ppermute | solution.py:412
  24.7 1.9 %collective-permute-start.1 = (f32[104,128]{1,0:T(8,128)S(1)}, f32[104,128]{1,0:T(8,128)S(1)}, u32[]{:S(2)}, u32[]{:S(2)}) collective-permute-start(f32[104,128]{1,0:T(8,128)S(1)} %pad_maximum_fusion), channel_id=1, source_target_pairs={{0,4},{4,8},{8,12},{12,16},{16,20},{20,24},{24,28},{28,32},{32,36}... | collective-permute-start | bytes 159752 | tf_op jit(solution)/shard_map/ppermute | solution.py:411
  26.6 0.0 collective-permute-done
  26.6 5.3 %collective-permute-done.1 = f32[104,128]{1,0:T(8,128)S(1)} collective-permute-done((f32[104,128]{1,0:T(8,128)S(1)}, f32[104,128]{1,0:T(8,128)S(1)}, u32[]{:S(2)}, u32[]{:S(2)}) %collective-permute-start.1) | collective-permute-done | bytes 53280 | tf_op jit(solution)/shard_map/ppermute | solution.py:411
  32.0 0.0 collective-permute-done.2
  32.0 0.0 copy-start.2
  32.0 0.0 collective-permute-done.3
  32.0 0.0 copy-start
  32.0 1.9 %collective-permute-start.5 = (f32[440,128]{1,0:T(8,128)S(1)}, f32[440,128]{1,0:T(8,128)S(1)}, u32[]{:S(2)}, u32[]{:S(2)}) collective-permute-start(f32[440,128]{1,0:T(8,128)S(1)} %constant_dynamic-update-slice_fusion.refs_3_), channel_id=1, source_target_pairs={{64,0},{128,64},{192,128},{256,192},{320,256},{384,320},{448,384},... | collective-permute-start | bytes 675848 | tf_op jit(solution)/shard_map/ppermute | solution.py:424
  34.0 2.4 %collective-permute-start.4 = (f32[440,128]{1,0:T(8,128)S(1)}, f32[440,128]{1,0:T(8,128)S(1)}, u32[]{:S(2)}, u32[]{:S(2)}) collective-permute-start(f32[440,128]{1,0:T(8,128)S(1)} %constant_dynamic-update-slice_fusion.refs_3_), channel_id=1, source_target_pairs={{0,64},{64,128},{128,192},{192,256},{256,320},{320,384},{384,448},... | collective-permute-start | bytes 675848 | tf_op jit(solution)/shard_map/ppermute | solution.py:423
  36.4 0.0 copy-done.2
  36.4 0.1 copy.7.refs_1_
  36.5 1.0 %collective-permute-done.5.refs_4_ = f32[440,128]{1,0:T(8,128)S(1)} collective-permute-done((f32[440,128]{1,0:T(8,128)S(1)}, f32[440,128]{1,0:T(8,128)S(1)}, u32[]{:S(2)}, u32[]{:S(2)}) %collective-permute-start.5) | collective-permute-done | bytes 225312 | tf_op jit(solution)/shard_map/ppermute | solution.py:424
  37.4 5.9 %collective-permute-done.4.refs_2_ = f32[440,128]{1,0:T(8,128)S(1)} collective-permute-done((f32[440,128]{1,0:T(8,128)S(1)}, f32[440,128]{1,0:T(8,128)S(1)}, u32[]{:S(2)}, u32[]{:S(2)}) %collective-permute-start.4) | collective-permute-done | bytes 225312 | tf_op jit(solution)/shard_map/ppermute | solution.py:423
  43.4 0.0 copy-done
  43.4 25.2 %sweep.1 = f32[64,128]{1,0:T(8,128)S(1)} custom-call(s32[3]{0:T(128)S(1)} %copy-done, s32[8,2]{1,0:T(8,128)S(1)} %copy.7.refs_1_, f32[440,128]{1,0:T(8,128)S(1)} %collective-permute-done.4.refs_2_, f32[440,128]{1,0:T(8,128)S(1)} %constant_dynamic-update-slice_fusion.refs_3_, f32[440,128]{1,0:T(8,128)S(1)} %collective-permute-done.5.refs_4_), custom_call_target="tpu_custom_call" | custom-call | tf_op jit(solution)/shard_map/sweep/pallas_call | solution.py:430
  68.6 8.5 %all_to_all.11 = f32[8,8,128]{2,1,0:T(8,128)} all-to-all(f32[8,8,128]{2,1,0:T(8,128)S(1)} %bitcast.8), channel_id=1, replica_groups=mesh['depth'=8,'gx'=16,'gy'=4] {'depth'}, dimensions={0} | all-to-all | bytes 65536 | tf_op jit(solution)/shard_map/all_to_all | solution.py:453
  77.1 1.5 %unpack.1 = f32[2,16,256]{2,1,0:T(8,128)} custom-call(f32[64,128]{1,0:T(8,128)} %bitcast.12), custom_call_target="tpu_custom_call" | custom-call | tf_op jit(solution)/shard_map/unpack/pallas_call | solution.py:456
  (7 shorter events, 0.0 us)
Async XLA Ops:
  2.5 16.8 %copy-start.1 = (f32[40,128]{1,0:T(8,128)S(1)}, f32[40,128]{1,0:T(8,128)}, u32[]{:S(2)}) copy-start(f32[40,128]{1,0:T(8,128)} %get-tuple-element.8) | copy-start | bytes 61444
  12.6 19.4 %collective-permute-start.3 = (f32[64,128]{1,0:T(8,128)S(1)}, f32[64,128]{1,0:T(8,128)S(1)}, u32[]{:S(2)}, u32[]{:S(2)}) collective-permute-start(f32[64,128]{1,0:T(8,128)S(1)} %bitcast.9), channel_id=1, source_target_pairs={{8,0},{12,4},{16,8},{20,12},{24,16},{28,20},{32,24},{36,28},{40,32... | collective-permute-start | bytes 98312 | tf_op jit(solution)/shard_map/ppermute | solution.py:414
  17.1 9.5 %collective-permute-start = (f32[64,128]{1,0:T(8,128)S(1)}, f32[64,128]{1,0:T(8,128)S(1)}, u32[]{:S(2)}, u32[]{:S(2)}) collective-permute-start(f32[64,128]{1,0:T(8,128)S(1)} %bitcast.10), channel_id=1, source_target_pairs={{0,8},{4,12},{8,16},{12,20},{16,24},{20,28},{24,32},{28,36},{32,40... | collective-permute-start | bytes 98312 | tf_op jit(solution)/shard_map/ppermute | solution.py:413
  19.4 12.6 %collective-permute-start.2 = (f32[104,128]{1,0:T(8,128)S(1)}, f32[104,128]{1,0:T(8,128)S(1)}, u32[]{:S(2)}, u32[]{:S(2)}) collective-permute-start(f32[104,128]{1,0:T(8,128)S(1)} %pad_maximum_fusion), channel_id=1, source_target_pairs={{4,0},{8,4},{12,8},{16,12},{20,16},{24,20},{28,24},{32,28},{36,32}... | collective-permute-start | bytes 159752 | tf_op jit(solution)/shard_map/ppermute | solution.py:412
  24.7 7.2 %collective-permute-start.1 = (f32[104,128]{1,0:T(8,128)S(1)}, f32[104,128]{1,0:T(8,128)S(1)}, u32[]{:S(2)}, u32[]{:S(2)}) collective-permute-start(f32[104,128]{1,0:T(8,128)S(1)} %pad_maximum_fusion), channel_id=1, source_target_pairs={{0,4},{4,8},{8,12},{12,16},{16,20},{20,24},{24,28},{28,32},{32,36}... | collective-permute-start | bytes 159752 | tf_op jit(solution)/shard_map/ppermute | solution.py:411
  32.0 4.4 %copy-start.2 = (s32[8,2]{0,1:T(2,128)S(1)}, s32[8,2]{0,1:T(2,128)}, u32[]{:S(2)}) copy-start(s32[8,2]{0,1:T(2,128)} %param.9) | copy-start | bytes 196
  32.0 11.3 %copy-start = (s32[3]{0:T(128)S(1)}, s32[3]{0:T(128)}, u32[]{:S(2)}) copy-start(s32[3]{0:T(128)} %pad_add_fusion.pos.refs_0_) | copy-start | bytes 40
  32.0 5.4 %collective-permute-start.5 = (f32[440,128]{1,0:T(8,128)S(1)}, f32[440,128]{1,0:T(8,128)S(1)}, u32[]{:S(2)}, u32[]{:S(2)}) collective-permute-start(f32[440,128]{1,0:T(8,128)S(1)} %constant_dynamic-update-slice_fusion.refs_3_), channel_id=1, source_target_pairs={{64,0},{128,64},{192,128},{256,192},{320,256},{384,320},{448,384},... | collective-permute-start | bytes 675848 | tf_op jit(solution)/shard_map/ppermute | solution.py:424
  34.0 9.4 %collective-permute-start.4 = (f32[440,128]{1,0:T(8,128)S(1)}, f32[440,128]{1,0:T(8,128)S(1)}, u32[]{:S(2)}, u32[]{:S(2)}) collective-permute-start(f32[440,128]{1,0:T(8,128)S(1)} %constant_dynamic-update-slice_fusion.refs_3_), channel_id=1, source_target_pairs={{0,64},{64,128},{128,192},{192,256},{256,320},{320,384},{384,448},... | collective-permute-start | bytes 675848 | tf_op jit(solution)/shard_map/ppermute | solution.py:423

commit v2 on v1

--- a/solution.py
+++ b/solution.py
@@ -28,6 +28,7 @@
 S_ROWS = 40
 A_AT = (0, A_ROWS, 2 * A_ROWS + S_ROWS, 3 * A_ROWS + 2 * S_ROWS, 4 * A_ROWS + 3 * S_ROWS)
 S_AT = (2 * A_ROWS, 3 * A_ROWS + S_ROWS, 4 * A_ROWS + 2 * S_ROWS)
+GEOMETRY = 40
 HALF = 8
 VMEM_BYTES = 40 * 1024 * 1024
 
@@ -98,7 +99,8 @@
     here_ref,
     right_ref,
     out_ref,
-    w_ref,
+    wa_ref,
+    wb_ref,
     e1_ref,
     e2_ref,
     e3_ref,
@@ -107,7 +109,8 @@
     hm_ref,
     hp_ref,
     head_ref,
-    mu_ref,
+    ma_ref,
+    mb_ref,
     src_ref,
     refl_ref,
     wsel_ref,
@@ -152,25 +155,24 @@
 
     def geometry(block, carry):
         before, now = carry
-        for i in range(8):
-            r = block * 8 + i
+        for i in range(GEOMETRY):
+            r = block * GEOMETRY + i
             after = surface(r + 1)
             gm_ref[r + PAD] = weight(near(pltpu.roll(now, 1, 1) - now))
             gp_ref[r + PAD] = weight(near(pltpu.roll(now, LANES - 1, 1) - now))
             hm_ref[r + PAD] = weight(before - now)
             hp_ref[r + PAD] = weight(after - now)
-            w_ref[0, r + PAD] = rim_factor(x_base + r)
+            wa_ref[r + PAD] = rim_factor(x_base + r)
             before, now = now, after
         return before, now
 
-    lax.fori_loop(0, FRAME // 8, geometry, (surface(-1), surface(0)))
+    lax.fori_loop(0, FRAME // GEOMETRY, geometry, (surface(-1), surface(0)))
     for ref in (gm_ref, gp_ref, hm_ref, hp_ref):
         ref[PAD - 1] = zero
         ref[PAD + FRAME] = zero
-    for k in range(PLANES + 1):
-        low, high = (-1, FRAME) if k < 8 else (7, FRAME - 8)
-        w_ref[k, low + PAD] = zero
-        w_ref[k, high + PAD] = zero
+    for ref in (wa_ref, wb_ref):
+        ref[PAD - 1] = zero
+        ref[PAD + FRAME] = zero
 
     def merged(tiles, j):
         part = tiles[0]
@@ -215,11 +217,8 @@
                 inside, merged(tiles, h), jnp.float32(-1.0)
             )
 
-    def clear(r, carry):
+    for r in range(48):
         wsel_ref[r] = zero + 1.0
-        return carry
-
-    lax.fori_loop(0, 48, clear, 0)
 
     def along_y(value, r):
         return (
@@ -227,139 +226,118 @@
             + gp_ref[r + PAD] * pltpu.roll(value, LANES - 1, 1)
         )
 
-    def down_rows(k, first, last, carry, select, keep):
+    def down_plane(k, w_ref, next_ref, first, last, select):
         level = k.astype(jnp.float32)
-
-        def block(b, carry):
-            w_before, q_before, w_now, q_now = carry
-            for i in range(8):
-                r = b * 8 + i
-                w_after = w_ref[k, r + 1 + PAD]
-                q_after = along_y(w_after, r + 1)
-                hm = hm_ref[r + PAD]
-                hp = hp_ref[r + PAD]
-                edge = q_now + (hm * w_before + hp * w_after)
-                corner = hm * q_before + hp * q_after
-                part1 = row_of(e1_ref, k, r) * w_now
-                part2 = row_of(e2_ref, k, r) * edge
-                part3 = row_of(e3_ref, k, r) * corner
-                w_next = part1 + part2 + part3
-                w_ref[k + 1, r + PAD] = w_next
-                if keep:
-                    head_ref[k, r - 24] = part1 + ROOT2 * part2 + ROOT3 * part3
-                if select:
-                    hit = row_of(refl_ref, None, r - 16) == level
-                    wsel_ref[r - 16] = jnp.where(hit, w_next, wsel_ref[r - 16])
-                w_before, q_before, w_now, q_now = w_now, q_now, w_after, q_after
-            return w_before, q_before, w_now, q_now
-
-        return lax.fori_loop(first, last, block, carry)
-
-    def down(first_block, segments):
-        def plane(k, carry):
-            r = first_block * 8
-            w_before, w_now = w_ref[k, r - 1 + PAD], w_ref[k, r + PAD]
-            state = (w_before, along_y(w_before, r - 1), w_now, along_y(w_now, r))
-            for first, last, select, keep in segments:
-                state = down_rows(k, first, last, state, select, keep)
+        w_before, w_now = w_ref[first - 1 + PAD], w_ref[first + PAD]
+        q_before, q_now = along_y(w_before, first - 1), along_y(w_now, first)
+        for r in range(first, last):
+            w_after = w_ref[r + 1 + PAD]
+            q_after = along_y(w_after, r + 1)
+            hm = hm_ref[r + PAD]
+            hp = hp_ref[r + PAD]
+            edge = q_now + (hm * w_before + hp * w_after)
+            corner = hm * q_before + hp * q_after
+            part1 = row_of(e1_ref, k, r) * w_now
+            part2 = row_of(e2_ref, k, r) * edge
+            part3 = row_of(e3_ref, k, r) * corner
+            w_next = part1 + part2 + part3
+            next_ref[r + PAD] = w_next
+            if 31 <= r < 49:
+                head_ref[k, r - 31] = part1 + ROOT2 * part2 + ROOT3 * part3
+            if select and 16 <= r < 64:
+                hit = row_of(refl_ref, None, r - 16) == level
+                wsel_ref[r - 16] = jnp.where(hit, w_next, wsel_ref[r - 16])
+            w_before, q_before, w_now, q_now = w_now, q_now, w_after, q_after
+
+    def down(first, last, select):
+        def two(i, carry):
+            down_plane(2 * i, wa_ref, wb_ref, first, last, select)
+            down_plane(2 * i + 1, wb_ref, wa_ref, first, last, select)
             return carry
 
-        return plane
-
-    lax.fori_loop(
-        0, 4, down(0, ((0, 3, False, False), (3, 7, False, True), (7, 10, False, False))), 0
-    )
-    hits = ((2, 3, True, False), (3, 7, True, True), (7, 8, True, False))
-    lax.fori_loop(
-        4, 7, down(0, ((0, 2, False, False), *hits, (8, 10, False, False))), 0
-    )
-    lax.fori_loop(
-        7, PLANES, down(1, ((1, 2, False, False), *hits, (8, 9, False, False))), 0
-    )
-
-    mu_ref[15 + PAD] = zero
-    mu_ref[64 + PAD] = zero
-
-    def start(r, carry):
+        return two
+
+    lax.fori_loop(0, 2, down(1, 79, False), 0)
+    lax.fori_loop(2, 4, down(5, 75, True), 0)
+    lax.fori_loop(4, 8, down(9, 71, True), 0)
+
+    for ref in (ma_ref, mb_ref):
+        ref[15 + PAD] = zero
+        ref[64 + PAD] = zero
+
+    for r in range(48):
         share = src_ref[r] / wsel_ref[r]
         wsel_ref[r] = share
         hit = row_of(refl_ref, None, r) == float(PLANES - 1)
-        mu_ref[r + 16 + PAD] = jnp.where(hit, share, jnp.float32(0.0))
-        return carry
-
-    lax.fori_loop(0, 48, start, 0)
+        ma_ref[r + 16 + PAD] = jnp.where(hit, share, jnp.float32(0.0))
     for i in range(18):
         col_ref[i : i + 1, :] = jnp.sum(src_ref[15 + i], axis=0, keepdims=True)
 
-    def gradient_rows(k):
+    def gradient_rows(k, mu_ref):
         for i in range(18):
-            product = mu_ref[31 + i + PAD] * head_ref[k, 7 + i]
+            product = mu_ref[31 + i + PAD] * head_ref[k, i]
             grad_ref[k, i : i + 1, :] = jnp.sum(product, axis=0, keepdims=True)
 
-    def spread(k, r):
-        mu = mu_ref[r + PAD]
-        u2 = row_of(e2_ref, k, r) * mu
-        u3 = row_of(e3_ref, k, r) * mu
-        hm = hm_ref[r + PAD]
-        hp = hp_ref[r + PAD]
-        return row_of(e1_ref, k, r) * mu, u2, hp * u2, hp * u3, hm * u2, hm * u3
-
-    def up(first_block, last_block, base):
-        def plane(step, carry):
-            k = base - step
-            gradient_rows(k)
-            level = (k - 1).astype(jnp.float32)
-
-            def block(b, carry):
-                a_before, c_before, u1, u2, a_now, c_now = carry
-                for i in range(8):
-                    r = b * 8 + i
-                    n1, n2, a_next, c_next, a_back, c_back = spread(k, r + 1)
-                    both = u2 + (c_before + c_back)
-                    side = pltpu.roll(gp_ref[r + PAD] * both, 1, 1) + pltpu.roll(
-                        gm_ref[r + PAD] * both, LANES - 1, 1
-                    )
-                    hit = row_of(refl_ref, None, r - 16) == level
-                    own = jnp.where(hit, wsel_ref[r - 16], jnp.float32(0.0))
-                    mu_ref[r + PAD] = (u1 + own) + (a_before + a_back) + side
-                    a_before, c_before, u1, u2, a_now, c_now = a_now, c_now, n1, n2, a_next, c_next
-                return a_before, c_before, u1, u2, a_now, c_now
-
-            _, _, a_before, c_before, _, _ = spread(k, first_block * 8 - 1)
-            u1, u2, a_now, c_now, _, _ = spread(k, first_block * 8)
-            lax.fori_loop(
-                first_block, last_block, block, (a_before, c_before, u1, u2, a_now, c_now)
+    def up(k, mu_ref, next_ref, first, last):
+        gradient_rows(k, mu_ref)
+        level = (k - 1).astype(jnp.float32)
+
+        def spread(r):
+            mu = mu_ref[r + PAD]
+            u2 = row_of(e2_ref, k, r) * mu
+            u3 = row_of(e3_ref, k, r) * mu
+            hm = hm_ref[r + PAD]
+            hp = hp_ref[r + PAD]
+            return row_of(e1_ref, k, r) * mu, u2, hp * u2, hp * u3, hm * u2, hm * u3
+
+        _, _, a_before, c_before, _, _ = spread(first - 1)
+        u1, u2, a_now, c_now, _, _ = spread(first)
+        for r in range(first, last):
+            n1, n2, a_next, c_next, a_back, c_back = spread(r + 1)
+            both = u2 + (c_before + c_back)
+            side = pltpu.roll(gp_ref[r + PAD] * both, 1, 1) + pltpu.roll(
+                gm_ref[r + PAD] * both, LANES - 1, 1
             )
+            hit = row_of(refl_ref, None, r - 16) == level
+            own = jnp.where(hit, wsel_ref[r - 16], jnp.float32(0.0))
+            next_ref[r + PAD] = (u1 + own) + (a_before + a_back) + side
+            a_before, c_before, u1, u2, a_now, c_now = a_now, c_now, n1, n2, a_next, c_next
+
+    def up_two(top, first, last):
+        def two(step, carry):
+            k = top - 2 * step
+            up(k, ma_ref, mb_ref, first, last)
+            up(k - 1, mb_ref, ma_ref, first, last)
             return carry
 
-        return plane
-
-    lax.fori_loop(0, 7, up(2, 8, 15), 0)
-    lax.fori_loop(0, 8, up(3, 7, 8), 0)
-    gradient_rows(0)
-
-    def finish(pair, carry):
+        return two
+
+    lax.fori_loop(0, 2, up_two(15, 17, 63), 0)
+    lax.fori_loop(0, 2, up_two(11, 21, 59), 0)
+    lax.fori_loop(0, 2, up_two(7, 25, 55), 0)
+    up_two(3, 29, 51)(jnp.int32(0), 0)
+    up(jnp.int32(1), ma_ref, mb_ref, 31, 49)
+    gradient_rows(0, mb_ref)
+
+    for pair in range(PLANES // 2):
         parts = []
         for p in range(2):
             k = 2 * pair + p
             shown = jnp.where(
-                k.astype(jnp.float32) <= refl_ref[15:33, :], col_ref[0:18, :], jnp.float32(0.0)
+                float(k) <= refl_ref[15:33, :], col_ref[0:18, :], jnp.float32(0.0)
             )
-            raw_ref[p, 0:18, :] = jnp.where(
+            raw_ref[k, 0:18, :] = jnp.where(
                 earth_ref[k, 7:25, :] < AIR_TEST, grad_ref[k, 0:18, :] + shown, jnp.float32(0.0)
             )
             for h in range(2):
-                mid = raw_ref[p, HALF * h + 1 : HALF * h + 9, :]
-                column = (raw_ref[p, HALF * h : HALF * h + 8, :] + mid) + raw_ref[
-                    p, HALF * h + 2 : HALF * h + 10, :
+                mid = raw_ref[k, HALF * h + 1 : HALF * h + 9, :]
+                column = (raw_ref[k, HALF * h : HALF * h + 8, :] + mid) + raw_ref[
+                    k, HALF * h + 2 : HALF * h + 10, :
                 ]
                 total = column + (pltpu.roll(column, 1, 1) + pltpu.roll(column, LANES - 1, 1))
                 smooth = 0.4375 * mid + 0.0625 * total
                 parts.append(rolled(smooth, STRIP * (2 * p + h - 1)))
-        out_ref[pl.ds(pl.multiple_of(HALF * pair, HALF), HALF), :] = quarters(parts, lane)
-        return carry
-
-    lax.fori_loop(0, PLANES // 2, finish, 0)
+        out_ref[pl.ds(HALF * pair, HALF), :] = quarters(parts, lane)
 
 
 def unpack_kernel(in_ref, out_ref):
@@ -379,6 +357,35 @@
 
 def line(count, shift):
     return [(i, i + shift) for i in range(count) if 0 <= i + shift < count]
+
+
+def sweep_call(pos, shot_cells, left, column, right, nx_total, ny_total):
+    def kernel(*refs):
+        sweep_kernel(*refs, nx_total=nx_total, ny_total=ny_total)
+
+    field = (FULL, SHOTS, LANES)
+    return pl.pallas_call(
+        kernel,
+        out_shape=jax.ShapeDtypeStruct((A_ROWS, LANES), jnp.float32),
+        in_specs=[pl.BlockSpec(memory_space=pltpu.SMEM), *in_vmem(4)],
+        out_specs=in_vmem(1)[0],
+        scratch_shapes=[
+            *[pltpu.VMEM(field, jnp.float32)] * 2,
+            *[pltpu.VMEM((PLANES, FULL, LANES), jnp.float32)] * 3,
+            *[pltpu.VMEM(field, jnp.float32)] * 4,
+            pltpu.VMEM((PLANES, 18, SHOTS, LANES), jnp.float32),
+            *[pltpu.VMEM(field, jnp.float32)] * 2,
+            pltpu.VMEM((48, SHOTS, LANES), jnp.float32),
+            pltpu.VMEM((56, LANES), jnp.float32),
+            pltpu.VMEM((48, SHOTS, LANES), jnp.float32),
+            pltpu.VMEM((PLANES, 32, LANES), jnp.float32),
+            pltpu.VMEM((PLANES, 24, LANES), jnp.float32),
+            pltpu.VMEM((24, LANES), jnp.float32),
+            pltpu.VMEM((PLANES, 24, LANES), jnp.float32),
+        ],
+        compiler_params=pltpu.CompilerParams(vmem_limit_bytes=VMEM_BYTES),
+        name="sweep",
+    )(pos, shot_cells, left, column, right)
 
 
 def local(slowness, air_mask, reflector, shot_cells, receiver_mask, residual):
@@ -423,33 +430,7 @@
     left = lax.ppermute(column, ("depth", "gy"), along(1))
     right = lax.ppermute(column, ("depth", "gy"), along(-1))
 
-    def kernel(*refs):
-        sweep_kernel(*refs, nx_total=nx_total, ny_total=ny_total)
-
-    field = (FULL, SHOTS, LANES)
-    strips_out = pl.pallas_call(
-        kernel,
-        out_shape=jax.ShapeDtypeStruct((A_ROWS, LANES), f32),
-        in_specs=[smem, *in_vmem(4)],
-        out_specs=in_vmem(1)[0],
-        scratch_shapes=[
-            pltpu.VMEM((PLANES + 1, *field), f32),
-            *[pltpu.VMEM((PLANES, FULL, LANES), f32)] * 3,
-            *[pltpu.VMEM(field, f32)] * 4,
-            pltpu.VMEM((PLANES, 32, SHOTS, LANES), f32),
-            pltpu.VMEM(field, f32),
-            pltpu.VMEM((48, SHOTS, LANES), f32),
-            pltpu.VMEM((56, LANES), f32),
-            pltpu.VMEM((48, SHOTS, LANES), f32),
-            pltpu.VMEM((PLANES, 32, LANES), f32),
-            pltpu.VMEM((PLANES, 24, LANES), f32),
-            pltpu.VMEM((24, LANES), f32),
-            pltpu.VMEM((2, 24, LANES), f32),
-        ],
-        compiler_params=pltpu.CompilerParams(vmem_limit_bytes=VMEM_BYTES),
-        name="sweep",
-    )(pos, shot_cells, left, column, right)
-
+    strips_out = sweep_call(pos, shot_cells, left, column, right, nx_total, ny_total)
     parts = lax.all_to_all(
         strips_out.reshape(8, HALF, LANES), "depth", 0, 0, tiled=True
     ).reshape(A_ROWS, LANES)

time: 79 us -> 61.9 us (0.78)
  Pallas kernels: 28.6 us -> 11.5 us
    pallas_call x1, Pallas kernels: 25.2 us -> 8.11 us  [sweep_call(): pl.pallas_call(kernel, out_shape=jax.ShapeDtypeStruct((A_ROWS, LANES), jn...]
where the time goes in v2:
time: 61.9 us; the launch traced here: 61.4 us
  blocking collectives  18.5 us (30%)
  starting transfers between devices  18.3 us (30%)
  waiting for transfers between devices  12.2 us (20%)
  Pallas kernels  11.5 us (19%)
  other arithmetic  0.66 us (1%)
    all_to_all x1, blocking collectives, local(): lax.all_to_all(packed.reshape(8, HALF, LANES), 'depth', 0, 0, tiled=True)  10 us
    all_to_all x1, blocking collectives, local(): lax.all_to_all(strips_out.reshape(8, HALF, LANES), 'depth', 0, 0, tiled=T...  8.49 us
    pallas_call x1, Pallas kernels, sweep_call(): pl.pallas_call(kernel, out_shape=jax.ShapeDtypeStruct((A_ROWS, LANES), jn...  8.11 us
    ppermute x1, waiting for transfers between devices, local(): left = lax.ppermute(column, ('depth', 'gy'), along(1))  5.93 us
    ppermute x1, starting transfers between devices, local(): below1 = lax.ppermute(whole, 'gx', line(x_count, -1))  5.34 us
    ppermute x1, waiting for transfers between devices, local(): above1 = lax.ppermute(whole, 'gx', line(x_count, 1))  5.29 us
    ppermute x1, starting transfers between devices, local(): below2 = lax.ppermute(strip, 'gx', line(x_count, -2))  4.56 us
    ppermute x1, starting transfers between devices, local(): left = lax.ppermute(column, ('depth', 'gy'), along(1))  2.41 us
  transfers between devices with their start and end apart: 6, of which 3 were waited for; matrix products, arithmetic and copies ran while one was open for 0% of the time, Pallas kernels for 0%

profile of v2, /device:TPU:388, one launch (start us, length us, event | category | flops | bytes accessed | tf_op | source)
XLA Modules:
  0.0 61.4 jit_solution(2042825926859356353)
XLA Ops:
  0.0 0.7 %pad_add_fusion.pos.refs_0_ = s32[3]{0:T(128)} fusion(s32[1]{0:T(128)} %bitcast.2, s32[1]{0:T(128)} %bitcast.1, s32[1]{0:T(128)} %bitcast), kind=kLoop, calls=%fused_computation.7 | loop fusion | flops 6 | bytes 24 | tf_op jit(solution)/shard_map/stack | solution.py:397
  0.7 1.9 %pack.1 = (f32[64,128]{1,0:T(8,128)}, f32[40,128]{1,0:T(8,128)}) custom-call(s32[3]{0:T(128)} %pad_add_fusion.pos.refs_0_, f32[2,16,256]{2,1,0:T(8,128)} %slow_ref.1, s32[2,16,256]{2,1,0:T(8,128)} %air_ref.1, s32[16,256]{1,0:T(8,128)} %refl_ref.1, s32[8,16,256]{2,1,0:T(8,128)} %mask_ref.1, f32[8,16,256]{2,1,0:T(8,128)} %resid_ref.1), custom_call_target="tpu_custom_call" | custom-call | tf_op jit(solution)/shard_map/pack/pallas_call | solution.py:403
  2.5 0.0 copy-start.1
  2.5 10.0 %all_to_all.10 = f32[8,8,128]{2,1,0:T(8,128)S(1)} all-to-all(f32[8,8,128]{2,1,0:T(8,128)} %bitcast.13), channel_id=1, replica_groups=mesh['depth'=8,'gx'=16,'gy'=4] {'depth'}, dimensions={0} | all-to-all | bytes 65536 | tf_op jit(solution)/shard_map/all_to_all | solution.py:414
  12.6 4.6 %collective-permute-start.3 = (f32[64,128]{1,0:T(8,128)S(1)}, f32[64,128]{1,0:T(8,128)S(1)}, u32[]{:S(2)}, u32[]{:S(2)}) collective-permute-start(f32[64,128]{1,0:T(8,128)S(1)} %bitcast.9), channel_id=1, source_target_pairs={{8,0},{12,4},{16,8},{20,12},{24,16},{28,20},{32,24},{36,28},{40,32... | collective-permute-start | bytes 98312 | tf_op jit(solution)/shard_map/ppermute | solution.py:421
  17.1 2.2 %collective-permute-start = (f32[64,128]{1,0:T(8,128)S(1)}, f32[64,128]{1,0:T(8,128)S(1)}, u32[]{:S(2)}, u32[]{:S(2)}) collective-permute-start(f32[64,128]{1,0:T(8,128)S(1)} %bitcast.10), channel_id=1, source_target_pairs={{0,8},{4,12},{8,16},{12,20},{16,24},{20,28},{24,32},{28,36},{32,40... | collective-permute-start | bytes 98312 | tf_op jit(solution)/shard_map/ppermute | solution.py:420
  19.3 0.0 copy-done.1
  19.4 5.3 %collective-permute-start.2 = (f32[104,128]{1,0:T(8,128)S(1)}, f32[104,128]{1,0:T(8,128)S(1)}, u32[]{:S(2)}, u32[]{:S(2)}) collective-permute-start(f32[104,128]{1,0:T(8,128)S(1)} %pad_maximum_fusion), channel_id=1, source_target_pairs={{4,0},{8,4},{12,8},{16,12},{20,16},{24,20},{28,24},{32,28},{36,32}... | collective-permute-start | bytes 159752 | tf_op jit(solution)/shard_map/ppermute | solution.py:419
  24.7 1.9 %collective-permute-start.1 = (f32[104,128]{1,0:T(8,128)S(1)}, f32[104,128]{1,0:T(8,128)S(1)}, u32[]{:S(2)}, u32[]{:S(2)}) collective-permute-start(f32[104,128]{1,0:T(8,128)S(1)} %pad_maximum_fusion), channel_id=1, source_target_pairs={{0,4},{4,8},{8,12},{12,16},{16,20},{20,24},{24,28},{28,32},{32,36}... | collective-permute-start | bytes 159752 | tf_op jit(solution)/shard_map/ppermute | solution.py:418
  26.6 0.0 collective-permute-done
  26.6 5.3 %collective-permute-done.1 = f32[104,128]{1,0:T(8,128)S(1)} collective-permute-done((f32[104,128]{1,0:T(8,128)S(1)}, f32[104,128]{1,0:T(8,128)S(1)}, u32[]{:S(2)}, u32[]{:S(2)}) %collective-permute-start.1) | collective-permute-done | bytes 53280 | tf_op jit(solution)/shard_map/ppermute | solution.py:418
  32.0 0.0 collective-permute-done.2
  32.0 0.0 copy-start.2
  32.0 0.0 collective-permute-done.3
  32.0 0.0 copy-start
  32.0 1.9 %collective-permute-start.5 = (f32[440,128]{1,0:T(8,128)S(1)}, f32[440,128]{1,0:T(8,128)S(1)}, u32[]{:S(2)}, u32[]{:S(2)}) collective-permute-start(f32[440,128]{1,0:T(8,128)S(1)} %constant_dynamic-update-slice_fusion.refs_3_), channel_id=1, source_target_pairs={{64,0},{128,64},{192,128},{256,192},{320,256},{384,320},{448,384},... | collective-permute-start | bytes 675848 | tf_op jit(solution)/shard_map/ppermute | solution.py:431
  34.0 2.4 %collective-permute-start.4 = (f32[440,128]{1,0:T(8,128)S(1)}, f32[440,128]{1,0:T(8,128)S(1)}, u32[]{:S(2)}, u32[]{:S(2)}) collective-permute-start(f32[440,128]{1,0:T(8,128)S(1)} %constant_dynamic-update-slice_fusion.refs_3_), channel_id=1, source_target_pairs={{0,64},{64,128},{128,192},{192,256},{256,320},{320,384},{384,448},... | collective-permute-start | bytes 675848 | tf_op jit(solution)/shard_map/ppermute | solution.py:430
  36.4 0.0 copy-done.2
  36.4 0.1 copy.7.refs_1_
  36.5 1.0 %collective-permute-done.5.refs_4_ = f32[440,128]{1,0:T(8,128)S(1)} collective-permute-done((f32[440,128]{1,0:T(8,128)S(1)}, f32[440,128]{1,0:T(8,128)S(1)}, u32[]{:S(2)}, u32[]{:S(2)}) %collective-permute-start.5) | collective-permute-done | bytes 225312 | tf_op jit(solution)/shard_map/ppermute | solution.py:431
  37.4 5.9 %collective-permute-done.4.refs_2_ = f32[440,128]{1,0:T(8,128)S(1)} collective-permute-done((f32[440,128]{1,0:T(8,128)S(1)}, f32[440,128]{1,0:T(8,128)S(1)}, u32[]{:S(2)}, u32[]{:S(2)}) %collective-permute-start.4) | collective-permute-done | bytes 225312 | tf_op jit(solution)/shard_map/ppermute | solution.py:430
  43.4 0.0 copy-done
  43.4 8.1 %sweep.1 = f32[64,128]{1,0:T(8,128)S(1)} custom-call(s32[3]{0:T(128)S(1)} %copy-done, s32[8,2]{1,0:T(8,128)S(1)} %copy.7.refs_1_, f32[440,128]{1,0:T(8,128)S(1)} %collective-permute-done.4.refs_2_, f32[440,128]{1,0:T(8,128)S(1)} %constant_dynamic-update-slice_fusion.refs_3_, f32[440,128]{1,0:T(8,128)S(1)} %collective-permute-done.5.refs_4_), custom_call_target="tpu_custom_call" | custom-call | tf_op jit(solution)/shard_map/sweep/pallas_call | solution.py:367
  51.5 8.5 %all_to_all.11 = f32[8,8,128]{2,1,0:T(8,128)} all-to-all(f32[8,8,128]{2,1,0:T(8,128)S(1)} %bitcast.8), channel_id=1, replica_groups=mesh['depth'=8,'gx'=16,'gy'=4] {'depth'}, dimensions={0} | all-to-all | bytes 65536 | tf_op jit(solution)/shard_map/all_to_all | solution.py:434
  60.0 1.5 %unpack.1 = f32[2,16,256]{2,1,0:T(8,128)} custom-call(f32[64,128]{1,0:T(8,128)} %bitcast.12), custom_call_target="tpu_custom_call" | custom-call | tf_op jit(solution)/shard_map/unpack/pallas_call | solution.py:437
  (7 shorter events, 0.0 us)
Async XLA Ops:
  2.5 16.8 %copy-start.1 = (f32[40,128]{1,0:T(8,128)S(1)}, f32[40,128]{1,0:T(8,128)}, u32[]{:S(2)}) copy-start(f32[40,128]{1,0:T(8,128)} %get-tuple-element.8) | copy-start | bytes 61444
  12.6 19.4 %collective-permute-start.3 = (f32[64,128]{1,0:T(8,128)S(1)}, f32[64,128]{1,0:T(8,128)S(1)}, u32[]{:S(2)}, u32[]{:S(2)}) collective-permute-start(f32[64,128]{1,0:T(8,128)S(1)} %bitcast.9), channel_id=1, source_target_pairs={{8,0},{12,4},{16,8},{20,12},{24,16},{28,20},{32,24},{36,28},{40,32... | collective-permute-start | bytes 98312 | tf_op jit(solution)/shard_map/ppermute | solution.py:421
  17.1 9.5 %collective-permute-start = (f32[64,128]{1,0:T(8,128)S(1)}, f32[64,128]{1,0:T(8,128)S(1)}, u32[]{:S(2)}, u32[]{:S(2)}) collective-permute-start(f32[64,128]{1,0:T(8,128)S(1)} %bitcast.10), channel_id=1, source_target_pairs={{0,8},{4,12},{8,16},{12,20},{16,24},{20,28},{24,32},{28,36},{32,40... | collective-permute-start | bytes 98312 | tf_op jit(solution)/shard_map/ppermute | solution.py:420
  19.4 12.6 %collective-permute-start.2 = (f32[104,128]{1,0:T(8,128)S(1)}, f32[104,128]{1,0:T(8,128)S(1)}, u32[]{:S(2)}, u32[]{:S(2)}) collective-permute-start(f32[104,128]{1,0:T(8,128)S(1)} %pad_maximum_fusion), channel_id=1, source_target_pairs={{4,0},{8,4},{12,8},{16,12},{20,16},{24,20},{28,24},{32,28},{36,32}... | collective-permute-start | bytes 159752 | tf_op jit(solution)/shard_map/ppermute | solution.py:419
  24.7 7.2 %collective-permute-start.1 = (f32[104,128]{1,0:T(8,128)S(1)}, f32[104,128]{1,0:T(8,128)S(1)}, u32[]{:S(2)}, u32[]{:S(2)}) collective-permute-start(f32[104,128]{1,0:T(8,128)S(1)} %pad_maximum_fusion), channel_id=1, source_target_pairs={{0,4},{4,8},{8,12},{12,16},{16,20},{20,24},{24,28},{28,32},{32,36}... | collective-permute-start | bytes 159752 | tf_op jit(solution)/shard_map/ppermute | solution.py:418
  32.0 4.4 %copy-start.2 = (s32[8,2]{0,1:T(2,128)S(1)}, s32[8,2]{0,1:T(2,128)}, u32[]{:S(2)}) copy-start(s32[8,2]{0,1:T(2,128)} %param.9) | copy-start | bytes 196
  32.0 11.3 %copy-start = (s32[3]{0:T(128)S(1)}, s32[3]{0:T(128)}, u32[]{:S(2)}) copy-start(s32[3]{0:T(128)} %pad_add_fusion.pos.refs_0_) | copy-start | bytes 40
  32.0 5.4 %collective-permute-start.5 = (f32[440,128]{1,0:T(8,128)S(1)}, f32[440,128]{1,0:T(8,128)S(1)}, u32[]{:S(2)}, u32[]{:S(2)}) collective-permute-start(f32[440,128]{1,0:T(8,128)S(1)} %constant_dynamic-update-slice_fusion.refs_3_), channel_id=1, source_target_pairs={{64,0},{128,64},{192,128},{256,192},{320,256},{384,320},{448,384},... | collective-permute-start | bytes 675848 | tf_op jit(solution)/shard_map/ppermute | solution.py:431
  34.0 9.4 %collective-permute-start.4 = (f32[440,128]{1,0:T(8,128)S(1)}, f32[440,128]{1,0:T(8,128)S(1)}, u32[]{:S(2)}, u32[]{:S(2)}) collective-permute-start(f32[440,128]{1,0:T(8,128)S(1)} %constant_dynamic-update-slice_fusion.refs_3_), channel_id=1, source_target_pairs={{0,64},{64,128},{128,192},{192,256},{256,320},{320,384},{384,448},... | collective-permute-start | bytes 675848 | tf_op jit(solution)/shard_map/ppermute | solution.py:430

commit v3 on v2

--- a/solution.py
+++ b/solution.py
@@ -28,9 +28,13 @@
 S_ROWS = 40
 A_AT = (0, A_ROWS, 2 * A_ROWS + S_ROWS, 3 * A_ROWS + 2 * S_ROWS, 4 * A_ROWS + 3 * S_ROWS)
 S_AT = (2 * A_ROWS, 3 * A_ROWS + S_ROWS, 4 * A_ROWS + 2 * S_ROWS)
-GEOMETRY = 40
+MIDDLE = 40
 HALF = 8
 VMEM_BYTES = 40 * 1024 * 1024
+
+
+def position(axis):
+    return lax.axis_index(axis)
 
 
 def rolled(value, shift):
@@ -49,7 +53,7 @@
     return out
 
 
-def pack_kernel(pos, slow_ref, air_ref, refl_ref, mask_ref, resid_ref, a_ref, s_ref):
+def pack_kernel(slow_ref, air_ref, refl_ref, mask_ref, resid_ref, a_ref, s_ref):
     lane = lane_index()
     speed = {}
     for p in range(2):
@@ -61,7 +65,7 @@
         c, q = divmod(target, 4)
         parts = [rolled(speed[j // 2, j % 2, c], STRIP * (j - q)) for j in range(4)]
         a_ref[pl.ds(HALF * target, HALF), :] = quarters(parts, lane)
-    depth_pos = pos[0]
+    depth_pos = position("depth")
     high = depth_pos >= 4
     back = (LANES - STRIP * (depth_pos % 4)) % LANES
 
@@ -93,21 +97,16 @@
 
 
 def sweep_kernel(
-    pos,
     shot_ref,
-    left_ref,
+    near_ref,
     here_ref,
-    right_ref,
+    far_ref,
     out_ref,
     wa_ref,
     wb_ref,
     e1_ref,
     e2_ref,
     e3_ref,
-    gm_ref,
-    gp_ref,
-    hm_ref,
-    hp_ref,
     head_ref,
     ma_ref,
     mb_ref,
@@ -123,8 +122,10 @@
 ):
     lane = lane_index()
     sub = lax.broadcasted_iota(jnp.int32, (8, LANES), 0)
-    x_base = pos[1] * ROWS - 2 * ROWS
-    y_base = pos[2] * (8 * STRIP) + pos[0] * STRIP - STRIP
+    depth_pos = position("depth")
+    x_base = position("gx") * ROWS - 2 * ROWS
+    y_base = position("gy") * (8 * STRIP) + depth_pos * STRIP - STRIP
+    odd = depth_pos % 2 == 1
     y_cell = y_base + lane
     y_inside = (y_cell >= 0) & (y_cell < ny_total)
     zero = jnp.zeros((8, LANES), jnp.float32)
@@ -153,23 +154,11 @@
     def near(diff):
         return jnp.clip(diff, -1.0, 1.0)
 
-    def geometry(block, carry):
-        before, now = carry
-        for i in range(GEOMETRY):
-            r = block * GEOMETRY + i
-            after = surface(r + 1)
-            gm_ref[r + PAD] = weight(near(pltpu.roll(now, 1, 1) - now))
-            gp_ref[r + PAD] = weight(near(pltpu.roll(now, LANES - 1, 1) - now))
-            hm_ref[r + PAD] = weight(before - now)
-            hp_ref[r + PAD] = weight(after - now)
-            wa_ref[r + PAD] = rim_factor(x_base + r)
-            before, now = now, after
-        return before, now
-
-    lax.fori_loop(0, FRAME // GEOMETRY, geometry, (surface(-1), surface(0)))
-    for ref in (gm_ref, gp_ref, hm_ref, hp_ref):
-        ref[PAD - 1] = zero
-        ref[PAD + FRAME] = zero
+    middle = surface(MIDDLE)
+    weight_minus = weight(near(pltpu.roll(middle, 1, 1) - middle))
+    weight_plus = weight(near(pltpu.roll(middle, LANES - 1, 1) - middle))
+    for r in range(FRAME):
+        wa_ref[r + PAD] = weight(surface(r) - middle) * rim_factor(x_base + r)
     for ref in (wa_ref, wb_ref):
         ref[PAD - 1] = zero
         ref[PAD + FRAME] = zero
@@ -183,16 +172,21 @@
 
     def strips(row):
         at = (pl.ds(row, HALF), slice(None))
-        return left_ref[at], rolled(here_ref[at], STRIP), rolled(right_ref[at], 2 * STRIP)
+        one, two = near_ref[at], far_ref[at]
+        left = jnp.where(odd, one, two)
+        right = jnp.where(odd, two, one)
+        return left, rolled(here_ref[at], STRIP), rolled(right, 2 * STRIP)
 
     rims = [rim_factor(x_base + HALF * g + sub) for g in range(FRAME // HALF)]
 
-    def exponents(pair, carry):
+    for pair in range(PLANES // 2):
         for offset in range(5):
-            tiles = strips(pl.multiple_of(A_AT[offset] + HALF * pair, HALF))
+            tiles = strips(A_AT[offset] + HALF * pair)
             for j in range(4):
                 p, h = divmod(j, 2)
                 group = 2 * offset + h
+                if pair >= 4 and group in (0, 9):
+                    continue
                 speed = merged(tiles, j)
                 at = (2 * pair + p, pl.ds(HALF * group, HALF), slice(None))
                 e1_ref[at] = jnp.exp(-speed * RATE) * rims[group]
@@ -201,9 +195,6 @@
                 if 3 <= group < 7:
                     here = (2 * pair + p, pl.ds(HALF * (group - 3), HALF), slice(None))
                     earth_ref[here] = speed
-        return carry
-
-    lax.fori_loop(0, PLANES // 2, exponents, 0)
 
     for offset in range(3):
         for v in range(4):
@@ -220,26 +211,21 @@
     for r in range(48):
         wsel_ref[r] = zero + 1.0
 
-    def along_y(value, r):
-        return (
-            gm_ref[r + PAD] * pltpu.roll(value, 1, 1)
-            + gp_ref[r + PAD] * pltpu.roll(value, LANES - 1, 1)
+    def along_y(value):
+        return weight_minus * pltpu.roll(value, 1, 1) + weight_plus * pltpu.roll(
+            value, LANES - 1, 1
         )
 
     def down_plane(k, w_ref, next_ref, first, last, select):
         level = k.astype(jnp.float32)
         w_before, w_now = w_ref[first - 1 + PAD], w_ref[first + PAD]
-        q_before, q_now = along_y(w_before, first - 1), along_y(w_now, first)
+        q_before, q_now = along_y(w_before), along_y(w_now)
         for r in range(first, last):
             w_after = w_ref[r + 1 + PAD]
-            q_after = along_y(w_after, r + 1)
-            hm = hm_ref[r + PAD]
-            hp = hp_ref[r + PAD]
-            edge = q_now + (hm * w_before + hp * w_after)
-            corner = hm * q_before + hp * q_after
+            q_after = along_y(w_after)
             part1 = row_of(e1_ref, k, r) * w_now
-            part2 = row_of(e2_ref, k, r) * edge
-            part3 = row_of(e3_ref, k, r) * corner
+            part2 = row_of(e2_ref, k, r) * (q_now + (w_before + w_after))
+            part3 = row_of(e3_ref, k, r) * (q_before + q_after)
             w_next = part1 + part2 + part3
             next_ref[r + PAD] = w_next
             if 31 <= r < 49:
@@ -259,7 +245,8 @@
 
     lax.fori_loop(0, 2, down(1, 79, False), 0)
     lax.fori_loop(2, 4, down(5, 75, True), 0)
-    lax.fori_loop(4, 8, down(9, 71, True), 0)
+    lax.fori_loop(4, 6, down(9, 71, True), 0)
+    lax.fori_loop(6, 8, down(13, 67, True), 0)
 
     for ref in (ma_ref, mb_ref):
         ref[15 + PAD] = zero
@@ -284,24 +271,20 @@
 
         def spread(r):
             mu = mu_ref[r + PAD]
-            u2 = row_of(e2_ref, k, r) * mu
-            u3 = row_of(e3_ref, k, r) * mu
-            hm = hm_ref[r + PAD]
-            hp = hp_ref[r + PAD]
-            return row_of(e1_ref, k, r) * mu, u2, hp * u2, hp * u3, hm * u2, hm * u3
-
-        _, _, a_before, c_before, _, _ = spread(first - 1)
-        u1, u2, a_now, c_now, _, _ = spread(first)
+            return row_of(e1_ref, k, r) * mu, row_of(e2_ref, k, r) * mu, row_of(e3_ref, k, r) * mu
+
+        _, u2_before, u3_before = spread(first - 1)
+        u1, u2, u3 = spread(first)
         for r in range(first, last):
-            n1, n2, a_next, c_next, a_back, c_back = spread(r + 1)
-            both = u2 + (c_before + c_back)
-            side = pltpu.roll(gp_ref[r + PAD] * both, 1, 1) + pltpu.roll(
-                gm_ref[r + PAD] * both, LANES - 1, 1
+            n1, n2, n3 = spread(r + 1)
+            both = u2 + (u3_before + n3)
+            side = pltpu.roll(weight_plus * both, 1, 1) + pltpu.roll(
+                weight_minus * both, LANES - 1, 1
             )
             hit = row_of(refl_ref, None, r - 16) == level
             own = jnp.where(hit, wsel_ref[r - 16], jnp.float32(0.0))
-            next_ref[r + PAD] = (u1 + own) + (a_before + a_back) + side
-            a_before, c_before, u1, u2, a_now, c_now = a_now, c_now, n1, n2, a_next, c_next
+            next_ref[r + PAD] = (u1 + own) + (u2_before + n2) + side
+            u2_before, u3_before, u1, u2, u3 = u2, u3, n1, n2, n3
 
     def up_two(top, first, last):
         def two(step, carry):
@@ -359,7 +342,7 @@
     return [(i, i + shift) for i in range(count) if 0 <= i + shift < count]
 
 
-def sweep_call(pos, shot_cells, left, column, right, nx_total, ny_total):
+def sweep_call(shot_cells, near, column, far, nx_total, ny_total):
     def kernel(*refs):
         sweep_kernel(*refs, nx_total=nx_total, ny_total=ny_total)
 
@@ -367,12 +350,11 @@
     return pl.pallas_call(
         kernel,
         out_shape=jax.ShapeDtypeStruct((A_ROWS, LANES), jnp.float32),
-        in_specs=[pl.BlockSpec(memory_space=pltpu.SMEM), *in_vmem(4)],
+        in_specs=in_vmem(4),
         out_specs=in_vmem(1)[0],
         scratch_shapes=[
             *[pltpu.VMEM(field, jnp.float32)] * 2,
             *[pltpu.VMEM((PLANES, FULL, LANES), jnp.float32)] * 3,
-            *[pltpu.VMEM(field, jnp.float32)] * 4,
             pltpu.VMEM((PLANES, 18, SHOTS, LANES), jnp.float32),
             *[pltpu.VMEM(field, jnp.float32)] * 2,
             pltpu.VMEM((48, SHOTS, LANES), jnp.float32),
@@ -385,7 +367,7 @@
         ],
         compiler_params=pltpu.CompilerParams(vmem_limit_bytes=VMEM_BYTES),
         name="sweep",
-    )(pos, shot_cells, left, column, right)
+    )(shot_cells, near, column, far)
 
 
 def local(slowness, air_mask, reflector, shot_cells, receiver_mask, residual):
@@ -394,10 +376,6 @@
     y_count = lax.axis_size("gy")
     nx_total = ROWS * x_count
     ny_total = STRIP * depth_count * y_count
-    pos = jnp.stack(
-        [lax.axis_index("depth"), lax.axis_index("gx"), lax.axis_index("gy")]
-    ).astype(jnp.int32)
-    smem = pl.BlockSpec(memory_space=pltpu.SMEM)
     f32 = jnp.float32
 
     packed, sources = pl.pallas_call(
@@ -406,10 +384,10 @@
             jax.ShapeDtypeStruct((A_ROWS, LANES), f32),
             jax.ShapeDtypeStruct((S_ROWS, LANES), f32),
         ),
-        in_specs=[smem, *in_vmem(5)],
+        in_specs=in_vmem(5),
         out_specs=tuple(in_vmem(2)),
         name="pack",
-    )(pos, slowness, air_mask, reflector, receiver_mask, residual)
+    )(slowness, air_mask, reflector, receiver_mask, residual)
 
     strip = lax.all_to_all(
         packed.reshape(8, HALF, LANES), "depth", 0, 0, tiled=True
@@ -424,13 +402,14 @@
     def place(q):
         return (q % depth_count) * y_count + q // depth_count
 
-    def along(shift):
-        return [(place(i), place(j)) for i, j in line(depth_count * y_count, shift)]
-
-    left = lax.ppermute(column, ("depth", "gy"), along(1))
-    right = lax.ppermute(column, ("depth", "gy"), along(-1))
-
-    strips_out = sweep_call(pos, shot_cells, left, column, right, nx_total, ny_total)
+    def swapped(first):
+        pairs = [(q, q + 1) for q in range(first, depth_count * y_count - 1, 2)]
+        return [(place(i), place(j)) for a, b in pairs for i, j in ((a, b), (b, a))]
+
+    near = lax.ppermute(column, ("depth", "gy"), swapped(0))
+    far = lax.ppermute(column, ("depth", "gy"), swapped(1))
+
+    strips_out = sweep_call(shot_cells, near, column, far, nx_total, ny_total)
     parts = lax.all_to_all(
         strips_out.reshape(8, HALF, LANES), "depth", 0, 0, tiled=True
     ).reshape(A_ROWS, LANES)

time: 61.9 us -> 58.5 us (0.945)
  waiting for transfers between devices: 12.2 us -> 10.1 us
  Pallas kernels: 11.5 us -> 10.7 us
  other arithmetic: 0.66 us -> 0.01 us
    ppermute x2, waiting for transfers between devices: 6.9 us -> 4.8 us  [the longest x1 4.8 us: local(): far = lax.ppermute(column, ('depth', 'gy'), swapped(1))]
    pallas_call x1, Pallas kernels: 8.11 us -> 7.34 us  [sweep_call(): pl.pallas_call(kernel, out_shape=jax.ShapeDtypeStruct((A_ROWS, LANES), jn...]
    another operation x1 -> x0, other arithmetic: 0.65 us -> none  [local(): jnp.stack([lax.axis_index('depth'), lax.axis_index('gx'), lax.axis_index(...]
  transfers between devices with their start and end apart: 6 -> 6, of which waited for: 3 -> 2; matrix products, arithmetic and copies ran while one was open for 0% -> 0% of each run, Pallas kernels for 0% -> 0%
where the time goes in v3:
time: 58.5 us; the launch traced here: 58.1 us
  blocking collectives  18.5 us (32%)
  starting transfers between devices  18.5 us (32%)
  Pallas kernels  10.7 us (18%)
  waiting for transfers between devices  10.1 us (17%)
    all_to_all x1, blocking collectives, local(): lax.all_to_all(packed.reshape(8, HALF, LANES), 'depth', 0, 0, tiled=True)  10 us
    all_to_all x1, blocking collectives, local(): lax.all_to_all(strips_out.reshape(8, HALF, LANES), 'depth', 0, 0, tiled=T...  8.5 us
    pallas_call x1, Pallas kernels, sweep_call(): pl.pallas_call(kernel, out_shape=jax.ShapeDtypeStruct((A_ROWS, LANES), jn...  7.34 us
    ppermute x1, starting transfers between devices, local(): below1 = lax.ppermute(whole, 'gx', line(x_count, -1))  5.34 us
    ppermute x1, waiting for transfers between devices, local(): above1 = lax.ppermute(whole, 'gx', line(x_count, 1))  5.29 us
    ppermute x1, waiting for transfers between devices, local(): far = lax.ppermute(column, ('depth', 'gy'), swapped(1))  4.8 us
    ppermute x1, starting transfers between devices, local(): below2 = lax.ppermute(strip, 'gx', line(x_count, -2))  4.56 us
    ppermute x1, starting transfers between devices, local(): near = lax.ppermute(column, ('depth', 'gy'), swapped(0))  2.58 us
  transfers between devices with their start and end apart: 6, of which 2 were waited for; matrix products, arithmetic and copies ran while one was open for 0% of the time, Pallas kernels for 0%

profile of v3, /device:TPU:388, one launch (start us, length us, event | category | flops | bytes accessed | tf_op | source)
XLA Modules:
  0.0 58.1 jit_solution(3393466430939954612)
XLA Ops:
  0.0 1.9 %pack.1 = (f32[64,128]{1,0:T(8,128)}, f32[40,128]{1,0:T(8,128)}) custom-call(f32[2,16,256]{2,1,0:T(8,128)} %slow_ref.1, s32[2,16,256]{2,1,0:T(8,128)} %air_ref.1, s32[16,256]{1,0:T(8,128)} %refl_ref.1, s32[8,16,256]{2,1,0:T(8,128)} %mask_ref.1, f32[8,16,256]{2,1,0:T(8,128)} %resid_ref.1), custom_call_target="tpu_custom_call" | custom-call | tf_op jit(solution)/shard_map/pack/pallas_call | solution.py:381
  1.9 0.0 copy-start
  1.9 10.0 %all_to_all.10 = f32[8,8,128]{2,1,0:T(8,128)S(1)} all-to-all(f32[8,8,128]{2,1,0:T(8,128)} %bitcast.10), channel_id=1, replica_groups=mesh['depth'=8,'gx'=16,'gy'=4] {'depth'}, dimensions={0} | all-to-all | bytes 65536 | tf_op jit(solution)/shard_map/all_to_all | solution.py:392
  11.9 4.6 %collective-permute-start.3 = (f32[64,128]{1,0:T(8,128)S(1)}, f32[64,128]{1,0:T(8,128)S(1)}, u32[]{:S(2)}, u32[]{:S(2)}) collective-permute-start(f32[64,128]{1,0:T(8,128)S(1)} %bitcast.6), channel_id=1, source_target_pairs={{8,0},{12,4},{16,8},{20,12},{24,16},{28,20},{32,24},{36,28},{40,32... | collective-permute-start | bytes 98312 | tf_op jit(solution)/shard_map/ppermute | solution.py:399
  16.5 2.2 %collective-permute-start = (f32[64,128]{1,0:T(8,128)S(1)}, f32[64,128]{1,0:T(8,128)S(1)}, u32[]{:S(2)}, u32[]{:S(2)}) collective-permute-start(f32[64,128]{1,0:T(8,128)S(1)} %bitcast.7), channel_id=1, source_target_pairs={{0,8},{4,12},{8,16},{12,20},{16,24},{20,28},{24,32},{28,36},{32,40... | collective-permute-start | bytes 98312 | tf_op jit(solution)/shard_map/ppermute | solution.py:398
  18.7 0.0 copy-done
  18.7 5.3 %collective-permute-start.2 = (f32[104,128]{1,0:T(8,128)S(1)}, f32[104,128]{1,0:T(8,128)S(1)}, u32[]{:S(2)}, u32[]{:S(2)}) collective-permute-start(f32[104,128]{1,0:T(8,128)S(1)} %pad_maximum_fusion), channel_id=1, source_target_pairs={{4,0},{8,4},{12,8},{16,12},{20,16},{24,20},{28,24},{32,28},{36,32}... | collective-permute-start | bytes 159752 | tf_op jit(solution)/shard_map/ppermute | solution.py:397
  24.0 1.9 %collective-permute-start.1 = (f32[104,128]{1,0:T(8,128)S(1)}, f32[104,128]{1,0:T(8,128)S(1)}, u32[]{:S(2)}, u32[]{:S(2)}) collective-permute-start(f32[104,128]{1,0:T(8,128)S(1)} %pad_maximum_fusion), channel_id=1, source_target_pairs={{0,4},{4,8},{8,12},{12,16},{16,20},{20,24},{24,28},{28,32},{32,36}... | collective-permute-start | bytes 159752 | tf_op jit(solution)/shard_map/ppermute | solution.py:396
  26.0 0.0 collective-permute-done
  26.0 5.3 %collective-permute-done.1 = f32[104,128]{1,0:T(8,128)S(1)} collective-permute-done((f32[104,128]{1,0:T(8,128)S(1)}, f32[104,128]{1,0:T(8,128)S(1)}, u32[]{:S(2)}, u32[]{:S(2)}) %collective-permute-start.1) | collective-permute-done | bytes 53280 | tf_op jit(solution)/shard_map/ppermute | solution.py:396
  31.3 0.0 collective-permute-done.2
  31.3 0.0 copy-start.1
  31.3 0.0 collective-permute-done.3
  31.4 1.9 %collective-permute-start.5 = (f32[440,128]{1,0:T(8,128)S(1)}, f32[440,128]{1,0:T(8,128)S(1)}, u32[]{:S(2)}, u32[]{:S(2)}) collective-permute-start(f32[440,128]{1,0:T(8,128)S(1)} %constant_dynamic-update-slice_fusion.refs_2_), channel_id=1, source_target_pairs={{64,128},{128,64},{192,256},{256,192},{320,384},{384,320},{448,1},... | collective-permute-start | bytes 675848 | tf_op jit(solution)/shard_map/ppermute | solution.py:410
  33.3 2.6 %collective-permute-start.4 = (f32[440,128]{1,0:T(8,128)S(1)}, f32[440,128]{1,0:T(8,128)S(1)}, u32[]{:S(2)}, u32[]{:S(2)}) collective-permute-start(f32[440,128]{1,0:T(8,128)S(1)} %constant_dynamic-update-slice_fusion.refs_2_), channel_id=1, source_target_pairs={{0,64},{64,0},{128,192},{192,128},{256,320},{320,256},{384,448},{4... | collective-permute-start | bytes 675848 | tf_op jit(solution)/shard_map/ppermute | solution.py:409
  35.9 0.0 copy-done.1
  35.9 0.1 copy.7.refs_0_
  36.0 4.8 %collective-permute-done.5.refs_3_ = f32[440,128]{1,0:T(8,128)S(1)} collective-permute-done((f32[440,128]{1,0:T(8,128)S(1)}, f32[440,128]{1,0:T(8,128)S(1)}, u32[]{:S(2)}, u32[]{:S(2)}) %collective-permute-start.5) | collective-permute-done | bytes 225312 | tf_op jit(solution)/shard_map/ppermute | solution.py:410
  40.8 0.0 collective-permute-done.4.refs_1_
  40.8 7.3 %sweep.1 = f32[64,128]{1,0:T(8,128)S(1)} custom-call(s32[8,2]{1,0:T(8,128)S(1)} %copy.7.refs_0_, f32[440,128]{1,0:T(8,128)S(1)} %collective-permute-done.4.refs_1_, f32[440,128]{1,0:T(8,128)S(1)} %constant_dynamic-update-slice_fusion.refs_2_, f32[440,128]{1,0:T(8,128)S(1)} %collective-permute-done.5.refs_3_), custom_call_target="tpu_custom_call" | custom-call | tf_op jit(solution)/shard_map/sweep/pallas_call | solution.py:350
  48.1 8.5 %all_to_all.11 = f32[8,8,128]{2,1,0:T(8,128)} all-to-all(f32[8,8,128]{2,1,0:T(8,128)S(1)} %bitcast.5), channel_id=1, replica_groups=mesh['depth'=8,'gx'=16,'gy'=4] {'depth'}, dimensions={0} | all-to-all | bytes 65536 | tf_op jit(solution)/shard_map/all_to_all | solution.py:413
  56.6 1.5 %unpack.1 = f32[2,16,256]{2,1,0:T(8,128)} custom-call(f32[64,128]{1,0:T(8,128)} %bitcast.9), custom_call_target="tpu_custom_call" | custom-call | tf_op jit(solution)/shard_map/unpack/pallas_call | solution.py:416
  (7 shorter events, 0.0 us)
Async XLA Ops:
  1.9 16.8 %copy-start = (f32[40,128]{1,0:T(8,128)S(1)}, f32[40,128]{1,0:T(8,128)}, u32[]{:S(2)}) copy-start(f32[40,128]{1,0:T(8,128)} %get-tuple-element.8) | copy-start | bytes 61444
  11.9 19.4 %collective-permute-start.3 = (f32[64,128]{1,0:T(8,128)S(1)}, f32[64,128]{1,0:T(8,128)S(1)}, u32[]{:S(2)}, u32[]{:S(2)}) collective-permute-start(f32[64,128]{1,0:T(8,128)S(1)} %bitcast.6), channel_id=1, source_target_pairs={{8,0},{12,4},{16,8},{20,12},{24,16},{28,20},{32,24},{36,28},{40,32... | collective-permute-start | bytes 98312 | tf_op jit(solution)/shard_map/ppermute | solution.py:399
  16.5 9.5 %collective-permute-start = (f32[64,128]{1,0:T(8,128)S(1)}, f32[64,128]{1,0:T(8,128)S(1)}, u32[]{:S(2)}, u32[]{:S(2)}) collective-permute-start(f32[64,128]{1,0:T(8,128)S(1)} %bitcast.7), channel_id=1, source_target_pairs={{0,8},{4,12},{8,16},{12,20},{16,24},{20,28},{24,32},{28,36},{32,40... | collective-permute-start | bytes 98312 | tf_op jit(solution)/shard_map/ppermute | solution.py:398
  18.7 12.6 %collective-permute-start.2 = (f32[104,128]{1,0:T(8,128)S(1)}, f32[104,128]{1,0:T(8,128)S(1)}, u32[]{:S(2)}, u32[]{:S(2)}) collective-permute-start(f32[104,128]{1,0:T(8,128)S(1)} %pad_maximum_fusion), channel_id=1, source_target_pairs={{4,0},{8,4},{12,8},{16,12},{20,16},{24,20},{28,24},{32,28},{36,32}... | collective-permute-start | bytes 159752 | tf_op jit(solution)/shard_map/ppermute | solution.py:397
  24.0 7.2 %collective-permute-start.1 = (f32[104,128]{1,0:T(8,128)S(1)}, f32[104,128]{1,0:T(8,128)S(1)}, u32[]{:S(2)}, u32[]{:S(2)}) collective-permute-start(f32[104,128]{1,0:T(8,128)S(1)} %pad_maximum_fusion), channel_id=1, source_target_pairs={{0,4},{4,8},{8,12},{12,16},{16,20},{20,24},{24,28},{28,32},{32,36}... | collective-permute-start | bytes 159752 | tf_op jit(solution)/shard_map/ppermute | solution.py:396
  31.3 4.5 %copy-start.1 = (s32[8,2]{0,1:T(2,128)S(1)}, s32[8,2]{0,1:T(2,128)}, u32[]{:S(2)}) copy-start(s32[8,2]{0,1:T(2,128)} %param.9) | copy-start | bytes 196
  31.4 9.4 %collective-permute-start.5 = (f32[440,128]{1,0:T(8,128)S(1)}, f32[440,128]{1,0:T(8,128)S(1)}, u32[]{:S(2)}, u32[]{:S(2)}) collective-permute-start(f32[440,128]{1,0:T(8,128)S(1)} %constant_dynamic-update-slice_fusion.refs_2_), channel_id=1, source_target_pairs={{64,128},{128,64},{192,256},{256,192},{320,384},{384,320},{448,1},... | collective-permute-start | bytes 675848 | tf_op jit(solution)/shard_map/ppermute | solution.py:410
  33.3 7.5 %collective-permute-start.4 = (f32[440,128]{1,0:T(8,128)S(1)}, f32[440,128]{1,0:T(8,128)S(1)}, u32[]{:S(2)}, u32[]{:S(2)}) collective-permute-start(f32[440,128]{1,0:T(8,128)S(1)} %constant_dynamic-update-slice_fusion.refs_2_), channel_id=1, source_target_pairs={{0,64},{64,0},{128,192},{192,128},{256,320},{320,256},{384,448},{4... | collective-permute-start | bytes 675848 | tf_op jit(solution)/shard_map/ppermute | solution.py:409

commit v4 on v3

--- a/solution.py
+++ b/solution.py
@@ -24,13 +24,15 @@
 FRAME = 80
 PAD = 8
 FULL = FRAME + 2 * PAD
-A_ROWS = 64
-S_ROWS = 40
-A_AT = (0, A_ROWS, 2 * A_ROWS + S_ROWS, 3 * A_ROWS + 2 * S_ROWS, 4 * A_ROWS + 3 * S_ROWS)
-S_AT = (2 * A_ROWS, 3 * A_ROWS + S_ROWS, 4 * A_ROWS + 2 * S_ROWS)
+TILE = 64
+A_AT = (0, 32, 96, 160, 224)
+SHARED_AT = 256
+S_AT = (288, 328, 368)
+COLUMN = 408
 MIDDLE = 40
 HALF = 8
-VMEM_BYTES = 40 * 1024 * 1024
+SWEEP_VMEM = 16 * 1024 * 1024
+SMALL_VMEM = 4 * 1024 * 1024
 
 
 def position(axis):
@@ -53,47 +55,84 @@
     return out
 
 
-def pack_kernel(slow_ref, air_ref, refl_ref, mask_ref, resid_ref, a_ref, s_ref):
+def pack_kernel(
+    slow_ref, air_ref, refl_ref, mask_ref, resid_ref, out_ref, live_ref, level_ref
+):
     lane = lane_index()
+    sub = lax.broadcasted_iota(jnp.int32, (8, LANES), 0)
+    first = 2 * position("depth")
     speed = {}
     for p in range(2):
         for h in range(2):
             for c in range(2):
                 at = (p, pl.ds(HALF * h, HALF), pl.ds(LANES * c, LANES))
                 speed[p, h, c] = jnp.where(air_ref[at] == 1, jnp.float32(AIR_SLOW), slow_ref[at])
+    for h in range(2):
+        for c in range(2):
+            here = pl.ds(HALF * h, HALF)
+            at = (here, pl.ds(LANES * c, LANES))
+            level_ref[c, here, :] = refl_ref[at].astype(jnp.float32)
+            for shot in range(SHOTS):
+                live_ref[c, shot, here, :] = jnp.where(
+                    mask_ref[shot, *at] == 1, resid_ref[shot, *at], jnp.float32(0.0)
+                )
+    rows = {}
+    for i in range(2):
+        for c in range(2):
+            at = (pl.ds(first + i, 8, stride=0), slice(None))
+            rows[2 + i, c] = level_ref[c, *at]
+            row = live_ref[c, 0, *at]
+            for shot in range(1, SHOTS):
+                row = jnp.where(sub >= shot, live_ref[c, shot, *at], row)
+            rows[i, c] = row
     for target in range(8):
         c, q = divmod(target, 4)
-        parts = [rolled(speed[j // 2, j % 2, c], STRIP * (j - q)) for j in range(4)]
-        a_ref[pl.ds(HALF * target, HALF), :] = quarters(parts, lane)
-    depth_pos = position("depth")
-    high = depth_pos >= 4
-    back = (LANES - STRIP * (depth_pos % 4)) % LANES
-
-    def strip(low_part, high_part):
-        return pltpu.roll(jnp.where(high, high_part, low_part), back, 1)
-
-    for v in range(4):
-        parts = []
-        for i in range(4):
-            x = 4 * v + i
-            pieces = [
-                jnp.where(
-                    mask_ref[:, x, pl.ds(LANES * c, LANES)] == 1,
-                    resid_ref[:, x, pl.ds(LANES * c, LANES)],
-                    jnp.float32(0.0),
-                )
-                for c in range(2)
-            ]
-            parts.append(rolled(strip(*pieces), STRIP * i))
-        s_ref[pl.ds(HALF * v, HALF), :] = quarters(parts, lane)
-    parts = []
-    for h in range(2):
-        pieces = [
-            refl_ref[pl.ds(HALF * h, HALF), pl.ds(LANES * c, LANES)].astype(jnp.float32)
-            for c in range(2)
-        ]
-        parts.append(rolled(strip(*pieces), STRIP * h))
-    s_ref[pl.ds(32, HALF), :] = quarters(parts, lane)
+        planes = quarters(
+            [rolled(speed[j // 2, j % 2, c], STRIP * (j - q)) for j in range(4)], lane
+        )
+        sources = quarters([rolled(rows[j, c], STRIP * (j - q)) for j in range(4)], lane)
+        for member in range(2):
+            at = 2 * HALF * (2 * target + member)
+            out_ref[pl.ds(at, HALF), :] = planes
+            out_ref[pl.ds(at + HALF, HALF), :] = sources
+
+
+def arrange_kernel(above_ref, own_ref, below_ref, out_ref):
+    lane = lane_index()
+    sub = lax.broadcasted_iota(jnp.int32, (8, LANES), 0)
+    second = position("gx") % 2 == 1
+    speeds = [(ref, i) for ref in (above_ref, own_ref, below_ref) for i in range(2)]
+    sources = [(above_ref, 2), (own_ref, 2), (own_ref, 3), (below_ref, 2)]
+
+    def picked(choices, i, part):
+        at = pl.ds(HALF * part, HALF)
+        (ref0, tile0), (ref1, tile1) = choices[i], choices[i + 1]
+        return jnp.where(second, ref1[tile1, at, :], ref0[tile0, at, :])
+
+    for offset in range(5):
+        for part in range(4 if offset in (0, 4) else 8):
+            out_ref[pl.ds(A_AT[offset] + HALF * part, HALF), :] = picked(speeds, offset, part)
+    lower = (lane // STRIP) % 2 == 1
+    for part in range(4, 8):
+        out_ref[pl.ds(SHARED_AT + HALF * (part - 4), HALF), :] = jnp.where(
+            lower, picked(speeds, 0, part), picked(speeds, 4, part)
+        )
+    for offset in range(3):
+        parts = [picked(sources, offset, d) for d in range(8)]
+        for v in range(4):
+            out_ref[pl.ds(S_AT[offset] + HALF * v, HALF), :] = jnp.where(
+                lane < 2 * STRIP, parts[2 * v], rolled(parts[2 * v + 1], 2 * STRIP)
+            )
+        levels = []
+        for h in range(2):
+            rows = parts[4 * h]
+            for d in range(1, 4):
+                rows = jnp.where(sub >= 2 * d, parts[4 * h + d], rows)
+            even, odd = rolled(rows, 2 * STRIP), rolled(rows, STRIP)
+            levels.append(jnp.where(sub % 2 == 1, odd, even))
+        out_ref[pl.ds(S_AT[offset] + 4 * HALF, HALF), :] = jnp.where(
+            lane < STRIP, levels[0], rolled(levels[1], STRIP)
+        )
 
 
 def sweep_kernel(
@@ -181,7 +220,10 @@
 
     for pair in range(PLANES // 2):
         for offset in range(5):
-            tiles = strips(A_AT[offset] + HALF * pair)
+            if pair >= 4 and offset in (0, 4):
+                tiles = strips(SHARED_AT + HALF * (pair - 4))
+            else:
+                tiles = strips(A_AT[offset] + HALF * pair)
             for j in range(4):
                 p, h = divmod(j, 2)
                 group = 2 * offset + h
@@ -349,7 +391,7 @@
     field = (FULL, SHOTS, LANES)
     return pl.pallas_call(
         kernel,
-        out_shape=jax.ShapeDtypeStruct((A_ROWS, LANES), jnp.float32),
+        out_shape=jax.ShapeDtypeStruct((TILE, LANES), jnp.float32),
         in_specs=in_vmem(4),
         out_specs=in_vmem(1)[0],
         scratch_shapes=[
@@ -365,7 +407,7 @@
             pltpu.VMEM((24, LANES), jnp.float32),
             pltpu.VMEM((PLANES, 24, LANES), jnp.float32),
         ],
-        compiler_params=pltpu.CompilerParams(vmem_limit_bytes=VMEM_BYTES),
+        compiler_params=pltpu.CompilerParams(vmem_limit_bytes=SWEEP_VMEM),
         name="sweep",
     )(shot_cells, near, column, far)
 
@@ -378,26 +420,45 @@
     ny_total = STRIP * depth_count * y_count
     f32 = jnp.float32
 
-    packed, sources = pl.pallas_call(
+    packed = pl.pallas_call(
         pack_kernel,
-        out_shape=(
-            jax.ShapeDtypeStruct((A_ROWS, LANES), f32),
-            jax.ShapeDtypeStruct((S_ROWS, LANES), f32),
-        ),
+        out_shape=jax.ShapeDtypeStruct((4 * TILE, LANES), f32),
         in_specs=in_vmem(5),
-        out_specs=tuple(in_vmem(2)),
+        out_specs=in_vmem(1)[0],
+        scratch_shapes=[
+            pltpu.VMEM((2, SHOTS, ROWS + 8, LANES), f32),
+            pltpu.VMEM((2, ROWS + 8, LANES), f32),
+        ],
+        compiler_params=pltpu.CompilerParams(vmem_limit_bytes=SMALL_VMEM),
         name="pack",
     )(slowness, air_mask, reflector, receiver_mask, residual)
 
-    strip = lax.all_to_all(
-        packed.reshape(8, HALF, LANES), "depth", 0, 0, tiled=True
-    ).reshape(A_ROWS, LANES)
-    whole = jnp.concatenate([strip, sources], 0)
-    above1 = lax.ppermute(whole, "gx", line(x_count, 1))
-    below1 = lax.ppermute(whole, "gx", line(x_count, -1))
-    above2 = lax.ppermute(strip, "gx", line(x_count, 2))
-    below2 = lax.ppermute(strip, "gx", line(x_count, -2))
-    column = jnp.concatenate([above2, above1, whole, below1, below2], 0)
+    pairs = [
+        [d * x_count + 2 * i + m for d in range(depth_count) for m in range(2)]
+        for i in range(x_count // 2)
+    ]
+    got = lax.all_to_all(
+        packed.reshape(16, 2 * HALF, LANES),
+        ("depth", "gx"),
+        0,
+        0,
+        tiled=True,
+        axis_index_groups=pairs,
+    )
+    own = got.reshape(8, 2, 2, HALF, LANES).transpose(2, 1, 0, 3, 4)
+    own = own.reshape(4, TILE, LANES)
+    above = lax.ppermute(
+        jnp.concatenate([own[0:2], own[3:4]], 0), "gx", line(x_count, 2)
+    )
+    below = lax.ppermute(own[0:3], "gx", line(x_count, -2))
+    column = pl.pallas_call(
+        arrange_kernel,
+        out_shape=jax.ShapeDtypeStruct((COLUMN, LANES), f32),
+        in_specs=in_vmem(3),
+        out_specs=in_vmem(1)[0],
+        compiler_params=pltpu.CompilerParams(vmem_limit_bytes=SMALL_VMEM),
+        name="arrange",
+    )(above, own, below)
 
     def place(q):
         return (q % depth_count) * y_count + q // depth_count
@@ -412,12 +473,13 @@
     strips_out = sweep_call(shot_cells, near, column, far, nx_total, ny_total)
     parts = lax.all_to_all(
         strips_out.reshape(8, HALF, LANES), "depth", 0, 0, tiled=True
-    ).reshape(A_ROWS, LANES)
+    ).reshape(TILE, LANES)
     return pl.pallas_call(
         unpack_kernel,
         out_shape=jax.ShapeDtypeStruct(slowness.shape, f32),
         in_specs=in_vmem(1),
         out_specs=in_vmem(1)[0],
+        compiler_params=pltpu.CompilerParams(vmem_limit_bytes=SMALL_VMEM),
         name="unpack",
     )(parts)
 

time: 58.5 us -> 56.4 us (0.964)
  the two profiles are of different devices: /device:TPU:388 before, /device:TPU:420 now
where the time goes in v4:
time: 56.4 us; the launch traced here: 55.9 us
  blocking collectives  19 us (34%)
  waiting for transfers between devices  13.3 us (24%)
  starting transfers between devices  11.1 us (20%)
  Pallas kernels  8.32 us (15%)
  local copies, waits for them, and re-layouts  4.15 us (7%)
    all_to_all x1, blocking collectives, local(): lax.all_to_all(packed.reshape(16, 2 * HALF, LANES), ('depth', 'gx'), 0, 0...  11.2 us
    all_to_all x1, blocking collectives, local(): lax.all_to_all(strips_out.reshape(8, HALF, LANES), 'depth', 0, 0, tiled=T...  7.81 us
    ppermute x1, waiting for transfers between devices, local(): lax.ppermute(jnp.concatenate([own[0:2], own[3:4]], 0), 'gx', line(x_count...  7.54 us
    pallas_call x1, Pallas kernels, sweep_call(): pl.pallas_call(kernel, out_shape=jax.ShapeDtypeStruct((TILE, LANES), jnp....  7.34 us
    ppermute x1, waiting for transfers between devices, local(): far = lax.ppermute(column, ('depth', 'gy'), swapped(1))  4.8 us
    ppermute x1, starting transfers between devices, local(): below = lax.ppermute(own[0:3], 'gx', line(x_count, -2))  4.57 us
    unnamed x13, local copies, waits for them, and re-layouts  4.13 us
    ppermute x1, starting transfers between devices, local(): near = lax.ppermute(column, ('depth', 'gy'), swapped(0))  2.4 us
  transfers between devices with their start and end apart: 4, of which 3 were waited for; matrix products, arithmetic and copies ran while one was open for 0% of the time, Pallas kernels for 0%

profile of v4, /device:TPU:420, one launch (start us, length us, event | category | flops | bytes accessed | tf_op | source)
XLA Modules:
  0.0 55.9 jit_solution(15818750029937839250)
XLA Ops:
  0.0 0.0 copy-start
  0.0 0.9 %copy-done = s32[8,16,256]{2,1,0:T(8,128)S(1)} copy-done((s32[8,16,256]{2,1,0:T(8,128)S(1)}, s32[8,16,256]{2,1,0:T(8,128)}, u32[]{:S(2)}) %copy-start) | copy-done | bytes 131096
  0.9 0.0 copy-start.1
  0.9 0.9 %copy-done.1 = f32[8,16,256]{2,1,0:T(8,128)S(1)} copy-done((f32[8,16,256]{2,1,0:T(8,128)S(1)}, f32[8,16,256]{2,1,0:T(8,128)}, u32[]{:S(2)}) %copy-start.1) | copy-done | bytes 131096
  1.8 0.0 copy-start.2
  1.8 0.8 %copy-done.2 = f32[2,16,256]{2,1,0:T(8,128)S(1)} copy-done((f32[2,16,256]{2,1,0:T(8,128)S(1)}, f32[2,16,256]{2,1,0:T(8,128)}, u32[]{:S(2)}) %copy-start.2) | copy-done | bytes 32792
  2.6 0.0 copy-start.3
  2.6 0.8 %copy-done.3 = s32[2,16,256]{2,1,0:T(8,128)S(1)} copy-done((s32[2,16,256]{2,1,0:T(8,128)S(1)}, s32[2,16,256]{2,1,0:T(8,128)}, u32[]{:S(2)}) %copy-start.3) | copy-done | bytes 32792
  3.3 0.0 copy-start.4
  3.3 0.7 %copy-done.4 = s32[16,256]{1,0:T(8,128)S(1)} copy-done((s32[16,256]{1,0:T(8,128)S(1)}, s32[16,256]{1,0:T(8,128)}, u32[]{:S(2)}) %copy-start.4) | copy-done | bytes 16408
  4.0 0.1 pack.1
  4.2 11.2 %all_to_all.10 = f32[16,16,128]{2,1,0:T(8,128)S(1)} all-to-all(f32[16,16,128]{2,1,0:T(8,128)S(1)} %bitcast.12), channel_id=1, replica_groups={{0,4,64,68,128,132,192,196,256,260,320,324,384,388,448,452},{8,12,72,76..., dimensions={0} | all-to-all | bytes 262144 | tf_op jit(solution)/shard_map/all_to_all | solution.py:440
  15.5 4.6 %collective-permute-start.1 = (f32[3,64,128]{2,1,0:T(8,128)S(1)}, f32[3,64,128]{2,1,0:T(8,128)S(1)}, u32[]{:S(2)}, u32[]{:S(2)}) collective-permute-start(f32[3,64,128]{2,1,0:T(8,128)S(1)} %slice.18), channel_id=1, source_target_pairs={{8,0},{12,4},{16,8},{20,12},{24,16},{28,20},{32,24},{36,28},{40,32... | collective-permute-start | bytes 294920 | tf_op jit(solution)/shard_map/ppermute | solution.py:453
  20.0 0.0 copy-start.5
  20.1 2.2 %collective-permute-start = (f32[3,64,128]{2,1,0:T(8,128)S(1)}, f32[3,64,128]{2,1,0:T(8,128)S(1)}, u32[]{:S(2)}, u32[]{:S(2)}) collective-permute-start(f32[3,64,128]{2,1,0:T(8,128)S(1)} %pad_maximum_fusion), channel_id=1, source_target_pairs={{0,8},{4,12},{8,16},{12,20},{16,24},{20,28},{24,32},{28,36},{32,40... | collective-permute-start | bytes 294920 | tf_op jit(solution)/shard_map/ppermute | solution.py:450
  22.2 0.9 %collective-permute-done.1.below_ref = f32[3,64,128]{2,1,0:T(8,128)S(1)} collective-permute-done((f32[3,64,128]{2,1,0:T(8,128)S(1)}, f32[3,64,128]{2,1,0:T(8,128)S(1)}, u32[]{:S(2)}, u32[]{:S(2)}) %collective-permute-start.1) | collective-permute-done | bytes 98336 | tf_op jit(solution)/shard_map/ppermute | solution.py:453
  23.2 7.5 %collective-permute-done.above_ref = f32[3,64,128]{2,1,0:T(8,128)S(1)} collective-permute-done((f32[3,64,128]{2,1,0:T(8,128)S(1)}, f32[3,64,128]{2,1,0:T(8,128)S(1)}, u32[]{:S(2)}, u32[]{:S(2)}) %collective-permute-start) | collective-permute-done | bytes 98336 | tf_op jit(solution)/shard_map/ppermute | solution.py:450
  30.7 0.1 arrange.1.refs_2_
  30.9 1.9 %collective-permute-start.3 = (f32[408,128]{1,0:T(8,128)S(1)}, f32[408,128]{1,0:T(8,128)S(1)}, u32[]{:S(2)}, u32[]{:S(2)}) collective-permute-start(f32[408,128]{1,0:T(8,128)S(1)} %arrange.1.refs_2_), channel_id=1, source_target_pairs={{64,128},{128,64},{192,256},{256,192},{320,384},{384,320},{448,1},... | collective-permute-start | bytes 626696 | tf_op jit(solution)/shard_map/ppermute | solution.py:471
  32.8 2.4 %collective-permute-start.2 = (f32[408,128]{1,0:T(8,128)S(1)}, f32[408,128]{1,0:T(8,128)S(1)}, u32[]{:S(2)}, u32[]{:S(2)}) collective-permute-start(f32[408,128]{1,0:T(8,128)S(1)} %arrange.1.refs_2_), channel_id=1, source_target_pairs={{0,64},{64,0},{128,192},{192,128},{256,320},{320,256},{384,448},{4... | collective-permute-start | bytes 626696 | tf_op jit(solution)/shard_map/ppermute | solution.py:470
  35.2 0.0 copy-done.5
  35.2 0.1 copy.10.refs_0_
  35.3 4.8 %collective-permute-done.3.refs_3_ = f32[408,128]{1,0:T(8,128)S(1)} collective-permute-done((f32[408,128]{1,0:T(8,128)S(1)}, f32[408,128]{1,0:T(8,128)S(1)}, u32[]{:S(2)}, u32[]{:S(2)}) %collective-permute-start.3) | collective-permute-done | bytes 208928 | tf_op jit(solution)/shard_map/ppermute | solution.py:471
  40.1 0.0 collective-permute-done.2.refs_1_
  40.1 7.3 %sweep.1 = f32[64,128]{1,0:T(8,128)S(1)} custom-call(s32[8,2]{1,0:T(8,128)S(1)} %copy.10.refs_0_, f32[408,128]{1,0:T(8,128)S(1)} %collective-permute-done.2.refs_1_, f32[408,128]{1,0:T(8,128)S(1)} %arrange.1.refs_2_, f32[408,128]{1,0:T(8,128)S(1)} %collective-permute-done.3.refs_3_), custom_call_target="tpu_custom_call" | custom-call | tf_op jit(solution)/shard_map/sweep/pallas_call | solution.py:392
  47.4 7.8 %all_to_all.11 = f32[8,8,128]{2,1,0:T(8,128)S(1)} all-to-all(f32[8,8,128]{2,1,0:T(8,128)S(1)} %bitcast.14), channel_id=1, replica_groups=mesh['depth'=8,'gx'=16,'gy'=4] {'depth'}, dimensions={0} | all-to-all | bytes 65536 | tf_op jit(solution)/shard_map/all_to_all | solution.py:474
  55.2 0.7 %unpack.1 = f32[2,16,256]{2,1,0:T(8,128)} custom-call(f32[64,128]{1,0:T(8,128)S(1)} %bitcast.13), custom_call_target="tpu_custom_call" | custom-call | tf_op jit(solution)/shard_map/unpack/pallas_call | solution.py:477
  (5 shorter events, 0.0 us)
Async XLA Ops:
  0.0 0.9 %copy-start = (s32[8,16,256]{2,1,0:T(8,128)S(1)}, s32[8,16,256]{2,1,0:T(8,128)}, u32[]{:S(2)}) copy-start(s32[8,16,256]{2,1,0:T(8,128)} %mask_ref.1) | copy-start | bytes 393220
  0.9 0.9 %copy-start.1 = (f32[8,16,256]{2,1,0:T(8,128)S(1)}, f32[8,16,256]{2,1,0:T(8,128)}, u32[]{:S(2)}) copy-start(f32[8,16,256]{2,1,0:T(8,128)} %resid_ref.1) | copy-start | bytes 393220
  1.8 0.8 %copy-start.2 = (f32[2,16,256]{2,1,0:T(8,128)S(1)}, f32[2,16,256]{2,1,0:T(8,128)}, u32[]{:S(2)}) copy-start(f32[2,16,256]{2,1,0:T(8,128)} %slow_ref.1) | copy-start | bytes 98308
  2.6 0.8 %copy-start.3 = (s32[2,16,256]{2,1,0:T(8,128)S(1)}, s32[2,16,256]{2,1,0:T(8,128)}, u32[]{:S(2)}) copy-start(s32[2,16,256]{2,1,0:T(8,128)} %air_ref.1) | copy-start | bytes 98308
  3.3 0.7 %copy-start.4 = (s32[16,256]{1,0:T(8,128)S(1)}, s32[16,256]{1,0:T(8,128)}, u32[]{:S(2)}) copy-start(s32[16,256]{1,0:T(8,128)} %refl_ref.1) | copy-start | bytes 49156
  15.5 7.7 %collective-permute-start.1 = (f32[3,64,128]{2,1,0:T(8,128)S(1)}, f32[3,64,128]{2,1,0:T(8,128)S(1)}, u32[]{:S(2)}, u32[]{:S(2)}) collective-permute-start(f32[3,64,128]{2,1,0:T(8,128)S(1)} %slice.18), channel_id=1, source_target_pairs={{8,0},{12,4},{16,8},{20,12},{24,16},{28,20},{32,24},{36,28},{40,32... | collective-permute-start | bytes 294920 | tf_op jit(solution)/shard_map/ppermute | solution.py:453
  20.0 15.1 %copy-start.5 = (s32[8,2]{0,1:T(2,128)S(1)}, s32[8,2]{0,1:T(2,128)}, u32[]{:S(2)}) copy-start(s32[8,2]{0,1:T(2,128)} %param.9) | copy-start | bytes 196
  20.1 10.6 %collective-permute-start = (f32[3,64,128]{2,1,0:T(8,128)S(1)}, f32[3,64,128]{2,1,0:T(8,128)S(1)}, u32[]{:S(2)}, u32[]{:S(2)}) collective-permute-start(f32[3,64,128]{2,1,0:T(8,128)S(1)} %pad_maximum_fusion), channel_id=1, source_target_pairs={{0,8},{4,12},{8,16},{12,20},{16,24},{20,28},{24,32},{28,36},{32,40... | collective-permute-start | bytes 294920 | tf_op jit(solution)/shard_map/ppermute | solution.py:450
  30.9 9.2 %collective-permute-start.3 = (f32[408,128]{1,0:T(8,128)S(1)}, f32[408,128]{1,0:T(8,128)S(1)}, u32[]{:S(2)}, u32[]{:S(2)}) collective-permute-start(f32[408,128]{1,0:T(8,128)S(1)} %arrange.1.refs_2_), channel_id=1, source_target_pairs={{64,128},{128,64},{192,256},{256,192},{320,384},{384,320},{448,1},... | collective-permute-start | bytes 626696 | tf_op jit(solution)/shard_map/ppermute | solution.py:471
  32.8 7.3 %collective-permute-start.2 = (f32[408,128]{1,0:T(8,128)S(1)}, f32[408,128]{1,0:T(8,128)S(1)}, u32[]{:S(2)}, u32[]{:S(2)}) collective-permute-start(f32[408,128]{1,0:T(8,128)S(1)} %arrange.1.refs_2_), channel_id=1, source_target_pairs={{0,64},{64,0},{128,192},{192,128},{256,320},{320,256},{384,448},{4... | collective-permute-start | bytes 626696 | tf_op jit(solution)/shard_map/ppermute | solution.py:470

commit v5 on v4

--- a/solution.py
+++ b/solution.py
@@ -33,6 +33,7 @@
 HALF = 8
 SWEEP_VMEM = 16 * 1024 * 1024
 SMALL_VMEM = 4 * 1024 * 1024
+PACK_VMEM = 60 * 1024 * 1024
 
 
 def position(axis):
@@ -55,9 +56,14 @@
     return out
 
 
-def pack_kernel(
-    slow_ref, air_ref, refl_ref, mask_ref, resid_ref, out_ref, live_ref, level_ref
-):
+def pack_kernel(*refs):
+    out_ref, live_ref, level_ref, sems = refs[5], refs[11], refs[12], refs[13]
+    copies = [pltpu.make_async_copy(refs[i], refs[6 + i], sems.at[i]) for i in range(5)]
+    for copy in copies:
+        copy.start()
+    for copy in copies:
+        copy.wait()
+    slow_ref, air_ref, refl_ref, mask_ref, resid_ref = refs[6:11]
     lane = lane_index()
     sub = lax.broadcasted_iota(jnp.int32, (8, LANES), 0)
     first = 2 * position("depth")
@@ -97,32 +103,18 @@
             out_ref[pl.ds(at + HALF, HALF), :] = sources
 
 
-def arrange_kernel(above_ref, own_ref, below_ref, out_ref):
+def stage_kernel(got_ref, own_ref, up_ref, down_ref):
     lane = lane_index()
     sub = lax.broadcasted_iota(jnp.int32, (8, LANES), 0)
-    second = position("gx") % 2 == 1
-    speeds = [(ref, i) for ref in (above_ref, own_ref, below_ref) for i in range(2)]
-    sources = [(above_ref, 2), (own_ref, 2), (own_ref, 3), (below_ref, 2)]
-
-    def picked(choices, i, part):
-        at = pl.ds(HALF * part, HALF)
-        (ref0, tile0), (ref1, tile1) = choices[i], choices[i + 1]
-        return jnp.where(second, ref1[tile1, at, :], ref0[tile0, at, :])
-
-    for offset in range(5):
-        for part in range(4 if offset in (0, 4) else 8):
-            out_ref[pl.ds(A_AT[offset] + HALF * part, HALF), :] = picked(speeds, offset, part)
-    lower = (lane // STRIP) % 2 == 1
-    for part in range(4, 8):
-        out_ref[pl.ds(SHARED_AT + HALF * (part - 4), HALF), :] = jnp.where(
-            lower, picked(speeds, 0, part), picked(speeds, 4, part)
-        )
-    for offset in range(3):
-        parts = [picked(sources, offset, d) for d in range(8)]
-        for v in range(4):
-            out_ref[pl.ds(S_AT[offset] + HALF * v, HALF), :] = jnp.where(
-                lane < 2 * STRIP, parts[2 * v], rolled(parts[2 * v + 1], 2 * STRIP)
-            )
+    odd_quarter = (lane // STRIP) % 2 == 1
+    speed = [[got_ref[4 * d + 2 * m] for d in range(8)] for m in range(2)]
+    source = []
+    for m in range(2):
+        parts = [got_ref[4 * d + 2 * m + 1] for d in range(8)]
+        tiles = [
+            jnp.where(lane < 2 * STRIP, parts[2 * v], rolled(parts[2 * v + 1], 2 * STRIP))
+            for v in range(4)
+        ]
         levels = []
         for h in range(2):
             rows = parts[4 * h]
@@ -130,9 +122,63 @@
                 rows = jnp.where(sub >= 2 * d, parts[4 * h + d], rows)
             even, odd = rolled(rows, 2 * STRIP), rolled(rows, STRIP)
             levels.append(jnp.where(sub % 2 == 1, odd, even))
-        out_ref[pl.ds(S_AT[offset] + 4 * HALF, HALF), :] = jnp.where(
-            lane < STRIP, levels[0], rolled(levels[1], STRIP)
+        tiles.append(jnp.where(lane < STRIP, levels[0], rolled(levels[1], STRIP)))
+        source.append(tiles)
+    outer_up = [
+        jnp.where(odd_quarter, speed[0][d], rolled(speed[0][d + 1], -STRIP)) for d in (4, 6)
+    ]
+    outer_down = [
+        jnp.where(odd_quarter, rolled(speed[1][d + 1], STRIP), speed[1][d]) for d in (4, 6)
+    ]
+    for ref, tiles in (
+        (own_ref, [*speed[0], *speed[1], *source[0], *source[1]]),
+        (up_ref, [*speed[0][:4], *outer_up, *speed[1], *source[1]]),
+        (down_ref, [*speed[0], *speed[1][:4], *outer_down, *source[0]]),
+    ):
+        for i, tile in enumerate(tiles):
+            ref[i] = tile
+
+
+def arrange_kernel(above_ref, own_ref, below_ref, out_ref):
+    lane = lane_index()
+    second = position("gx") % 2 == 1
+    odd_quarter = (lane // STRIP) % 2 == 1
+
+    def outer(ref, first, shift):
+        tiles = [ref[first + i] for i in range(4)]
+        for i in (4, 5):
+            part = ref[first + i]
+            moved = rolled(part, shift)
+            tiles += [part, moved]
+        return tiles
+
+    speeds = [
+        outer(above_ref, 0, STRIP),
+        [above_ref[6 + i] for i in range(8)],
+        [own_ref[i] for i in range(8)],
+        [own_ref[8 + i] for i in range(8)],
+        [below_ref[i] for i in range(8)],
+        outer(below_ref, 8, -STRIP),
+    ]
+    sources = [
+        [ref[first + i] for i in range(5)]
+        for ref, first in ((above_ref, 14), (own_ref, 16), (own_ref, 21), (below_ref, 14))
+    ]
+
+    def picked(choices, i, part):
+        return jnp.where(second, choices[i + 1][part], choices[i][part])
+
+    for offset in range(5):
+        for part in range(4 if offset in (0, 4) else 8):
+            out_ref[pl.ds(A_AT[offset] + HALF * part, HALF), :] = picked(speeds, offset, part)
+    for part in range(4, 8):
+        out_ref[pl.ds(SHARED_AT + HALF * (part - 4), HALF), :] = jnp.where(
+            odd_quarter, picked(speeds, 0, part), picked(speeds, 4, part)
         )
+    for offset in range(3):
+        for part in range(5):
+            at = pl.ds(S_AT[offset] + HALF * part, HALF)
+            out_ref[at, :] = picked(sources, offset, part)
 
 
 def sweep_kernel(
@@ -423,13 +469,18 @@
     packed = pl.pallas_call(
         pack_kernel,
         out_shape=jax.ShapeDtypeStruct((4 * TILE, LANES), f32),
-        in_specs=in_vmem(5),
+        in_specs=[pl.BlockSpec(memory_space=pltpu.HBM)] * 5,
         out_specs=in_vmem(1)[0],
         scratch_shapes=[
+            *[
+                pltpu.VMEM(arg.shape, arg.dtype)
+                for arg in (slowness, air_mask, reflector, receiver_mask, residual)
+            ],
             pltpu.VMEM((2, SHOTS, ROWS + 8, LANES), f32),
             pltpu.VMEM((2, ROWS + 8, LANES), f32),
+            pltpu.SemaphoreType.DMA((5,)),
         ],
-        compiler_params=pltpu.CompilerParams(vmem_limit_bytes=SMALL_VMEM),
+        compiler_params=pltpu.CompilerParams(vmem_limit_bytes=PACK_VMEM),
         name="pack",
     )(slowness, air_mask, reflector, receiver_mask, residual)
 
@@ -445,12 +496,16 @@
         tiled=True,
         axis_index_groups=pairs,
     )
-    own = got.reshape(8, 2, 2, HALF, LANES).transpose(2, 1, 0, 3, 4)
-    own = own.reshape(4, TILE, LANES)
-    above = lax.ppermute(
-        jnp.concatenate([own[0:2], own[3:4]], 0), "gx", line(x_count, 2)
-    )
-    below = lax.ppermute(own[0:3], "gx", line(x_count, -2))
+    own, up, down = pl.pallas_call(
+        stage_kernel,
+        out_shape=tuple(jax.ShapeDtypeStruct((n, HALF, LANES), f32) for n in (26, 19, 19)),
+        in_specs=in_vmem(1),
+        out_specs=tuple(in_vmem(3)),
+        compiler_params=pltpu.CompilerParams(vmem_limit_bytes=SMALL_VMEM),
+        name="stage",
+    )(got.reshape(32, HALF, LANES))
+    above = lax.ppermute(up, "gx", line(x_count, 2))
+    below = lax.ppermute(down, "gx", line(x_count, -2))
     column = pl.pallas_call(
         arrange_kernel,
         out_shape=jax.ShapeDtypeStruct((COLUMN, LANES), f32),

time: 56.4 us -> 56.1 us (level)
  the two profiles are of different devices: /device:TPU:420 before, /device:TPU:66 now
where the time goes in v5:
time: 56.1 us; the launch traced here: 55.8 us
  blocking collectives  20.3 us (36%)
  starting transfers between devices  12.8 us (23%)
  waiting for transfers between devices  12.5 us (22%)
  Pallas kernels  10.1 us (18%)
    all_to_all x1, blocking collectives, local(): lax.all_to_all(packed.reshape(16, 2 * HALF, LANES), ('depth', 'gx'), 0, 0...  12.5 us
    all_to_all x1, blocking collectives, local(): lax.all_to_all(strips_out.reshape(8, HALF, LANES), 'depth', 0, 0, tiled=T...  7.81 us
    pallas_call x1, Pallas kernels, sweep_call(): pl.pallas_call(kernel, out_shape=jax.ShapeDtypeStruct((TILE, LANES), jnp....  7.34 us
    ppermute x1, waiting for transfers between devices, local(): below = lax.ppermute(down, 'gx', line(x_count, -2))  7.27 us
    ppermute x1, starting transfers between devices, local(): above = lax.ppermute(up, 'gx', line(x_count, 2))  6.38 us
    ppermute x1, waiting for transfers between devices, local(): far = lax.ppermute(column, ('depth', 'gy'), swapped(1))  4.62 us
    ppermute x1, starting transfers between devices, local(): far = lax.ppermute(column, ('depth', 'gy'), swapped(1))  2.45 us
    ppermute x1, starting transfers between devices, local(): near = lax.ppermute(column, ('depth', 'gy'), swapped(0))  2.03 us
  transfers between devices with their start and end apart: 4, of which 3 were waited for; matrix products, arithmetic and copies ran while one was open for 0% of the time, Pallas kernels for 0%

profile of v5, /device:TPU:66, one launch (start us, length us, event | category | flops | bytes accessed | tf_op | source)
XLA Modules:
  0.0 55.8 jit_solution(10348986127588845495)
XLA Ops:
  0.0 1.8 %pack.1 = f32[256,128]{1,0:T(8,128)} custom-call(f32[2,16,256]{2,1,0:T(8,128)} %refs_0_.2, s32[2,16,256]{2,1,0:T(8,128)} %refs_1_.1, s32[16,256]{1,0:T(8,128)} %refs_2_.1, s32[8,16,256]{2,1,0:T(8,128)} %refs_3_.1, f32[8,16,256]{2,1,0:T(8,128)} %refs_4_.1), custom_call_target="tpu_custom_call" | custom-call | tf_op jit(solution)/shard_map/pack/pallas_call | solution.py:469
  1.8 12.5 %all_to_all.10 = f32[16,16,128]{2,1,0:T(8,128)S(1)} all-to-all(f32[16,16,128]{2,1,0:T(8,128)} %bitcast.7), channel_id=1, replica_groups={{0,4,64,68,128,132,192,196,256,260,320,324,384,388,448,452},{8,12,72,76..., dimensions={0} | all-to-all | bytes 262144 | tf_op jit(solution)/shard_map/all_to_all | solution.py:491
  14.4 0.1 stage.1
  14.5 6.4 %collective-permute-start = (f32[19,8,128]{2,1,0:T(8,128)S(1)}, f32[19,8,128]{2,1,0:T(8,128)S(1)}, u32[]{:S(2)}, u32[]{:S(2)}) collective-permute-start(f32[19,8,128]{2,1,0:T(8,128)S(1)} %get-tuple-element.8), channel_id=1, source_target_pairs={{0,8},{4,12},{8,16},{12,20},{16,24},{20,28},{24,32},{28,36},{32,40... | collective-permute-start | bytes 233480 | tf_op jit(solution)/shard_map/ppermute | solution.py:507
  20.9 1.9 %collective-permute-start.1 = (f32[19,8,128]{2,1,0:T(8,128)S(1)}, f32[19,8,128]{2,1,0:T(8,128)S(1)}, u32[]{:S(2)}, u32[]{:S(2)}) collective-permute-start(f32[19,8,128]{2,1,0:T(8,128)S(1)} %get-tuple-element.10), channel_id=1, source_target_pairs={{8,0},{12,4},{16,8},{20,12},{24,16},{28,20},{32,24},{36,28},{40,32... | collective-permute-start | bytes 233480 | tf_op jit(solution)/shard_map/ppermute | solution.py:508
  22.8 0.6 %collective-permute-done.above_ref = f32[19,8,128]{2,1,0:T(8,128)S(1)} collective-permute-done((f32[19,8,128]{2,1,0:T(8,128)S(1)}, f32[19,8,128]{2,1,0:T(8,128)S(1)}, u32[]{:S(2)}, u32[]{:S(2)}) %collective-permute-start) | collective-permute-done | bytes 77856 | tf_op jit(solution)/shard_map/ppermute | solution.py:507
  23.4 7.3 %collective-permute-done.1.below_ref = f32[19,8,128]{2,1,0:T(8,128)S(1)} collective-permute-done((f32[19,8,128]{2,1,0:T(8,128)S(1)}, f32[19,8,128]{2,1,0:T(8,128)S(1)}, u32[]{:S(2)}, u32[]{:S(2)}) %collective-permute-start.1) | collective-permute-done | bytes 77856 | tf_op jit(solution)/shard_map/ppermute | solution.py:508
  30.7 0.0 copy-start
  30.7 0.1 arrange.1.refs_2_
  30.8 2.5 %collective-permute-start.3 = (f32[408,128]{1,0:T(8,128)S(1)}, f32[408,128]{1,0:T(8,128)S(1)}, u32[]{:S(2)}, u32[]{:S(2)}) collective-permute-start(f32[408,128]{1,0:T(8,128)S(1)} %arrange.1.refs_2_), channel_id=1, source_target_pairs={{64,128},{128,64},{192,256},{256,192},{320,384},{384,320},{448,1},... | collective-permute-start | bytes 626696 | tf_op jit(solution)/shard_map/ppermute | solution.py:526
  33.2 2.0 %collective-permute-start.2 = (f32[408,128]{1,0:T(8,128)S(1)}, f32[408,128]{1,0:T(8,128)S(1)}, u32[]{:S(2)}, u32[]{:S(2)}) collective-permute-start(f32[408,128]{1,0:T(8,128)S(1)} %arrange.1.refs_2_), channel_id=1, source_target_pairs={{0,64},{64,0},{128,192},{192,128},{256,320},{320,256},{384,448},{4... | collective-permute-start | bytes 626696 | tf_op jit(solution)/shard_map/ppermute | solution.py:525
  35.3 0.0 copy-done
  35.3 0.1 copy.7.refs_0_
  35.4 4.6 %collective-permute-done.3.refs_3_ = f32[408,128]{1,0:T(8,128)S(1)} collective-permute-done((f32[408,128]{1,0:T(8,128)S(1)}, f32[408,128]{1,0:T(8,128)S(1)}, u32[]{:S(2)}, u32[]{:S(2)}) %collective-permute-start.3) | collective-permute-done | bytes 208928 | tf_op jit(solution)/shard_map/ppermute | solution.py:526
  40.0 0.0 collective-permute-done.2.refs_1_
  40.0 7.3 %sweep.1 = f32[64,128]{1,0:T(8,128)S(1)} custom-call(s32[8,2]{1,0:T(8,128)S(1)} %copy.7.refs_0_, f32[408,128]{1,0:T(8,128)S(1)} %collective-permute-done.2.refs_1_, f32[408,128]{1,0:T(8,128)S(1)} %arrange.1.refs_2_, f32[408,128]{1,0:T(8,128)S(1)} %collective-permute-done.3.refs_3_), custom_call_target="tpu_custom_call" | custom-call | tf_op jit(solution)/shard_map/sweep/pallas_call | solution.py:438
  47.3 7.8 %all_to_all.11 = f32[8,8,128]{2,1,0:T(8,128)S(1)} all-to-all(f32[8,8,128]{2,1,0:T(8,128)S(1)} %bitcast.6), channel_id=1, replica_groups=mesh['depth'=8,'gx'=16,'gy'=4] {'depth'}, dimensions={0} | all-to-all | bytes 65536 | tf_op jit(solution)/shard_map/all_to_all | solution.py:529
  55.1 0.7 %unpack.1 = f32[2,16,256]{2,1,0:T(8,128)} custom-call(f32[64,128]{1,0:T(8,128)S(1)} %bitcast.5), custom_call_target="tpu_custom_call" | custom-call | tf_op jit(solution)/shard_map/unpack/pallas_call | solution.py:532
Async XLA Ops:
  14.5 8.9 %collective-permute-start = (f32[19,8,128]{2,1,0:T(8,128)S(1)}, f32[19,8,128]{2,1,0:T(8,128)S(1)}, u32[]{:S(2)}, u32[]{:S(2)}) collective-permute-start(f32[19,8,128]{2,1,0:T(8,128)S(1)} %get-tuple-element.8), channel_id=1, source_target_pairs={{0,8},{4,12},{8,16},{12,20},{16,24},{20,28},{24,32},{28,36},{32,40... | collective-permute-start | bytes 233480 | tf_op jit(solution)/shard_map/ppermute | solution.py:507
  20.9 9.8 %collective-permute-start.1 = (f32[19,8,128]{2,1,0:T(8,128)S(1)}, f32[19,8,128]{2,1,0:T(8,128)S(1)}, u32[]{:S(2)}, u32[]{:S(2)}) collective-permute-start(f32[19,8,128]{2,1,0:T(8,128)S(1)} %get-tuple-element.10), channel_id=1, source_target_pairs={{8,0},{12,4},{16,8},{20,12},{24,16},{28,20},{32,24},{36,28},{40,32... | collective-permute-start | bytes 233480 | tf_op jit(solution)/shard_map/ppermute | solution.py:508
  30.7 4.6 %copy-start = (s32[8,2]{0,1:T(2,128)S(1)}, s32[8,2]{0,1:T(2,128)}, u32[]{:S(2)}) copy-start(s32[8,2]{0,1:T(2,128)} %param.9) | copy-start | bytes 196
  30.8 9.2 %collective-permute-start.3 = (f32[408,128]{1,0:T(8,128)S(1)}, f32[408,128]{1,0:T(8,128)S(1)}, u32[]{:S(2)}, u32[]{:S(2)}) collective-permute-start(f32[408,128]{1,0:T(8,128)S(1)} %arrange.1.refs_2_), channel_id=1, source_target_pairs={{64,128},{128,64},{192,256},{256,192},{320,384},{384,320},{448,1},... | collective-permute-start | bytes 626696 | tf_op jit(solution)/shard_map/ppermute | solution.py:526
  33.2 6.8 %collective-permute-start.2 = (f32[408,128]{1,0:T(8,128)S(1)}, f32[408,128]{1,0:T(8,128)S(1)}, u32[]{:S(2)}, u32[]{:S(2)}) collective-permute-start(f32[408,128]{1,0:T(8,128)S(1)} %arrange.1.refs_2_), channel_id=1, source_target_pairs={{0,64},{64,0},{128,192},{192,128},{256,320},{320,256},{384,448},{4... | collective-permute-start | bytes 626696 | tf_op jit(solution)/shard_map/ppermute | solution.py:525

commit v6 on v5

--- a/solution.py
+++ b/solution.py
@@ -12,7 +12,7 @@
 AIR_SLOW = 2.5
 AIR_TEST = 2.0
 STEP_PENALTY = 10000.0
-RATE = 1.0 / SOFTMIN_TEMPER
+RATE = -1.0 / (SOFTMIN_TEMPER * math.log(2.0))
 ROOT2 = math.sqrt(2.0)
 ROOT3 = math.sqrt(3.0)
 
@@ -33,7 +33,6 @@
 HALF = 8
 SWEEP_VMEM = 16 * 1024 * 1024
 SMALL_VMEM = 4 * 1024 * 1024
-PACK_VMEM = 60 * 1024 * 1024
 
 
 def position(axis):
@@ -220,10 +219,9 @@
             return ref[pl.ds(r, 8, stride=0), :]
         return ref[lead, pl.ds(r, 8, stride=0), :]
 
-    def rim_factor(x_cell):
+    def penalty(x_cell):
         inside = (x_cell >= 0) & (x_cell < nx_total) & y_inside
-        penalty = jnp.where(inside, jnp.float32(0.0), jnp.float32(STEP_PENALTY))
-        return jnp.exp(-penalty * RATE)
+        return jnp.where(inside, jnp.float32(0.0), jnp.float32(STEP_PENALTY))
 
     shot_x = jnp.broadcast_to(shot_ref[:, 0:1].astype(jnp.float32), (8, LANES))
     shot_y = jnp.broadcast_to(shot_ref[:, 1:2].astype(jnp.float32), (8, LANES))
@@ -234,7 +232,7 @@
         return SURF * jnp.sqrt((x_cell - shot_x) ** 2 + y_square)
 
     def weight(diff):
-        return jnp.exp(-diff * RATE)
+        return jnp.exp2(diff * RATE)
 
     def near(diff):
         return jnp.clip(diff, -1.0, 1.0)
@@ -243,7 +241,7 @@
     weight_minus = weight(near(pltpu.roll(middle, 1, 1) - middle))
     weight_plus = weight(near(pltpu.roll(middle, LANES - 1, 1) - middle))
     for r in range(FRAME):
-        wa_ref[r + PAD] = weight(surface(r) - middle) * rim_factor(x_base + r)
+        wa_ref[r + PAD] = weight((surface(r) - middle) + penalty(x_base + r))
     for ref in (wa_ref, wb_ref):
         ref[PAD - 1] = zero
         ref[PAD + FRAME] = zero
@@ -262,7 +260,7 @@
         right = jnp.where(odd, two, one)
         return left, rolled(here_ref[at], STRIP), rolled(right, 2 * STRIP)
 
-    rims = [rim_factor(x_base + HALF * g + sub) for g in range(FRAME // HALF)]
+    rims = [penalty(x_base + HALF * g + sub) for g in range(FRAME // HALF)]
 
     for pair in range(PLANES // 2):
         for offset in range(5):
@@ -277,9 +275,10 @@
                     continue
                 speed = merged(tiles, j)
                 at = (2 * pair + p, pl.ds(HALF * group, HALF), slice(None))
-                e1_ref[at] = jnp.exp(-speed * RATE) * rims[group]
-                e2_ref[at] = jnp.exp(-(speed * ROOT2) * RATE) * rims[group]
-                e3_ref[at] = jnp.exp(-(speed * ROOT3) * RATE) * rims[group]
+                slow = speed + rims[group]
+                e1_ref[at] = jnp.exp2(slow * RATE)
+                e2_ref[at] = jnp.exp2(slow * (ROOT2 * RATE))
+                e3_ref[at] = jnp.exp2(slow * (ROOT3 * RATE))
                 if 3 <= group < 7:
                     here = (2 * pair + p, pl.ds(HALF * (group - 3), HALF), slice(None))
                     earth_ref[here] = speed
@@ -291,7 +290,7 @@
                 src_ref[ROWS * offset + 4 * v + i] = merged(tiles, i)
         tiles = strips(S_AT[offset] + 32)
         for h in range(2):
-            inside = rims[2 + 2 * offset + h] > 0.5
+            inside = rims[2 + 2 * offset + h] < 0.5
             refl_ref[pl.ds(ROWS * offset + HALF * h, HALF), :] = jnp.where(
                 inside, merged(tiles, h), jnp.float32(-1.0)
             )
@@ -466,6 +465,10 @@
     ny_total = STRIP * depth_count * y_count
     f32 = jnp.float32
 
+    stay = [
+        pltpu.with_memory_space_constraint(a, pltpu.HBM)
+        for a in (slowness, air_mask, reflector, receiver_mask, residual)
+    ]
     packed = pl.pallas_call(
         pack_kernel,
         out_shape=jax.ShapeDtypeStruct((4 * TILE, LANES), f32),
@@ -480,9 +483,9 @@
             pltpu.VMEM((2, ROWS + 8, LANES), f32),
             pltpu.SemaphoreType.DMA((5,)),
         ],
-        compiler_params=pltpu.CompilerParams(vmem_limit_bytes=PACK_VMEM),
+        compiler_params=pltpu.CompilerParams(vmem_limit_bytes=SMALL_VMEM),
         name="pack",
-    )(slowness, air_mask, reflector, receiver_mask, residual)
+    )(*stay)
 
     pairs = [
         [d * x_count + 2 * i + m for d in range(depth_count) for m in range(2)]

time: 56.1 us -> 55.2 us (0.984)
  the two profiles are of different devices: /device:TPU:66 before, /device:TPU:68 now
where the time goes in v6:
time: 55.2 us; the launch traced here: 54.9 us
  blocking collectives  20.1 us (36%)
  starting transfers between devices  12.8 us (23%)
  waiting for transfers between devices  12.5 us (23%)
  Pallas kernels  9.4 us (17%)
    all_to_all x1, blocking collectives, local(): lax.all_to_all(packed.reshape(16, 2 * HALF, LANES), ('depth', 'gx'), 0, 0...  12.3 us
    all_to_all x1, blocking collectives, local(): lax.all_to_all(strips_out.reshape(8, HALF, LANES), 'depth', 0, 0, tiled=T...  7.81 us
    pallas_call x1, Pallas kernels, sweep_call(): pl.pallas_call(kernel, out_shape=jax.ShapeDtypeStruct((TILE, LANES), jnp....  7.28 us
    ppermute x1, waiting for transfers between devices, local(): below = lax.ppermute(down, 'gx', line(x_count, -2))  7.27 us
    ppermute x1, starting transfers between devices, local(): above = lax.ppermute(up, 'gx', line(x_count, 2))  6.38 us
    ppermute x1, waiting for transfers between devices, local(): far = lax.ppermute(column, ('depth', 'gy'), swapped(1))  4.62 us
    ppermute x1, starting transfers between devices, local(): far = lax.ppermute(column, ('depth', 'gy'), swapped(1))  2.45 us
    ppermute x1, starting transfers between devices, local(): near = lax.ppermute(column, ('depth', 'gy'), swapped(0))  2.03 us
  transfers between devices with their start and end apart: 4, of which 3 were waited for; matrix products, arithmetic and copies ran while one was open for 0% of the time, Pallas kernels for 0%

profile of v6, /device:TPU:68, one launch (start us, length us, event | category | flops | bytes accessed | tf_op | source)
XLA Modules:
  0.0 54.9 jit_solution(7398250921720713223)
XLA Ops:
  0.0 1.2 %pack.1 = f32[256,128]{1,0:T(8,128)S(1)} custom-call(f32[2,16,256]{2,1,0:T(8,128)} %refs_0_.2, s32[2,16,256]{2,1,0:T(8,128)} %refs_1_.1, s32[16,256]{1,0:T(8,128)} %refs_2_.1, s32[8,16,256]{2,1,0:T(8,128)} %refs_3_.1, f32[8,16,256]{2,1,0:T(8,128)} %refs_4_.1), custom_call_target="tpu_custom_call" | custom-call | tf_op jit(solution)/shard_map/pack/pallas_call | solution.py:472
  1.2 12.3 %all_to_all.10 = f32[16,16,128]{2,1,0:T(8,128)S(1)} all-to-all(f32[16,16,128]{2,1,0:T(8,128)S(1)} %bitcast.5), channel_id=1, replica_groups={{0,4,64,68,128,132,192,196,256,260,320,324,384,388,448,452},{8,12,72,76..., dimensions={0} | all-to-all | bytes 262144 | tf_op jit(solution)/shard_map/all_to_all | solution.py:494
  13.5 0.1 stage.1
  13.7 6.4 %collective-permute-start = (f32[19,8,128]{2,1,0:T(8,128)S(1)}, f32[19,8,128]{2,1,0:T(8,128)S(1)}, u32[]{:S(2)}, u32[]{:S(2)}) collective-permute-start(f32[19,8,128]{2,1,0:T(8,128)S(1)} %get-tuple-element.8), channel_id=1, source_target_pairs={{0,8},{4,12},{8,16},{12,20},{16,24},{20,28},{24,32},{28,36},{32,40... | collective-permute-start | bytes 233480 | tf_op jit(solution)/shard_map/ppermute | solution.py:510
  20.1 1.9 %collective-permute-start.1 = (f32[19,8,128]{2,1,0:T(8,128)S(1)}, f32[19,8,128]{2,1,0:T(8,128)S(1)}, u32[]{:S(2)}, u32[]{:S(2)}) collective-permute-start(f32[19,8,128]{2,1,0:T(8,128)S(1)} %get-tuple-element.10), channel_id=1, source_target_pairs={{8,0},{12,4},{16,8},{20,12},{24,16},{28,20},{32,24},{36,28},{40,32... | collective-permute-start | bytes 233480 | tf_op jit(solution)/shard_map/ppermute | solution.py:511
  22.0 0.6 %collective-permute-done.above_ref = f32[19,8,128]{2,1,0:T(8,128)S(1)} collective-permute-done((f32[19,8,128]{2,1,0:T(8,128)S(1)}, f32[19,8,128]{2,1,0:T(8,128)S(1)}, u32[]{:S(2)}, u32[]{:S(2)}) %collective-permute-start) | collective-permute-done | bytes 77856 | tf_op jit(solution)/shard_map/ppermute | solution.py:510
  22.6 7.3 %collective-permute-done.1.below_ref = f32[19,8,128]{2,1,0:T(8,128)S(1)} collective-permute-done((f32[19,8,128]{2,1,0:T(8,128)S(1)}, f32[19,8,128]{2,1,0:T(8,128)S(1)}, u32[]{:S(2)}, u32[]{:S(2)}) %collective-permute-start.1) | collective-permute-done | bytes 77856 | tf_op jit(solution)/shard_map/ppermute | solution.py:511
  29.8 0.0 copy-start
  29.8 0.1 arrange.1.refs_2_
  29.9 2.5 %collective-permute-start.3 = (f32[408,128]{1,0:T(8,128)S(1)}, f32[408,128]{1,0:T(8,128)S(1)}, u32[]{:S(2)}, u32[]{:S(2)}) collective-permute-start(f32[408,128]{1,0:T(8,128)S(1)} %arrange.1.refs_2_), channel_id=1, source_target_pairs={{64,128},{128,64},{192,256},{256,192},{320,384},{384,320},{448,1},... | collective-permute-start | bytes 626696 | tf_op jit(solution)/shard_map/ppermute | solution.py:529
  32.4 2.0 %collective-permute-start.2 = (f32[408,128]{1,0:T(8,128)S(1)}, f32[408,128]{1,0:T(8,128)S(1)}, u32[]{:S(2)}, u32[]{:S(2)}) collective-permute-start(f32[408,128]{1,0:T(8,128)S(1)} %arrange.1.refs_2_), channel_id=1, source_target_pairs={{0,64},{64,0},{128,192},{192,128},{256,320},{320,256},{384,448},{4... | collective-permute-start | bytes 626696 | tf_op jit(solution)/shard_map/ppermute | solution.py:528
  34.4 0.0 copy-done
  34.4 0.1 copy.7.refs_0_
  34.5 4.6 %collective-permute-done.3.refs_3_ = f32[408,128]{1,0:T(8,128)S(1)} collective-permute-done((f32[408,128]{1,0:T(8,128)S(1)}, f32[408,128]{1,0:T(8,128)S(1)}, u32[]{:S(2)}, u32[]{:S(2)}) %collective-permute-start.3) | collective-permute-done | bytes 208928 | tf_op jit(solution)/shard_map/ppermute | solution.py:529
  39.1 0.0 collective-permute-done.2.refs_1_
  39.1 7.3 %sweep.1 = f32[64,128]{1,0:T(8,128)S(1)} custom-call(s32[8,2]{1,0:T(8,128)S(1)} %copy.7.refs_0_, f32[408,128]{1,0:T(8,128)S(1)} %collective-permute-done.2.refs_1_, f32[408,128]{1,0:T(8,128)S(1)} %arrange.1.refs_2_, f32[408,128]{1,0:T(8,128)S(1)} %collective-permute-done.3.refs_3_), custom_call_target="tpu_custom_call" | custom-call | tf_op jit(solution)/shard_map/sweep/pallas_call | solution.py:437
  46.4 7.8 %all_to_all.11 = f32[8,8,128]{2,1,0:T(8,128)S(1)} all-to-all(f32[8,8,128]{2,1,0:T(8,128)S(1)} %bitcast.7), channel_id=1, replica_groups=mesh['depth'=8,'gx'=16,'gy'=4] {'depth'}, dimensions={0} | all-to-all | bytes 65536 | tf_op jit(solution)/shard_map/all_to_all | solution.py:532
  54.2 0.7 %unpack.1 = f32[2,16,256]{2,1,0:T(8,128)} custom-call(f32[64,128]{1,0:T(8,128)S(1)} %bitcast.6), custom_call_target="tpu_custom_call" | custom-call | tf_op jit(solution)/shard_map/unpack/pallas_call | solution.py:535
Async XLA Ops:
  13.7 8.9 %collective-permute-start = (f32[19,8,128]{2,1,0:T(8,128)S(1)}, f32[19,8,128]{2,1,0:T(8,128)S(1)}, u32[]{:S(2)}, u32[]{:S(2)}) collective-permute-start(f32[19,8,128]{2,1,0:T(8,128)S(1)} %get-tuple-element.8), channel_id=1, source_target_pairs={{0,8},{4,12},{8,16},{12,20},{16,24},{20,28},{24,32},{28,36},{32,40... | collective-permute-start | bytes 233480 | tf_op jit(solution)/shard_map/ppermute | solution.py:510
  20.1 9.8 %collective-permute-start.1 = (f32[19,8,128]{2,1,0:T(8,128)S(1)}, f32[19,8,128]{2,1,0:T(8,128)S(1)}, u32[]{:S(2)}, u32[]{:S(2)}) collective-permute-start(f32[19,8,128]{2,1,0:T(8,128)S(1)} %get-tuple-element.10), channel_id=1, source_target_pairs={{8,0},{12,4},{16,8},{20,12},{24,16},{28,20},{32,24},{36,28},{40,32... | collective-permute-start | bytes 233480 | tf_op jit(solution)/shard_map/ppermute | solution.py:511
  29.8 4.6 %copy-start = (s32[8,2]{0,1:T(2,128)S(1)}, s32[8,2]{0,1:T(2,128)}, u32[]{:S(2)}) copy-start(s32[8,2]{0,1:T(2,128)} %param.9) | copy-start | bytes 196
  29.9 9.2 %collective-permute-start.3 = (f32[408,128]{1,0:T(8,128)S(1)}, f32[408,128]{1,0:T(8,128)S(1)}, u32[]{:S(2)}, u32[]{:S(2)}) collective-permute-start(f32[408,128]{1,0:T(8,128)S(1)} %arrange.1.refs_2_), channel_id=1, source_target_pairs={{64,128},{128,64},{192,256},{256,192},{320,384},{384,320},{448,1},... | collective-permute-start | bytes 626696 | tf_op jit(solution)/shard_map/ppermute | solution.py:529
  32.4 6.8 %collective-permute-start.2 = (f32[408,128]{1,0:T(8,128)S(1)}, f32[408,128]{1,0:T(8,128)S(1)}, u32[]{:S(2)}, u32[]{:S(2)}) collective-permute-start(f32[408,128]{1,0:T(8,128)S(1)} %arrange.1.refs_2_), channel_id=1, source_target_pairs={{0,64},{64,0},{128,192},{192,128},{256,320},{320,256},{384,448},{4... | collective-permute-start | bytes 626696 | tf_op jit(solution)/shard_map/ppermute | solution.py:528

commit v7 on v6

--- a/solution.py
+++ b/solution.py
@@ -180,8 +180,48 @@
             out_ref[at, :] = picked(sources, offset, part)
 
 
+def frame_of(nx_total, ny_total):
+    x_base = position("gx") * ROWS - 2 * ROWS
+    y_base = position("gy") * (8 * STRIP) + position("depth") * STRIP - STRIP
+    y_cell = y_base + lane_index()
+    y_inside = (y_cell >= 0) & (y_cell < ny_total)
+
+    def penalty(x_cell):
+        inside = (x_cell >= 0) & (x_cell < nx_total) & y_inside
+        return jnp.where(inside, jnp.float32(0.0), jnp.float32(STEP_PENALTY))
+
+    return x_base, y_cell, penalty
+
+
+def start_kernel(shot_ref, start_ref, weight_ref, nx_total, ny_total):
+    x_base, y_cell, penalty = frame_of(nx_total, ny_total)
+    zero = jnp.zeros((8, LANES), jnp.float32)
+    shot_x = jnp.broadcast_to(shot_ref[:, 0:1].astype(jnp.float32), (8, LANES))
+    shot_y = jnp.broadcast_to(shot_ref[:, 1:2].astype(jnp.float32), (8, LANES))
+    y_square = (y_cell.astype(jnp.float32) - shot_y) ** 2
+
+    def surface(r):
+        x_cell = (x_base + r).astype(jnp.float32)
+        return SURF * jnp.sqrt((x_cell - shot_x) ** 2 + y_square)
+
+    def weight(diff):
+        return jnp.exp2(diff * RATE)
+
+    def near(diff):
+        return jnp.clip(diff, -1.0, 1.0)
+
+    middle = surface(MIDDLE)
+    weight_ref[0] = weight(near(pltpu.roll(middle, 1, 1) - middle))
+    weight_ref[1] = weight(near(pltpu.roll(middle, LANES - 1, 1) - middle))
+    for r in range(FRAME):
+        start_ref[r + PAD] = weight((surface(r) - middle) + penalty(x_base + r))
+    start_ref[PAD - 1] = zero
+    start_ref[PAD + FRAME] = zero
+
+
 def sweep_kernel(
-    shot_ref,
+    start_ref,
+    weight_ref,
     near_ref,
     here_ref,
     far_ref,
@@ -206,42 +246,16 @@
 ):
     lane = lane_index()
     sub = lax.broadcasted_iota(jnp.int32, (8, LANES), 0)
-    depth_pos = position("depth")
-    x_base = position("gx") * ROWS - 2 * ROWS
-    y_base = position("gy") * (8 * STRIP) + depth_pos * STRIP - STRIP
-    odd = depth_pos % 2 == 1
-    y_cell = y_base + lane
-    y_inside = (y_cell >= 0) & (y_cell < ny_total)
+    odd = position("depth") % 2 == 1
     zero = jnp.zeros((8, LANES), jnp.float32)
+    x_base, _, penalty = frame_of(nx_total, ny_total)
 
     def row_of(ref, lead, r):
         if lead is None:
             return ref[pl.ds(r, 8, stride=0), :]
         return ref[lead, pl.ds(r, 8, stride=0), :]
 
-    def penalty(x_cell):
-        inside = (x_cell >= 0) & (x_cell < nx_total) & y_inside
-        return jnp.where(inside, jnp.float32(0.0), jnp.float32(STEP_PENALTY))
-
-    shot_x = jnp.broadcast_to(shot_ref[:, 0:1].astype(jnp.float32), (8, LANES))
-    shot_y = jnp.broadcast_to(shot_ref[:, 1:2].astype(jnp.float32), (8, LANES))
-    y_square = (y_cell.astype(jnp.float32) - shot_y) ** 2
-
-    def surface(r):
-        x_cell = (x_base + r).astype(jnp.float32)
-        return SURF * jnp.sqrt((x_cell - shot_x) ** 2 + y_square)
-
-    def weight(diff):
-        return jnp.exp2(diff * RATE)
-
-    def near(diff):
-        return jnp.clip(diff, -1.0, 1.0)
-
-    middle = surface(MIDDLE)
-    weight_minus = weight(near(pltpu.roll(middle, 1, 1) - middle))
-    weight_plus = weight(near(pltpu.roll(middle, LANES - 1, 1) - middle))
-    for r in range(FRAME):
-        wa_ref[r + PAD] = weight((surface(r) - middle) + penalty(x_base + r))
+    weight_minus, weight_plus = weight_ref[0], weight_ref[1]
     for ref in (wa_ref, wb_ref):
         ref[PAD - 1] = zero
         ref[PAD + FRAME] = zero
@@ -330,7 +344,10 @@
 
         return two
 
-    lax.fori_loop(0, 2, down(1, 79, False), 0)
+    down_plane(jnp.int32(0), start_ref, wb_ref, 1, 79, False)
+    down_plane(jnp.int32(1), wb_ref, wa_ref, 2, 78, False)
+    down_plane(jnp.int32(2), wa_ref, wb_ref, 3, 77, False)
+    down_plane(jnp.int32(3), wb_ref, wa_ref, 4, 76, False)
     lax.fori_loop(2, 4, down(5, 75, True), 0)
     lax.fori_loop(4, 6, down(9, 71, True), 0)
     lax.fori_loop(6, 8, down(13, 67, True), 0)
@@ -429,7 +446,7 @@
     return [(i, i + shift) for i in range(count) if 0 <= i + shift < count]
 
 
-def sweep_call(shot_cells, near, column, far, nx_total, ny_total):
+def sweep_call(start, weights, near, column, far, nx_total, ny_total):
     def kernel(*refs):
         sweep_kernel(*refs, nx_total=nx_total, ny_total=ny_total)
 
@@ -437,7 +454,7 @@
     return pl.pallas_call(
         kernel,
         out_shape=jax.ShapeDtypeStruct((TILE, LANES), jnp.float32),
-        in_specs=in_vmem(4),
+        in_specs=in_vmem(5),
         out_specs=in_vmem(1)[0],
         scratch_shapes=[
             *[pltpu.VMEM(field, jnp.float32)] * 2,
@@ -454,7 +471,7 @@
         ],
         compiler_params=pltpu.CompilerParams(vmem_limit_bytes=SWEEP_VMEM),
         name="sweep",
-    )(shot_cells, near, column, far)
+    )(start, weights, near, column, far)
 
 
 def local(slowness, air_mask, reflector, shot_cells, receiver_mask, residual):
@@ -518,6 +535,26 @@
         name="arrange",
     )(above, own, below)
 
+    shots, column = lax.optimization_barrier((shot_cells, column))
+
+    def start_body(*refs):
+        start_kernel(*refs, nx_total=nx_total, ny_total=ny_total)
+
+    start, weights = pl.pallas_call(
+        start_body,
+        out_shape=(
+            jax.ShapeDtypeStruct((FULL, SHOTS, LANES), f32),
+            jax.ShapeDtypeStruct((2, SHOTS, LANES), f32),
+        ),
+        in_specs=in_vmem(1),
+        out_specs=tuple(in_vmem(2)),
+        compiler_params=pltpu.CompilerParams(vmem_limit_bytes=SMALL_VMEM),
+        cost_estimate=pl.CostEstimate(
+            flops=20 * FRAME * 1024, bytes_accessed=4 * FULL * 1024, transcendentals=FRAME * 2048
+        ),
+        name="start",
+    )(shots)
+
     def place(q):
         return (q % depth_count) * y_count + q // depth_count
 
@@ -528,7 +565,7 @@
     near = lax.ppermute(column, ("depth", "gy"), swapped(0))
     far = lax.ppermute(column, ("depth", "gy"), swapped(1))
 
-    strips_out = sweep_call(shot_cells, near, column, far, nx_total, ny_total)
+    strips_out = sweep_call(start, weights, near, column, far, nx_total, ny_total)
     parts = lax.all_to_all(
         strips_out.reshape(8, HALF, LANES), "depth", 0, 0, tiled=True
     ).reshape(TILE, LANES)

time: 55.2 us -> 55.6 us (level)
  Pallas kernels: 9.4 us -> 10.1 us
  transfers between devices with their start and end apart: 4 -> 4, of which waited for: 3 -> 3; matrix products, arithmetic and copies ran while one was open for 0% -> 0% of each run, Pallas kernels for 0% -> 1%
where the time goes in v7:
time: 55.6 us; the launch traced here: 55.3 us
  blocking collectives  20.1 us (36%)
  starting transfers between devices  12.8 us (23%)
  waiting for transfers between devices  12.2 us (22%)
  Pallas kernels  10.1 us (18%)
    all_to_all x1, blocking collectives, local(): lax.all_to_all(packed.reshape(16, 2 * HALF, LANES), ('depth', 'gx'), 0, 0...  12.3 us
    all_to_all x1, blocking collectives, local(): lax.all_to_all(strips_out.reshape(8, HALF, LANES), 'depth', 0, 0, tiled=T...  7.81 us
    pallas_call x1, Pallas kernels, sweep_call(): pl.pallas_call(kernel, out_shape=jax.ShapeDtypeStruct((TILE, LANES), jnp....  7.69 us
    ppermute x1, waiting for transfers between devices, local(): below = lax.ppermute(down, 'gx', line(x_count, -2))  7.27 us
    ppermute x1, starting transfers between devices, local(): above = lax.ppermute(up, 'gx', line(x_count, 2))  6.38 us
    ppermute x1, waiting for transfers between devices, local(): far = lax.ppermute(column, ('depth', 'gy'), swapped(1))  4.34 us
    ppermute x1, starting transfers between devices, local(): far = lax.ppermute(column, ('depth', 'gy'), swapped(1))  2.45 us
    ppermute x1, starting transfers between devices, local(): near = lax.ppermute(column, ('depth', 'gy'), swapped(0))  2.03 us
  transfers between devices with their start and end apart: 4, of which 3 were waited for; matrix products, arithmetic and copies ran while one was open for 0% of the time, Pallas kernels for 1%

profile of v7, /device:TPU:68, one launch (start us, length us, event | category | flops | bytes accessed | tf_op | source)
XLA Modules:
  0.0 55.3 jit_solution(7407972618743723295)
XLA Ops:
  0.0 1.2 %pack.1 = f32[256,128]{1,0:T(8,128)S(1)} custom-call(f32[2,16,256]{2,1,0:T(8,128)} %refs_0_.1, s32[2,16,256]{2,1,0:T(8,128)} %refs_1_.1, s32[16,256]{1,0:T(8,128)} %refs_2_.1, s32[8,16,256]{2,1,0:T(8,128)} %refs_3_.1, f32[8,16,256]{2,1,0:T(8,128)} %refs_4_.1), custom_call_target="tpu_custom_call" | custom-call | tf_op jit(solution)/shard_map/pack/pallas_call | solution.py:489
  1.2 12.3 %all_to_all.10 = f32[16,16,128]{2,1,0:T(8,128)S(1)} all-to-all(f32[16,16,128]{2,1,0:T(8,128)S(1)} %bitcast.5), channel_id=1, replica_groups={{0,4,64,68,128,132,192,196,256,260,320,324,384,388,448,452},{8,12,72,76..., dimensions={0} | all-to-all | bytes 262144 | tf_op jit(solution)/shard_map/all_to_all | solution.py:511
  13.5 0.1 stage.1
  13.7 6.4 %collective-permute-start = (f32[19,8,128]{2,1,0:T(8,128)S(1)}, f32[19,8,128]{2,1,0:T(8,128)S(1)}, u32[]{:S(2)}, u32[]{:S(2)}) collective-permute-start(f32[19,8,128]{2,1,0:T(8,128)S(1)} %get-tuple-element.12), channel_id=1, source_target_pairs={{0,8},{4,12},{8,16},{12,20},{16,24},{20,28},{24,32},{28,36},{32,40... | collective-permute-start | bytes 233480 | tf_op jit(solution)/shard_map/ppermute | solution.py:527
  20.1 1.9 %collective-permute-start.1 = (f32[19,8,128]{2,1,0:T(8,128)S(1)}, f32[19,8,128]{2,1,0:T(8,128)S(1)}, u32[]{:S(2)}, u32[]{:S(2)}) collective-permute-start(f32[19,8,128]{2,1,0:T(8,128)S(1)} %get-tuple-element.14), channel_id=1, source_target_pairs={{8,0},{12,4},{16,8},{20,12},{24,16},{28,20},{32,24},{36,28},{40,32... | collective-permute-start | bytes 233480 | tf_op jit(solution)/shard_map/ppermute | solution.py:528
  22.0 0.6 %collective-permute-done.above_ref = f32[19,8,128]{2,1,0:T(8,128)S(1)} collective-permute-done((f32[19,8,128]{2,1,0:T(8,128)S(1)}, f32[19,8,128]{2,1,0:T(8,128)S(1)}, u32[]{:S(2)}, u32[]{:S(2)}) %collective-permute-start) | collective-permute-done | bytes 77856 | tf_op jit(solution)/shard_map/ppermute | solution.py:527
  22.6 7.3 %collective-permute-done.1.below_ref = f32[19,8,128]{2,1,0:T(8,128)S(1)} collective-permute-done((f32[19,8,128]{2,1,0:T(8,128)S(1)}, f32[19,8,128]{2,1,0:T(8,128)S(1)}, u32[]{:S(2)}, u32[]{:S(2)}) %collective-permute-start.1) | collective-permute-done | bytes 77856 | tf_op jit(solution)/shard_map/ppermute | solution.py:528
  29.8 0.0 copy-start
  29.8 0.1 arrange.1.refs_3_
  29.9 2.5 %collective-permute-start.3 = (f32[408,128]{1,0:T(8,128)S(1)}, f32[408,128]{1,0:T(8,128)S(1)}, u32[]{:S(2)}, u32[]{:S(2)}) collective-permute-start(f32[408,128]{1,0:T(8,128)S(1)} %arrange.1.refs_3_), channel_id=1, source_target_pairs={{64,128},{128,64},{192,256},{256,192},{320,384},{384,320},{448,1},... | collective-permute-start | bytes 626696 | tf_op jit(solution)/shard_map/ppermute | solution.py:566
  32.4 2.0 %collective-permute-start.2 = (f32[408,128]{1,0:T(8,128)S(1)}, f32[408,128]{1,0:T(8,128)S(1)}, u32[]{:S(2)}, u32[]{:S(2)}) collective-permute-start(f32[408,128]{1,0:T(8,128)S(1)} %arrange.1.refs_3_), channel_id=1, source_target_pairs={{0,64},{64,0},{128,192},{192,128},{256,320},{320,256},{384,448},{4... | collective-permute-start | bytes 626696 | tf_op jit(solution)/shard_map/ppermute | solution.py:565
  34.4 0.0 copy-done
  34.4 0.1 copy.7.refs_0_
  34.5 0.3 start.1
  34.8 4.3 %collective-permute-done.3.refs_4_ = f32[408,128]{1,0:T(8,128)S(1)} collective-permute-done((f32[408,128]{1,0:T(8,128)S(1)}, f32[408,128]{1,0:T(8,128)S(1)}, u32[]{:S(2)}, u32[]{:S(2)}) %collective-permute-start.3) | collective-permute-done | bytes 208928 | tf_op jit(solution)/shard_map/ppermute | solution.py:566
  39.1 0.0 collective-permute-done.2.refs_2_
  39.1 7.7 %sweep.1 = f32[64,128]{1,0:T(8,128)S(1)} custom-call(f32[96,8,128]{2,1,0:T(8,128)S(1)} %get-tuple-element.16.refs_0_, f32[2,8,128]{2,1,0:T(8,128)S(1)} %get-tuple-element.17.refs_1_, f32[408,128]{1,0:T(8,128)S(1)} %collective-permute-done.2.refs_2_, f32[408,128]{1,0:T(8,128)S(1)} %arrange.1.refs_3_, f32[408,128]{1,0:T(8,128)S(1)} %collective-permute-done.3.refs_4_), custom_call_target="tpu_custom_call" | custom-call | tf_op jit(solution)/shard_map/sweep/pallas_call | solution.py:454
  46.8 7.8 %all_to_all.11 = f32[8,8,128]{2,1,0:T(8,128)S(1)} all-to-all(f32[8,8,128]{2,1,0:T(8,128)S(1)} %bitcast.6), channel_id=1, replica_groups=mesh['depth'=8,'gx'=16,'gy'=4] {'depth'}, dimensions={0} | all-to-all | bytes 65536 | tf_op jit(solution)/shard_map/all_to_all | solution.py:569
  54.6 0.7 %unpack.1 = f32[2,16,256]{2,1,0:T(8,128)} custom-call(f32[64,128]{1,0:T(8,128)S(1)} %bitcast.7), custom_call_target="tpu_custom_call" | custom-call | tf_op jit(solution)/shard_map/unpack/pallas_call | solution.py:572
Async XLA Ops:
  13.7 8.9 %collective-permute-start = (f32[19,8,128]{2,1,0:T(8,128)S(1)}, f32[19,8,128]{2,1,0:T(8,128)S(1)}, u32[]{:S(2)}, u32[]{:S(2)}) collective-permute-start(f32[19,8,128]{2,1,0:T(8,128)S(1)} %get-tuple-element.12), channel_id=1, source_target_pairs={{0,8},{4,12},{8,16},{12,20},{16,24},{20,28},{24,32},{28,36},{32,40... | collective-permute-start | bytes 233480 | tf_op jit(solution)/shard_map/ppermute | solution.py:527
  20.1 9.8 %collective-permute-start.1 = (f32[19,8,128]{2,1,0:T(8,128)S(1)}, f32[19,8,128]{2,1,0:T(8,128)S(1)}, u32[]{:S(2)}, u32[]{:S(2)}) collective-permute-start(f32[19,8,128]{2,1,0:T(8,128)S(1)} %get-tuple-element.14), channel_id=1, source_target_pairs={{8,0},{12,4},{16,8},{20,12},{24,16},{28,20},{32,24},{36,28},{40,32... | collective-permute-start | bytes 233480 | tf_op jit(solution)/shard_map/ppermute | solution.py:528
  29.8 4.6 %copy-start = (s32[8,2]{0,1:T(2,128)S(1)}, s32[8,2]{0,1:T(2,128)}, u32[]{:S(2)}) copy-start(s32[8,2]{0,1:T(2,128)} %param.9) | copy-start | bytes 196
  29.9 9.2 %collective-permute-start.3 = (f32[408,128]{1,0:T(8,128)S(1)}, f32[408,128]{1,0:T(8,128)S(1)}, u32[]{:S(2)}, u32[]{:S(2)}) collective-permute-start(f32[408,128]{1,0:T(8,128)S(1)} %arrange.1.refs_3_), channel_id=1, source_target_pairs={{64,128},{128,64},{192,256},{256,192},{320,384},{384,320},{448,1},... | collective-permute-start | bytes 626696 | tf_op jit(solution)/shard_map/ppermute | solution.py:566
  32.4 6.8 %collective-permute-start.2 = (f32[408,128]{1,0:T(8,128)S(1)}, f32[408,128]{1,0:T(8,128)S(1)}, u32[]{:S(2)}, u32[]{:S(2)}) collective-permute-start(f32[408,128]{1,0:T(8,128)S(1)} %arrange.1.refs_3_), channel_id=1, source_target_pairs={{0,64},{64,0},{128,192},{192,128},{256,320},{320,256},{384,448},{4... | collective-permute-start | bytes 626696 | tf_op jit(solution)/shard_map/ppermute | solution.py:565

commit v8 on v7

--- a/solution.py
+++ b/solution.py
@@ -1,3 +1,4 @@
+import functools
 import math
 
 import jax
@@ -260,6 +261,13 @@
         ref[PAD - 1] = zero
         ref[PAD + FRAME] = zero
 
+    def copy_start(b, carry):
+        for i in range(16):
+            wa_ref[PAD + b * 16 + i] = start_ref[PAD + b * 16 + i]
+        return carry
+
+    lax.fori_loop(0, FRAME // 16, copy_start, 0)
+
     def merged(tiles, j):
         part = tiles[0]
         one, two = (j + 1) % 4, (j + 2) % 4
@@ -276,26 +284,31 @@
 
     rims = [penalty(x_base + HALF * g + sub) for g in range(FRAME // HALF)]
 
-    for pair in range(PLANES // 2):
-        for offset in range(5):
-            if pair >= 4 and offset in (0, 4):
-                tiles = strips(SHARED_AT + HALF * (pair - 4))
-            else:
-                tiles = strips(A_AT[offset] + HALF * pair)
-            for j in range(4):
-                p, h = divmod(j, 2)
-                group = 2 * offset + h
-                if pair >= 4 and group in (0, 9):
-                    continue
-                speed = merged(tiles, j)
-                at = (2 * pair + p, pl.ds(HALF * group, HALF), slice(None))
-                slow = speed + rims[group]
-                e1_ref[at] = jnp.exp2(slow * RATE)
-                e2_ref[at] = jnp.exp2(slow * (ROOT2 * RATE))
-                e3_ref[at] = jnp.exp2(slow * (ROOT3 * RATE))
-                if 3 <= group < 7:
-                    here = (2 * pair + p, pl.ds(HALF * (group - 3), HALF), slice(None))
-                    earth_ref[here] = speed
+    def exponents(first, step, carry):
+        for i in range(2):
+            pair = first + 2 * step + i
+            for offset in range(5):
+                if first and offset in (0, 4):
+                    tiles = strips(pl.multiple_of(SHARED_AT + HALF * (pair - 4), HALF))
+                else:
+                    tiles = strips(pl.multiple_of(A_AT[offset] + HALF * pair, HALF))
+                for j in range(4):
+                    p, h = divmod(j, 2)
+                    group = 2 * offset + h
+                    if first and group in (0, 9):
+                        continue
+                    slow = merged(tiles, j) + rims[group]
+                    at = (2 * pair + p, pl.ds(HALF * group, HALF), slice(None))
+                    e1_ref[at] = jnp.exp2(slow * RATE)
+                    e2_ref[at] = jnp.exp2(slow * (ROOT2 * RATE))
+                    e3_ref[at] = jnp.exp2(slow * (ROOT3 * RATE))
+                    if 3 <= group < 7:
+                        here = (2 * pair + p, pl.ds(HALF * (group - 3), HALF), slice(None))
+                        earth_ref[here] = slow
+        return carry
+
+    for first in (0, 4):
+        lax.fori_loop(0, 2, functools.partial(exponents, first), 0)
 
     for offset in range(3):
         for v in range(4):
@@ -344,13 +357,8 @@
 
         return two
 
-    down_plane(jnp.int32(0), start_ref, wb_ref, 1, 79, False)
-    down_plane(jnp.int32(1), wb_ref, wa_ref, 2, 78, False)
-    down_plane(jnp.int32(2), wa_ref, wb_ref, 3, 77, False)
-    down_plane(jnp.int32(3), wb_ref, wa_ref, 4, 76, False)
-    lax.fori_loop(2, 4, down(5, 75, True), 0)
-    lax.fori_loop(4, 6, down(9, 71, True), 0)
-    lax.fori_loop(6, 8, down(13, 67, True), 0)
+    lax.fori_loop(0, 4, down(1, 79, True), 0)
+    lax.fori_loop(4, 8, down(9, 71, True), 0)
 
     for ref in (ma_ref, mb_ref):
         ref[15 + PAD] = zero

time: 55.6 us -> 54 us (0.971)
  Pallas kernels: 10.1 us -> 8.48 us
    pallas_call x1, Pallas kernels: 7.69 us -> 6.08 us  [sweep_call(): pl.pallas_call(kernel, out_shape=jax.ShapeDtypeStruct((TILE, LANES), jnp....]
where the time goes in v8:
time: 54 us; the launch traced here: 53.7 us
  blocking collectives  20.1 us (37%)
  starting transfers between devices  12.8 us (24%)
  waiting for transfers between devices  12.2 us (23%)
  Pallas kernels  8.48 us (16%)
    all_to_all x1, blocking collectives, local(): lax.all_to_all(packed.reshape(16, 2 * HALF, LANES), ('depth', 'gx'), 0, 0...  12.3 us
    all_to_all x1, blocking collectives, local(): lax.all_to_all(strips_out.reshape(8, HALF, LANES), 'depth', 0, 0, tiled=T...  7.81 us
    ppermute x1, waiting for transfers between devices, local(): below = lax.ppermute(down, 'gx', line(x_count, -2))  7.27 us
    ppermute x1, starting transfers between devices, local(): above = lax.ppermute(up, 'gx', line(x_count, 2))  6.38 us
    pallas_call x1, Pallas kernels, sweep_call(): pl.pallas_call(kernel, out_shape=jax.ShapeDtypeStruct((TILE, LANES), jnp....  6.08 us
    ppermute x1, waiting for transfers between devices, local(): far = lax.ppermute(column, ('depth', 'gy'), swapped(1))  4.34 us
    ppermute x1, starting transfers between devices, local(): far = lax.ppermute(column, ('depth', 'gy'), swapped(1))  2.45 us
    ppermute x1, starting transfers between devices, local(): near = lax.ppermute(column, ('depth', 'gy'), swapped(0))  2.03 us
  transfers between devices with their start and end apart: 4, of which 3 were waited for; matrix products, arithmetic and copies ran while one was open for 0% of the time, Pallas kernels for 1%

profile of v8, /device:TPU:68, one launch (start us, length us, event | category | flops | bytes accessed | tf_op | source)
XLA Modules:
  0.0 53.7 jit_solution(13357314000897934127)
XLA Ops:
  0.0 1.2 %pack.1 = f32[256,128]{1,0:T(8,128)S(1)} custom-call(f32[2,16,256]{2,1,0:T(8,128)} %refs_0_.1, s32[2,16,256]{2,1,0:T(8,128)} %refs_1_.1, s32[16,256]{1,0:T(8,128)} %refs_2_.1, s32[8,16,256]{2,1,0:T(8,128)} %refs_3_.1, f32[8,16,256]{2,1,0:T(8,128)} %refs_4_.1), custom_call_target="tpu_custom_call" | custom-call | tf_op jit(solution)/shard_map/pack/pallas_call | solution.py:497
  1.2 12.3 %all_to_all.10 = f32[16,16,128]{2,1,0:T(8,128)S(1)} all-to-all(f32[16,16,128]{2,1,0:T(8,128)S(1)} %bitcast.5), channel_id=1, replica_groups={{0,4,64,68,128,132,192,196,256,260,320,324,384,388,448,452},{8,12,72,76..., dimensions={0} | all-to-all | bytes 262144 | tf_op jit(solution)/shard_map/all_to_all | solution.py:519
  13.5 0.1 stage.1
  13.7 6.4 %collective-permute-start = (f32[19,8,128]{2,1,0:T(8,128)S(1)}, f32[19,8,128]{2,1,0:T(8,128)S(1)}, u32[]{:S(2)}, u32[]{:S(2)}) collective-permute-start(f32[19,8,128]{2,1,0:T(8,128)S(1)} %get-tuple-element.12), channel_id=1, source_target_pairs={{0,8},{4,12},{8,16},{12,20},{16,24},{20,28},{24,32},{28,36},{32,40... | collective-permute-start | bytes 233480 | tf_op jit(solution)/shard_map/ppermute | solution.py:535
  20.1 1.9 %collective-permute-start.1 = (f32[19,8,128]{2,1,0:T(8,128)S(1)}, f32[19,8,128]{2,1,0:T(8,128)S(1)}, u32[]{:S(2)}, u32[]{:S(2)}) collective-permute-start(f32[19,8,128]{2,1,0:T(8,128)S(1)} %get-tuple-element.14), channel_id=1, source_target_pairs={{8,0},{12,4},{16,8},{20,12},{24,16},{28,20},{32,24},{36,28},{40,32... | collective-permute-start | bytes 233480 | tf_op jit(solution)/shard_map/ppermute | solution.py:536
  22.0 0.6 %collective-permute-done.above_ref = f32[19,8,128]{2,1,0:T(8,128)S(1)} collective-permute-done((f32[19,8,128]{2,1,0:T(8,128)S(1)}, f32[19,8,128]{2,1,0:T(8,128)S(1)}, u32[]{:S(2)}, u32[]{:S(2)}) %collective-permute-start) | collective-permute-done | bytes 77856 | tf_op jit(solution)/shard_map/ppermute | solution.py:535
  22.6 7.3 %collective-permute-done.1.below_ref = f32[19,8,128]{2,1,0:T(8,128)S(1)} collective-permute-done((f32[19,8,128]{2,1,0:T(8,128)S(1)}, f32[19,8,128]{2,1,0:T(8,128)S(1)}, u32[]{:S(2)}, u32[]{:S(2)}) %collective-permute-start.1) | collective-permute-done | bytes 77856 | tf_op jit(solution)/shard_map/ppermute | solution.py:536
  29.8 0.0 copy-start
  29.8 0.1 arrange.1.refs_3_
  29.9 2.5 %collective-permute-start.3 = (f32[408,128]{1,0:T(8,128)S(1)}, f32[408,128]{1,0:T(8,128)S(1)}, u32[]{:S(2)}, u32[]{:S(2)}) collective-permute-start(f32[408,128]{1,0:T(8,128)S(1)} %arrange.1.refs_3_), channel_id=1, source_target_pairs={{64,128},{128,64},{192,256},{256,192},{320,384},{384,320},{448,1},... | collective-permute-start | bytes 626696 | tf_op jit(solution)/shard_map/ppermute | solution.py:574
  32.4 2.0 %collective-permute-start.2 = (f32[408,128]{1,0:T(8,128)S(1)}, f32[408,128]{1,0:T(8,128)S(1)}, u32[]{:S(2)}, u32[]{:S(2)}) collective-permute-start(f32[408,128]{1,0:T(8,128)S(1)} %arrange.1.refs_3_), channel_id=1, source_target_pairs={{0,64},{64,0},{128,192},{192,128},{256,320},{320,256},{384,448},{4... | collective-permute-start | bytes 626696 | tf_op jit(solution)/shard_map/ppermute | solution.py:573
  34.4 0.0 copy-done
  34.4 0.1 copy.7.refs_0_
  34.5 0.3 start.1
  34.8 4.3 %collective-permute-done.3.refs_4_ = f32[408,128]{1,0:T(8,128)S(1)} collective-permute-done((f32[408,128]{1,0:T(8,128)S(1)}, f32[408,128]{1,0:T(8,128)S(1)}, u32[]{:S(2)}, u32[]{:S(2)}) %collective-permute-start.3) | collective-permute-done | bytes 208928 | tf_op jit(solution)/shard_map/ppermute | solution.py:574
  39.1 0.0 collective-permute-done.2.refs_2_
  39.1 6.1 %sweep.1 = f32[64,128]{1,0:T(8,128)S(1)} custom-call(f32[96,8,128]{2,1,0:T(8,128)S(1)} %get-tuple-element.16.refs_0_, f32[2,8,128]{2,1,0:T(8,128)S(1)} %get-tuple-element.17.refs_1_, f32[408,128]{1,0:T(8,128)S(1)} %collective-permute-done.2.refs_2_, f32[408,128]{1,0:T(8,128)S(1)} %arrange.1.refs_3_, f32[408,128]{1,0:T(8,128)S(1)} %collective-permute-done.3.refs_4_), custom_call_target="tpu_custom_call" | custom-call | tf_op jit(solution)/shard_map/sweep/pallas_call | solution.py:462
  45.2 7.8 %all_to_all.11 = f32[8,8,128]{2,1,0:T(8,128)S(1)} all-to-all(f32[8,8,128]{2,1,0:T(8,128)S(1)} %bitcast.6), channel_id=1, replica_groups=mesh['depth'=8,'gx'=16,'gy'=4] {'depth'}, dimensions={0} | all-to-all | bytes 65536 | tf_op jit(solution)/shard_map/all_to_all | solution.py:577
  53.0 0.7 %unpack.1 = f32[2,16,256]{2,1,0:T(8,128)} custom-call(f32[64,128]{1,0:T(8,128)S(1)} %bitcast.7), custom_call_target="tpu_custom_call" | custom-call | tf_op jit(solution)/shard_map/unpack/pallas_call | solution.py:580
Async XLA Ops:
  13.7 8.9 %collective-permute-start = (f32[19,8,128]{2,1,0:T(8,128)S(1)}, f32[19,8,128]{2,1,0:T(8,128)S(1)}, u32[]{:S(2)}, u32[]{:S(2)}) collective-permute-start(f32[19,8,128]{2,1,0:T(8,128)S(1)} %get-tuple-element.12), channel_id=1, source_target_pairs={{0,8},{4,12},{8,16},{12,20},{16,24},{20,28},{24,32},{28,36},{32,40... | collective-permute-start | bytes 233480 | tf_op jit(solution)/shard_map/ppermute | solution.py:535
  20.1 9.8 %collective-permute-start.1 = (f32[19,8,128]{2,1,0:T(8,128)S(1)}, f32[19,8,128]{2,1,0:T(8,128)S(1)}, u32[]{:S(2)}, u32[]{:S(2)}) collective-permute-start(f32[19,8,128]{2,1,0:T(8,128)S(1)} %get-tuple-element.14), channel_id=1, source_target_pairs={{8,0},{12,4},{16,8},{20,12},{24,16},{28,20},{32,24},{36,28},{40,32... | collective-permute-start | bytes 233480 | tf_op jit(solution)/shard_map/ppermute | solution.py:536
  29.8 4.6 %copy-start = (s32[8,2]{0,1:T(2,128)S(1)}, s32[8,2]{0,1:T(2,128)}, u32[]{:S(2)}) copy-start(s32[8,2]{0,1:T(2,128)} %param.9) | copy-start | bytes 196
  29.9 9.2 %collective-permute-start.3 = (f32[408,128]{1,0:T(8,128)S(1)}, f32[408,128]{1,0:T(8,128)S(1)}, u32[]{:S(2)}, u32[]{:S(2)}) collective-permute-start(f32[408,128]{1,0:T(8,128)S(1)} %arrange.1.refs_3_), channel_id=1, source_target_pairs={{64,128},{128,64},{192,256},{256,192},{320,384},{384,320},{448,1},... | collective-permute-start | bytes 626696 | tf_op jit(solution)/shard_map/ppermute | solution.py:574
  32.4 6.8 %collective-permute-start.2 = (f32[408,128]{1,0:T(8,128)S(1)}, f32[408,128]{1,0:T(8,128)S(1)}, u32[]{:S(2)}, u32[]{:S(2)}) collective-permute-start(f32[408,128]{1,0:T(8,128)S(1)} %arrange.1.refs_3_), channel_id=1, source_target_pairs={{0,64},{64,0},{128,192},{192,128},{256,320},{320,256},{384,448},{4... | collective-permute-start | bytes 626696 | tf_op jit(solution)/shard_map/ppermute | solution.py:573

commit v9 on v8

--- a/solution.py
+++ b/solution.py
@@ -58,7 +58,9 @@
 
 def pack_kernel(*refs):
     out_ref, live_ref, level_ref, sems = refs[5], refs[11], refs[12], refs[13]
-    copies = [pltpu.make_async_copy(refs[i], refs[6 + i], sems.at[i]) for i in range(5)]
+    half = pl.ds(pl.multiple_of(HALF * (position("depth") // 4), HALF), HALF)
+    parts = [refs[0], refs[1], refs[2].at[half], refs[3].at[:, half], refs[4].at[:, half]]
+    copies = [pltpu.make_async_copy(parts[i], refs[6 + i], sems.at[i]) for i in range(5)]
     for copy in copies:
         copy.start()
     for copy in copies:
@@ -66,22 +68,21 @@
     slow_ref, air_ref, refl_ref, mask_ref, resid_ref = refs[6:11]
     lane = lane_index()
     sub = lax.broadcasted_iota(jnp.int32, (8, LANES), 0)
-    first = 2 * position("depth")
+    first = 2 * (position("depth") % 4)
     speed = {}
     for p in range(2):
         for h in range(2):
             for c in range(2):
                 at = (p, pl.ds(HALF * h, HALF), pl.ds(LANES * c, LANES))
                 speed[p, h, c] = jnp.where(air_ref[at] == 1, jnp.float32(AIR_SLOW), slow_ref[at])
-    for h in range(2):
-        for c in range(2):
-            here = pl.ds(HALF * h, HALF)
-            at = (here, pl.ds(LANES * c, LANES))
-            level_ref[c, here, :] = refl_ref[at].astype(jnp.float32)
-            for shot in range(SHOTS):
-                live_ref[c, shot, here, :] = jnp.where(
-                    mask_ref[shot, *at] == 1, resid_ref[shot, *at], jnp.float32(0.0)
-                )
+    for c in range(2):
+        here = pl.ds(0, HALF)
+        at = (slice(None), pl.ds(LANES * c, LANES))
+        level_ref[c, here, :] = refl_ref[at].astype(jnp.float32)
+        for shot in range(SHOTS):
+            live_ref[c, shot, here, :] = jnp.where(
+                mask_ref[shot, *at] == 1, resid_ref[shot, *at], jnp.float32(0.0)
+            )
     rows = {}
     for i in range(2):
         for c in range(2):
@@ -501,11 +502,17 @@
         out_specs=in_vmem(1)[0],
         scratch_shapes=[
             *[
-                pltpu.VMEM(arg.shape, arg.dtype)
-                for arg in (slowness, air_mask, reflector, receiver_mask, residual)
+                pltpu.VMEM((*arg.shape[:-2], rows, arg.shape[-1]), arg.dtype)
+                for arg, rows in (
+                    (slowness, ROWS),
+                    (air_mask, ROWS),
+                    (reflector, HALF),
+                    (receiver_mask, HALF),
+                    (residual, HALF),
+                )
             ],
-            pltpu.VMEM((2, SHOTS, ROWS + 8, LANES), f32),
-            pltpu.VMEM((2, ROWS + 8, LANES), f32),
+            pltpu.VMEM((2, SHOTS, HALF + 8, LANES), f32),
+            pltpu.VMEM((2, HALF + 8, LANES), f32),
             pltpu.SemaphoreType.DMA((5,)),
         ],
         compiler_params=pltpu.CompilerParams(vmem_limit_bytes=SMALL_VMEM),

time: 54 us -> 53.9 us (level)
  the two profiles are of different devices: /device:TPU:68 before, /device:TPU:66 now
where the time goes in v9:
time: 53.9 us; the launch traced here: 53.6 us
  blocking collectives  20.1 us (37%)
  starting transfers between devices  12.8 us (24%)
  waiting for transfers between devices  12.2 us (23%)
  Pallas kernels  8.37 us (16%)
    all_to_all x1, blocking collectives, local(): lax.all_to_all(packed.reshape(16, 2 * HALF, LANES), ('depth', 'gx'), 0, 0...  12.3 us
    all_to_all x1, blocking collectives, local(): lax.all_to_all(strips_out.reshape(8, HALF, LANES), 'depth', 0, 0, tiled=T...  7.81 us
    ppermute x1, waiting for transfers between devices, local(): below = lax.ppermute(down, 'gx', line(x_count, -2))  7.27 us
    ppermute x1, starting transfers between devices, local(): above = lax.ppermute(up, 'gx', line(x_count, 2))  6.38 us
    pallas_call x1, Pallas kernels, sweep_call(): pl.pallas_call(kernel, out_shape=jax.ShapeDtypeStruct((TILE, LANES), jnp....  6.08 us
    ppermute x1, waiting for transfers between devices, local(): far = lax.ppermute(column, ('depth', 'gy'), swapped(1))  4.34 us
    ppermute x1, starting transfers between devices, local(): far = lax.ppermute(column, ('depth', 'gy'), swapped(1))  2.45 us
    ppermute x1, starting transfers between devices, local(): near = lax.ppermute(column, ('depth', 'gy'), swapped(0))  2.03 us
  transfers between devices with their start and end apart: 4, of which 3 were waited for; matrix products, arithmetic and copies ran while one was open for 0% of the time, Pallas kernels for 1%

profile of v9, /device:TPU:66, one launch (start us, length us, event | category | flops | bytes accessed | tf_op | source)
XLA Modules:
  0.0 53.6 jit_solution(13206983915222227305)
XLA Ops:
  0.0 1.1 %pack.1 = f32[256,128]{1,0:T(8,128)S(1)} custom-call(f32[2,16,256]{2,1,0:T(8,128)} %refs_0_.1, s32[2,16,256]{2,1,0:T(8,128)} %refs_1_.1, s32[16,256]{1,0:T(8,128)} %refs_2_.1, s32[8,16,256]{2,1,0:T(8,128)} %refs_3_.1, f32[8,16,256]{2,1,0:T(8,128)} %refs_4_.1), custom_call_target="tpu_custom_call" | custom-call | tf_op jit(solution)/shard_map/pack/pallas_call | solution.py:498
  1.1 12.3 %all_to_all.10 = f32[16,16,128]{2,1,0:T(8,128)S(1)} all-to-all(f32[16,16,128]{2,1,0:T(8,128)S(1)} %bitcast.5), channel_id=1, replica_groups={{0,4,64,68,128,132,192,196,256,260,320,324,384,388,448,452},{8,12,72,76..., dimensions={0} | all-to-all | bytes 262144 | tf_op jit(solution)/shard_map/all_to_all | solution.py:526
  13.4 0.1 stage.1
  13.6 6.4 %collective-permute-start = (f32[19,8,128]{2,1,0:T(8,128)S(1)}, f32[19,8,128]{2,1,0:T(8,128)S(1)}, u32[]{:S(2)}, u32[]{:S(2)}) collective-permute-start(f32[19,8,128]{2,1,0:T(8,128)S(1)} %get-tuple-element.12), channel_id=1, source_target_pairs={{0,8},{4,12},{8,16},{12,20},{16,24},{20,28},{24,32},{28,36},{32,40... | collective-permute-start | bytes 233480 | tf_op jit(solution)/shard_map/ppermute | solution.py:542
  20.0 1.9 %collective-permute-start.1 = (f32[19,8,128]{2,1,0:T(8,128)S(1)}, f32[19,8,128]{2,1,0:T(8,128)S(1)}, u32[]{:S(2)}, u32[]{:S(2)}) collective-permute-start(f32[19,8,128]{2,1,0:T(8,128)S(1)} %get-tuple-element.14), channel_id=1, source_target_pairs={{8,0},{12,4},{16,8},{20,12},{24,16},{28,20},{32,24},{36,28},{40,32... | collective-permute-start | bytes 233480 | tf_op jit(solution)/shard_map/ppermute | solution.py:543
  21.9 0.6 %collective-permute-done.above_ref = f32[19,8,128]{2,1,0:T(8,128)S(1)} collective-permute-done((f32[19,8,128]{2,1,0:T(8,128)S(1)}, f32[19,8,128]{2,1,0:T(8,128)S(1)}, u32[]{:S(2)}, u32[]{:S(2)}) %collective-permute-start) | collective-permute-done | bytes 77856 | tf_op jit(solution)/shard_map/ppermute | solution.py:542
  22.4 7.3 %collective-permute-done.1.below_ref = f32[19,8,128]{2,1,0:T(8,128)S(1)} collective-permute-done((f32[19,8,128]{2,1,0:T(8,128)S(1)}, f32[19,8,128]{2,1,0:T(8,128)S(1)}, u32[]{:S(2)}, u32[]{:S(2)}) %collective-permute-start.1) | collective-permute-done | bytes 77856 | tf_op jit(solution)/shard_map/ppermute | solution.py:543
  29.7 0.0 copy-start
  29.7 0.1 arrange.1.refs_3_
  29.8 2.5 %collective-permute-start.3 = (f32[408,128]{1,0:T(8,128)S(1)}, f32[408,128]{1,0:T(8,128)S(1)}, u32[]{:S(2)}, u32[]{:S(2)}) collective-permute-start(f32[408,128]{1,0:T(8,128)S(1)} %arrange.1.refs_3_), channel_id=1, source_target_pairs={{64,128},{128,64},{192,256},{256,192},{320,384},{384,320},{448,1},... | collective-permute-start | bytes 626696 | tf_op jit(solution)/shard_map/ppermute | solution.py:581
  32.3 2.0 %collective-permute-start.2 = (f32[408,128]{1,0:T(8,128)S(1)}, f32[408,128]{1,0:T(8,128)S(1)}, u32[]{:S(2)}, u32[]{:S(2)}) collective-permute-start(f32[408,128]{1,0:T(8,128)S(1)} %arrange.1.refs_3_), channel_id=1, source_target_pairs={{0,64},{64,0},{128,192},{192,128},{256,320},{320,256},{384,448},{4... | collective-permute-start | bytes 626696 | tf_op jit(solution)/shard_map/ppermute | solution.py:580
  34.3 0.0 copy-done
  34.3 0.1 copy.7.refs_0_
  34.4 0.3 start.1
  34.7 4.3 %collective-permute-done.3.refs_4_ = f32[408,128]{1,0:T(8,128)S(1)} collective-permute-done((f32[408,128]{1,0:T(8,128)S(1)}, f32[408,128]{1,0:T(8,128)S(1)}, u32[]{:S(2)}, u32[]{:S(2)}) %collective-permute-start.3) | collective-permute-done | bytes 208928 | tf_op jit(solution)/shard_map/ppermute | solution.py:581
  39.0 0.0 collective-permute-done.2.refs_2_
  39.0 6.1 %sweep.1 = f32[64,128]{1,0:T(8,128)S(1)} custom-call(f32[96,8,128]{2,1,0:T(8,128)S(1)} %get-tuple-element.16.refs_0_, f32[2,8,128]{2,1,0:T(8,128)S(1)} %get-tuple-element.17.refs_1_, f32[408,128]{1,0:T(8,128)S(1)} %collective-permute-done.2.refs_2_, f32[408,128]{1,0:T(8,128)S(1)} %arrange.1.refs_3_, f32[408,128]{1,0:T(8,128)S(1)} %collective-permute-done.3.refs_4_), custom_call_target="tpu_custom_call" | custom-call | tf_op jit(solution)/shard_map/sweep/pallas_call | solution.py:463
  45.1 7.8 %all_to_all.11 = f32[8,8,128]{2,1,0:T(8,128)S(1)} all-to-all(f32[8,8,128]{2,1,0:T(8,128)S(1)} %bitcast.6), channel_id=1, replica_groups=mesh['depth'=8,'gx'=16,'gy'=4] {'depth'}, dimensions={0} | all-to-all | bytes 65536 | tf_op jit(solution)/shard_map/all_to_all | solution.py:584
  52.9 0.7 %unpack.1 = f32[2,16,256]{2,1,0:T(8,128)} custom-call(f32[64,128]{1,0:T(8,128)S(1)} %bitcast.7), custom_call_target="tpu_custom_call" | custom-call | tf_op jit(solution)/shard_map/unpack/pallas_call | solution.py:587
Async XLA Ops:
  13.6 8.9 %collective-permute-start = (f32[19,8,128]{2,1,0:T(8,128)S(1)}, f32[19,8,128]{2,1,0:T(8,128)S(1)}, u32[]{:S(2)}, u32[]{:S(2)}) collective-permute-start(f32[19,8,128]{2,1,0:T(8,128)S(1)} %get-tuple-element.12), channel_id=1, source_target_pairs={{0,8},{4,12},{8,16},{12,20},{16,24},{20,28},{24,32},{28,36},{32,40... | collective-permute-start | bytes 233480 | tf_op jit(solution)/shard_map/ppermute | solution.py:542
  20.0 9.8 %collective-permute-start.1 = (f32[19,8,128]{2,1,0:T(8,128)S(1)}, f32[19,8,128]{2,1,0:T(8,128)S(1)}, u32[]{:S(2)}, u32[]{:S(2)}) collective-permute-start(f32[19,8,128]{2,1,0:T(8,128)S(1)} %get-tuple-element.14), channel_id=1, source_target_pairs={{8,0},{12,4},{16,8},{20,12},{24,16},{28,20},{32,24},{36,28},{40,32... | collective-permute-start | bytes 233480 | tf_op jit(solution)/shard_map/ppermute | solution.py:543
  29.7 4.6 %copy-start = (s32[8,2]{0,1:T(2,128)S(1)}, s32[8,2]{0,1:T(2,128)}, u32[]{:S(2)}) copy-start(s32[8,2]{0,1:T(2,128)} %param.9) | copy-start | bytes 196
  29.8 9.2 %collective-permute-start.3 = (f32[408,128]{1,0:T(8,128)S(1)}, f32[408,128]{1,0:T(8,128)S(1)}, u32[]{:S(2)}, u32[]{:S(2)}) collective-permute-start(f32[408,128]{1,0:T(8,128)S(1)} %arrange.1.refs_3_), channel_id=1, source_target_pairs={{64,128},{128,64},{192,256},{256,192},{320,384},{384,320},{448,1},... | collective-permute-start | bytes 626696 | tf_op jit(solution)/shard_map/ppermute | solution.py:581
  32.3 6.8 %collective-permute-start.2 = (f32[408,128]{1,0:T(8,128)S(1)}, f32[408,128]{1,0:T(8,128)S(1)}, u32[]{:S(2)}, u32[]{:S(2)}) collective-permute-start(f32[408,128]{1,0:T(8,128)S(1)} %arrange.1.refs_3_), channel_id=1, source_target_pairs={{0,64},{64,0},{128,192},{192,128},{256,320},{320,256},{384,448},{4... | collective-permute-start | bytes 626696 | tf_op jit(solution)/shard_map/ppermute | solution.py:580
